TPU v7x, 128 devices: a whole 4x4x4 slice. The times are simulated.
128 devices in a mesh: ctx: 16 (over z, y_hi, core), head: 8 (over y_lo, x).
Axes of the slice: x: 4, y: 4 (y_hi: 2, y_lo: 2; y = y_hi * 2 + y_lo), z: 4, core: 2. Of those that a mesh axis runs over, the one named last changes fastest.
Arguments:
- query: bfloat16 [8192, 64, 128], P('ctx', 'head'), may hold values from -8 to 8
- keys: bfloat16 [8192, 8, 128], P('ctx', 'head'), may hold values from -8 to 8
- values: bfloat16 [8192, 8, 128], P('ctx', 'head'), may hold values from -6 to 6
- k_scale: bfloat16 [32, 8], P('ctx', 'head'), may hold values from 0.59765625 to 1.59375
- v_scale: bfloat16 [32, 8], P('ctx', 'head'), may hold values from 0.5 to 2
- block_place: int32 [32], P('ctx'), may hold values from 0 to 31, as said below
- out_weight: bfloat16 [8192, 8192], P('head'), may hold values from -1 to 1
Outputs:
- mixed: bfloat16 [8192, 8192], P(('ctx', 'head'))
Inputs may be any that keep to these rules, and one draw needn't show every extreme that they name: `block_place`: A permutation of the block indices in which entries 2r and 2r + 1 sum to 31 and entry 2r is below 16.
All inputs are finite; a program needn't handle non-finite values.
Results may differ from a plain program's by a relative error of at most 0.015.
Values may be sent and summed in bfloat16 or wider, within the bound.
No kernel may reach another device: no remote copies, remote signals or barrier semaphores. Data moves between devices by JAX's collectives and lax.ppermute only.
A program may use at most 128 MiB of HBM per device.

v0:
```python
import math

import jax
import jax.numpy as jnp
from jax import lax
from jax.sharding import PartitionSpec as P

masked_value = -1e30


def joined_along(pieces, dim):
    shape = list(pieces.shape[1:])
    shape[dim] *= pieces.shape[0]
    return jnp.moveaxis(pieces, 0, dim).reshape(shape)


def from_everyone(x, axis):
    copies = jnp.broadcast_to(x, (lax.axis_size(axis), *x.shape))
    return lax.all_to_all(copies, axis, split_axis=0, concat_axis=0, tiled=True)


def gathered_copies(x, axis, dim):
    return joined_along(from_everyone(x, axis), dim)


def sent_together(arrays, axis, dim, along):
    columns = [a.reshape(*a.shape[:along], -1) for a in arrays]
    both = jnp.concatenate(columns, axis=along)
    out, at, gathered = (lax.all_gather(both, axis, axis=dim, tiled=True), 0, [])
    for a, column in zip(arrays, columns):
        section = out[..., at : at + column.shape[along]]
        gathered.append(section.reshape(*section.shape[:along], *a.shape[along:]))
        at += column.shape[along]
    return tuple(gathered)


def attend_tile(
    carried,
    queries,
    query_slot,
    query_place,
    key_block,
    value_block,
    key_gain,
    value_gain,
    key_place,
    inv_root,
):
    block_len = key_block.shape[0]

    def compute(current):
        maxima, totals, running = current
        scores = jnp.einsum(
            "qgrd,kgd->qgrk", queries[query_slot], key_block, preferred_element_type=jnp.float32
        )
        scores = scores * (key_gain.astype(jnp.float32) * inv_root)[None, :, None, None]
        offsets = jnp.arange(block_len, dtype=jnp.int32)
        visible = (query_place * block_len + offsets)[:, None] >= (key_place * block_len + offsets)[
            None, :
        ]
        scores = jnp.where(visible[:, None, None, :], scores, masked_value)
        old_max = maxima[query_slot]
        new_max = jnp.maximum(old_max, jnp.max(scores, axis=-1))
        factor = jnp.exp(old_max - new_max)
        weights = jnp.exp(scores - new_max[..., None])
        new_total = factor * totals[query_slot] + jnp.sum(weights, axis=-1)
        product = jnp.einsum(
            "qgrk,kgd->qgrd",
            weights.astype(jnp.bfloat16),
            value_block,
            preferred_element_type=jnp.float32,
        )
        new_sum = (
            factor[..., None] * running[query_slot]
            + value_gain.astype(jnp.float32)[None, :, None, None] * product
        )
        return (
            maxima.at[query_slot].set(new_max),
            totals.at[query_slot].set(new_total),
            running.at[query_slot].set(new_sum),
        )

    return lax.cond(key_place <= query_place, compute, lambda current: current, carried)


def body(query, keys, values, k_scale, v_scale, block_place, out_weight):
    local_rows, head_count, head_dim = query.shape
    group_count = keys.shape[1]
    block_len = local_rows // 2
    per_group = head_count // group_count
    inv_root = 1.0 / math.sqrt(head_dim)
    position = lax.axis_index("ctx")
    all_places = gathered_copies(block_place, "ctx", 0)
    queries = query.reshape(2, block_len, group_count, per_group, head_dim)
    own_block = (
        keys.reshape(2, block_len, group_count, head_dim),
        values.reshape(2, block_len, group_count, head_dim),
        k_scale,
        v_scale,
    )
    own_places = lax.dynamic_slice_in_dim(all_places, 2 * position, 2)
    maxima = jnp.full((2, block_len, group_count, per_group), masked_value, jnp.float32)
    totals = jnp.zeros((2, block_len, group_count, per_group), jnp.float32)
    running = jnp.zeros((2, block_len, group_count, per_group, head_dim), jnp.float32)
    carried = (maxima, totals, running)
    current = carried
    key_part, value_part, key_gains, value_gains = sent_together(
        (own_block[0], own_block[1], own_block[2], own_block[3]), "ctx", 0, 1
    )

    def one_block(inner, items):
        key_block, value_block, key_gain, value_gain, key_place = items
        for query_slot in range(2):
            inner = attend_tile(
                inner,
                queries,
                query_slot,
                own_places[query_slot],
                key_block,
                value_block,
                key_gain,
                value_gain,
                key_place,
                inv_root,
            )
        return (inner, None)

    current, unused = lax.scan(
        one_block, current, (key_part, value_part, key_gains, value_gains, all_places)
    )
    carried = current
    maxima, totals, running = carried
    attended = (
        (running / totals[..., None])
        .astype(jnp.bfloat16)
        .reshape(local_rows, head_count * head_dim)
    )
    return lax.psum_scatter(
        jnp.dot(attended, out_weight, preferred_element_type=jnp.float32).astype(jnp.bfloat16),
        "head",
        scatter_dimension=0,
        tiled=True,
    )


def solution(mesh):
    placed = (
        P("ctx", "head", None),
        P("ctx", "head", None),
        P("ctx", "head", None),
        P("ctx", "head"),
        P("ctx", "head"),
        P("ctx"),
        P("head", None),
    )
    return jax.shard_map(
        body, mesh=mesh, in_specs=placed, out_specs=P(("ctx", "head"), None), check_vma=False
    )
```

profile of v0, /device:TPU:24, one launch (start us, length us, event | category | flops | bytes accessed | tf_op | source)
XLA Modules:
  0.0 512.9 jit_solution(14754643074542454275)
XLA Ops:
  12.2 8.3 %all-to-all-start = ((s32[16,1,2]{2,1,0:T(1,128)}), s32[16,1,2]{2,1,0:T(1,128)S(1)}, u32[]{:S(2)}, u32[]{:S(2)}) async-start(s32[16,1,2]{2,1,0:T(1,128)} %broadcast_in_dim.50), calls=%async_computation | async-start | bytes 16384 | tf_op jit(solution)/shard_map/all_to_all | solution.py:19
  20.7 4.4 all-to-all-done
  26.6 40.4 %all-gather.3.cloned.1.call-done = bf16[16,2,65538]{2,1,0:T(2,128)(2,1)} async-done(((bf16[1,2,65538]{2,1,0:T(2,128)(2,1)}), bf16[16,2,65538]{2,1,0:T(2,128)(2,1)}) %all-gather.3.cloned.1.call-update) | async-done | bytes 4194448 | tf_op jit(solution)/shard_map/all_gather | solution.py:29
  67.1 6.2 %reshape.509 = bf16[32,65538]{1,0:T(8,128)(2,1)} reshape(bf16[16,2,65538]{2,1,0:T(2,128)(2,1)} %all-gather.3.cloned.1.call-done) | data formatting | bytes 8388864
  80.5 316.5 %while.20 = (s32[]{:T(128)}, f32[2,256,1,8]{1,3,2,0:T(8,128)S(1)}, f32[2,256,1,8]{1,3,2,0:T(8,128)S(1)}, f32[2,256,1,8,128]{4,1,3,2,0:T(8,128)S(1)}, s32[32]{0:T...) while((s32[]{:T(128)}, f32[2,256,1,8]{1,3,2,0:T(8,128)S(1)}, ...), condition=%wide.region_9.10_spmd, body=%wide.region_0.9_spmd.sunk | while | flops 545932288 | bytes 23061036 | solution.py:128
  95.5 4.4 conditional.5
  109.6 4.4 conditional.5
  129.1 4.4 conditional.5
  138.8 4.4 conditional.5
  152.9 4.4 conditional.5
  168.0 4.4 conditional.5
  177.8 4.4 conditional.5
  187.6 4.4 conditional.5
  197.3 4.4 conditional.5
  207.1 4.4 conditional.5
  216.9 4.4 conditional.5
  226.6 4.4 conditional.5
  236.4 4.4 conditional.5
  246.2 4.4 conditional.5
  255.9 4.4 conditional.5
  285.1 4.4 conditional.5
  294.9 4.4 conditional.5
  304.7 4.4 conditional.5
  314.4 4.4 conditional.5
  324.2 4.4 conditional.5
  334.0 4.4 conditional.5
  363.2 4.4 conditional.5
  372.9 4.4 conditional.5
  382.7 4.4 conditional.5
  392.5 4.4 conditional.5
  398.4 16.8 %convolution_convert_fusion = bf16[512,8192]{1,0:T(8,128)(2,1)} fusion(bf16[1024,8192]{1,0:T(8,128)(2,1)} %param.31, bf16[64,8,8,128]{3,2,1,0:T(8,128)(2,1)S(1)} %bitcast.178), kind=kOutput, calls=%fused_computation.56 | convolution fusion | flops 8594128896 | bytes 26214400 | tf_op jit(solution)/shard_map/dot_general | solution.py:139
  415.2 90.9 %reduce-scatter.2.cloned.1.call-done = bf16[64,8192]{1,0:T(8,128)(2,1)} async-done(((bf16[512,8192]{1,0:T(8,128)(2,1)}), bf16[64,8192]{1,0:T(8,128)(2,1)}) %reduce-scatter.2.cloned.1.call-update) | async-done | bytes 1048592 | tf_op jit(solution)/shard_map/reduce_scatter | solution.py:138
  (460 shorter events, 196.9 us)
Async XLA Ops:
  6.5 14.0 %copy-start = (bf16[512,8,128]{2,1,0:T(8,128)(2,1)S(1)}, bf16[512,8,128]{2,1,0:T(8,128)(2,1)}, u32[]{:S(2)}) copy-start(bf16[512,8,128]{2,1,0:T(8,128)(2,1)} %param.25) | copy-start | bytes 3145732
  6.5 60.6 %all-gather.3.cloned.1.call-start = ((), (), s32[]{:S(2)}) async-start(), calls=%async_computation.3 | async-start | bytes 4465152 | tf_op jit(solution)/shard_map/all_gather | solution.py:29
  10.2 0.7 copy-start.1
  12.2 13.0 %all-to-all-start = ((s32[16,1,2]{2,1,0:T(1,128)}), s32[16,1,2]{2,1,0:T(1,128)S(1)}, u32[]{:S(2)}, u32[]{:S(2)}) async-start(s32[16,1,2]{2,1,0:T(1,128)} %broadcast_in_dim.50), calls=%async_computation | async-start | bytes 16384 | tf_op jit(solution)/shard_map/all_to_all | solution.py:19
  20.5 485.6 %reduce-scatter.2.cloned.1.call-start = ((), (), s32[]{:S(2)}) async-start(), calls=%async_computation.2 | async-start | bytes 9437184 | tf_op jit(solution)/shard_map/reduce_scatter | solution.py:138
Sparse Core Ops, SparseCore 0:
  11.0 56.0 all-gather.2
  415.3 90.6 reduce-scatter.1
where the time goes:
time: 519 us; the launch traced here: 513 us
  loops' own time  171 us (33%)
  waiting for transfers between devices  136 us (26%)
  local copies, waits for them, and re-layouts  110 us (21%)
  matrix products  58.7 us (11%)
  other arithmetic  15.5 us (3%)
  between operations  13.5 us (3%)
  starting transfers between devices  8.33 us (2%)
    reduce_scatter x1, waiting for transfers between devices, body(): lax.psum_scatter(jnp.dot(attended, out_weight, preferred_element_type=jnp...  90.9 us
    another operation x64, loops' own time, attend_tile(): lax.cond(key_place <= query_place, compute, lambda current: current, carr...  88.3 us
    another operation x1, loops' own time, body(): lax.scan(one_block, current, (key_part, value_part, key_gains, value_gain...  82.7 us
    all_gather x1, waiting for transfers between devices, sent_together(): lax.all_gather(both, axis, axis=dim, tiled=True)  40.4 us
    dynamic_slice x64, local copies, waits for them, and re-layouts, body(): lax.scan(one_block, current, (key_part, value_part, key_gains, value_gain...  38.1 us
    squeeze x32, local copies, waits for them, and re-layouts, body(): lax.scan(one_block, current, (key_part, value_part, key_gains, value_gain...  28.4 us
    dot_general x33, matrix products, compute(): jnp.einsum('qgrk,kgd->qgrd', weights.astype(jnp.bfloat16), value_block, p...  26.9 us
    slice x32, local copies, waits for them, and re-layouts, one_block(): own_places[query_slot]  20.7 us
  transfers between devices with their start and end apart: 3, of which 3 were waited for; matrix products, arithmetic and copies ran while one was open for 1% of the time, Pallas kernels for 0%

commit v1 on v0

v1 whole, which is shorter than its diff:
```python
import itertools
import math

import jax
import jax.numpy as jnp
from jax import lax
from jax.experimental import pallas as pl
from jax.experimental.pallas import tpu as pltpu
from jax.sharding import PartitionSpec as P

F32 = jnp.float32
BF16 = jnp.bfloat16
AXES = ("ctx", "head")
NEG = -1e30
CHUNK = 128
NT = (((1,), (1,)), ((), ()))
NN = (((1,), (0,)), ((), ()))
META = 16


def index_of(z, yh, c, yl, x):
    return ((z % 4) * 4 + (yh % 2) * 2 + c % 2) * 8 + (yl % 2) * 4 + x % 4


def moved(array, step):
    pairs = []
    for z, yh, c, yl, x in itertools.product(range(4), range(2), range(2), range(2), range(4)):
        target = tuple(a + b for a, b in zip((z, yh, c, yl, x), step))
        pairs.append((index_of(z, yh, c, yl, x), index_of(*target)))
    return lax.ppermute(array, AXES, pairs)


def attend_rows(q_ref, acc_ref, l_ref, m_ref, base, count, keys, vals, gains, first=False, visible=None):
    width = keys.shape[0]
    for j in range(count):
        rows = pl.ds(pl.multiple_of(base + j * CHUNK, CHUNK), CHUNK)
        scores = lax.dot_general(q_ref[rows, :], keys, NT, preferred_element_type=F32) * gains
        if visible is not None:
            scores = jnp.where(visible(j), scores, NEG)
        top = jnp.max(scores, axis=1, keepdims=True)
        if first:
            new_m = jnp.broadcast_to(top, (CHUNK, 128))
        else:
            old_m = m_ref[rows, :]
            new_m = jnp.maximum(old_m, top)
        weights = jnp.exp2(scores - jnp.tile(new_m, (1, width // 128)))
        product = lax.dot_general(weights.astype(BF16), vals, NN, preferred_element_type=F32)
        if first:
            acc_ref[rows, :] = product[:, :128]
            l_ref[rows, :] = product[:, 128:]
        else:
            factor = jnp.exp2(old_m - new_m)
            acc_ref[rows, :] = acc_ref[rows, :] * factor + product[:, :128]
            l_ref[rows, :] = l_ref[rows, :] * factor + product[:, 128:]
        m_ref[rows, :] = new_m


def own_steps(q_ref, acc_ref, l_ref, m_ref, own_ref, inv):
    ones = jnp.ones((256, 128), BF16)
    low_k, high_k = own_ref[0:256, :], own_ref[256:512, :]
    low_v = jnp.concatenate([own_ref[512:768, :], ones], axis=1)
    high_v = jnp.concatenate([own_ref[768:1024, :], ones], axis=1)
    low_g = own_ref[1024:1025, :].astype(F32) * inv
    high_g = own_ref[1025:1026, :].astype(F32) * inv

    def low_visible(j):
        token = j * (CHUNK // 8) + lax.broadcasted_iota(jnp.int32, (CHUNK, 256), 0) // 8
        return lax.broadcasted_iota(jnp.int32, (CHUNK, 256), 1) <= token

    def high_visible(j):
        token = 256 + j * (CHUNK // 8) + lax.broadcasted_iota(jnp.int32, (CHUNK, 512), 0) // 8
        return lax.broadcasted_iota(jnp.int32, (CHUNK, 512), 1) <= token

    attend_rows(
        q_ref, acc_ref, l_ref, m_ref, 0, 16, low_k, low_v, jnp.tile(low_g, (1, 2)), True, low_visible
    )
    attend_rows(
        q_ref,
        acc_ref,
        l_ref,
        m_ref,
        2048,
        16,
        jnp.concatenate([low_k, high_k], axis=0),
        jnp.concatenate([low_v, high_v], axis=0),
        jnp.concatenate([low_g, low_g, high_g, high_g], axis=1),
        True,
        high_visible,
    )


def place_of(ref):
    return jnp.max(ref[1026:1027, :].astype(F32)).astype(jnp.int32)


def other_steps(q_ref, acc_ref, l_ref, m_ref, own_place, refs, kbuf, vbuf, gbuf, inv):
    count = len(refs)
    vbuf[:, 128:] = jnp.ones((2 * count * 256, 128), BF16)
    highs = jnp.int32(count)
    lows = jnp.int32(0)

    def put(slot, ref, half):
        at = pl.ds(pl.multiple_of(slot * 256, 256), 256)
        kbuf[at, :] = ref[pl.ds(pl.multiple_of(half * 256, 256), 256), :]
        vbuf[at, :128] = ref[pl.ds(pl.multiple_of(512 + half * 256, 256), 256), :]
        gain = jnp.where(half == 0, ref[1024:1025, :].astype(F32), ref[1025:1026, :].astype(F32))
        gbuf[pl.ds(slot, 1), :] = gain * inv

    for i, ref in enumerate(refs):
        put(i, ref, 0)
    for ref in refs:
        is_low = (place_of(ref) < own_place).astype(jnp.int32)
        slot = jnp.where(is_low == 1, 2 * count - 1 - lows, highs)
        put(slot, ref, 1 - is_low)
        lows = lows + is_low
        highs = highs + 1 - is_low

    def step(i, carry):
        first = 2 * i
        mixed = (first + 1) == highs
        base = jnp.where(first + 1 < highs, 2048, 0)
        at = pl.multiple_of(i * 512, 512)
        g0 = gbuf[pl.ds(first, 1), :]
        g1 = gbuf[pl.ds(first + 1, 1), :]

        @pl.when(jnp.logical_not(mixed))
        def _():
            attend_rows(
                q_ref,
                acc_ref,
                l_ref,
                m_ref,
                base,
                16,
                kbuf[pl.ds(at, 512), :],
                vbuf[pl.ds(at, 512), :],
                jnp.concatenate([g0, g0, g1, g1], axis=1),
            )

        @pl.when(mixed)
        def _():
            attend_rows(
                q_ref,
                acc_ref,
                l_ref,
                m_ref,
                2048,
                16,
                kbuf[pl.ds(at, 256), :],
                vbuf[pl.ds(at, 256), :],
                jnp.concatenate([g0, g0], axis=1),
            )
            attend_rows(
                q_ref,
                acc_ref,
                l_ref,
                m_ref,
                0,
                16,
                kbuf[pl.ds(at + 256, 256), :],
                vbuf[pl.ds(at + 256, 256), :],
                jnp.concatenate([g1, g1], axis=1),
            )

        return carry

    lax.fori_loop(0, count, step, 0)


def group_kernel(inv, count, start, finish, *refs):
    refs = list(refs)
    q_ref = refs.pop(0)
    own_ref = refs.pop(0)
    others = [refs.pop(0) for _ in range(count)]
    if not start:
        del refs[:3]
    att_ref = refs.pop(0) if finish else None
    acc_ref, l_ref, m_ref, kbuf, vbuf, gbuf = refs
    if start:
        own_steps(q_ref, acc_ref, l_ref, m_ref, own_ref, inv)
    other_steps(q_ref, acc_ref, l_ref, m_ref, place_of(own_ref), others, kbuf, vbuf, gbuf, inv)
    if finish:
        acc_ref[...] = acc_ref[...] / l_ref[...]
        for h in range(8):
            rows = pl.ds(h, 512, stride=8)
            att_ref[:, h * 128 : (h + 1) * 128] = acc_ref[rows, :].astype(BF16)


def attend(q, own, others, state, finish, inv, name):
    count = len(others)
    start = state is None
    vmem = pl.BlockSpec(memory_space=pltpu.VMEM)
    shapes = [jax.ShapeDtypeStruct((4096, 128), F32)] * 3
    operands = [q, own, *others] + ([] if start else list(state))
    scratch = [
        pltpu.VMEM((2 * count * 256, 128), BF16),
        pltpu.VMEM((2 * count * 256, 256), BF16),
        pltpu.VMEM((2 * count, 128), F32),
    ]
    aliases = {}
    if finish:
        outs = [jax.ShapeDtypeStruct((512, 1024), BF16)]
        scratch = [pltpu.VMEM(s.shape, s.dtype) for s in shapes] + scratch
        if not start:
            outs = outs + shapes
            scratch = scratch[3:]
            aliases = {2 + count + i: 1 + i for i in range(3)}
    else:
        outs = shapes
        if not start:
            aliases = {2 + count + i: i for i in range(3)}
    tiles = 2 * count + (3 if start else 0)
    import functools

    return pl.pallas_call(
        functools.partial(group_kernel, inv, count, start, finish),
        out_shape=outs,
        in_specs=[vmem] * len(operands),
        out_specs=[vmem] * len(outs),
        scratch_shapes=scratch,
        input_output_aliases=aliases,
        compiler_params=pltpu.CompilerParams(vmem_limit_bytes=40 << 20),
        cost_estimate=pl.CostEstimate(
            flops=tiles * 4 * 2048 * 256 * 128 * 4,
            transcendentals=tiles * 2048 * 256,
            bytes_accessed=1 << 20,
        ),
        name=name,
    )(*operands)


def body(query, keys, values, k_scale, v_scale, block_place, out_weight):
    inv = math.log2(math.e) / math.sqrt(128)
    q = query.reshape(4096, 128)
    k = keys.reshape(512, 128)
    gain = jnp.repeat(v_scale.reshape(2).astype(F32), 256)[:, None]
    v = (values.reshape(512, 128).astype(F32) * gain).astype(BF16)
    meta = jnp.concatenate(
        [k_scale.reshape(2), block_place.astype(BF16), jnp.zeros((META - 4,), BF16)]
    )
    own = jnp.concatenate([k, v, jnp.broadcast_to(meta[:, None], (META, 128))], axis=0)
    swap = (0, 0, 1, 0, 0)
    partner = moved(own, swap)
    up = moved(own, (1, 0, 0, 0, 0))
    down = moved(own, (-1, 0, 0, 0, 0))
    over = moved(own, (0, 1, 0, 0, 0))
    far = moved(own, (2, 0, 0, 0, 0))
    up2, down2 = moved(up, swap), moved(down, swap)
    state = attend(q, own, [partner], None, False, inv, "attend_own")
    state = attend(q, own, [up, down, up2, down2], state, False, inv, "attend_near")
    over2, far2 = moved(over, swap), moved(far, swap)
    oup = moved(over, (1, 0, 0, 0, 0))
    odown = moved(over, (-1, 0, 0, 0, 0))
    ofar = moved(over, (2, 0, 0, 0, 0))
    state = attend(q, own, [over, far, over2, far2], state, False, inv, "attend_over")
    rest = [oup, odown, ofar]
    rest = rest + [moved(r, swap) for r in rest]
    attended = attend(q, own, rest, state, True, inv, "attend_rest")[0]
    return lax.psum_scatter(
        jnp.dot(attended, out_weight, preferred_element_type=F32).astype(BF16),
        "head",
        scatter_dimension=0,
        tiled=True,
    )


def solution(mesh):
    placed = (
        P("ctx", "head", None),
        P("ctx", "head", None),
        P("ctx", "head", None),
        P("ctx", "head"),
        P("ctx", "head"),
        P("ctx"),
        P("head", None),
    )
    return jax.shard_map(
        body, mesh=mesh, in_specs=placed, out_specs=P(("ctx", "head"), None), check_vma=False
    )
```

time: 519 us -> 188 us (0.36)
  loops' own time: 171 us -> 0 us
  local copies, waits for them, and re-layouts: 110 us -> 1.31 us
  matrix products: 58.7 us -> 17.1 us
  waiting for transfers between devices: 136 us -> 99.1 us
  Pallas kernels: 0 us -> 31.9 us
  other arithmetic: 15.5 us -> 4.42 us
  starting transfers between devices: 8.33 us -> 18.7 us
    another operation x65 -> x0, loops' own time: 171 us -> none  [the longest x64 88.3 us: attend_tile(): lax.cond(key_place <= query_place, compute, lambda current: current, carr...]
    dot_general x67 -> x1, matrix products: 58.7 us -> 17.1 us  [body(): jnp.dot(attended, out_weight, preferred_element_type=F32).astype(BF16)]
    all_gather x1 -> x0, waiting for transfers between devices: 40.4 us -> none  [sent_together(): lax.all_gather(both, axis, axis=dim, tiled=True)]
    dynamic_slice x65 -> x0, local copies, waits for them, and re-layouts: 38.1 us -> none  [the longest x64 38.1 us: body(): lax.scan(one_block, current, (key_part, value_part, key_gains, value_gain...]
    pallas_call x0 -> x4, Pallas kernels: none -> 31.9 us  [attend(): pl.pallas_call(functools.partial(group_kernel, inv, count, start, finish)...]
    squeeze x32 -> x0, local copies, waits for them, and re-layouts: 28.4 us -> none  [body(): lax.scan(one_block, current, (key_part, value_part, key_gains, value_gain...]
    slice x66 -> x0, local copies, waits for them, and re-layouts: 23.9 us -> none  [the longest x32 20.7 us: one_block(): own_places[query_slot]]
    ppermute x0 -> x15, starting transfers between devices: none -> 18.7 us  [moved(): return lax.ppermute(array, AXES, pairs)]
  transfers between devices with their start and end apart: 3 -> 16, of which waited for: 3 -> 4; matrix products, arithmetic and copies ran while one was open for 1% -> 0% of each run, Pallas kernels for 0% -> 11%
where the time goes in v1:
time: 188 us; the launch traced here: 186 us
  waiting for transfers between devices  99.1 us (53%)
  Pallas kernels  31.9 us (17%)
  starting transfers between devices  18.7 us (10%)
  matrix products  17.1 us (9%)
  between operations  13.5 us (7%)
  other arithmetic  4.42 us (2%)
    reduce_scatter x1, waiting for transfers between devices, body(): lax.psum_scatter(jnp.dot(attended, out_weight, preferred_element_type=F32...  92.4 us
    pallas_call x4, Pallas kernels, attend(): pl.pallas_call(functools.partial(group_kernel, inv, count, start, finish)...  31.9 us
    ppermute x15, starting transfers between devices, moved(): return lax.ppermute(array, AXES, pairs)  18.7 us
    dot_general x1, matrix products, body(): jnp.dot(attended, out_weight, preferred_element_type=F32).astype(BF16)  17.1 us
    ppermute x15, waiting for transfers between devices, moved(): return lax.ppermute(array, AXES, pairs)  6.75 us
  transfers between devices with their start and end apart: 16, of which 4 were waited for; matrix products, arithmetic and copies ran while one was open for 0% of the time, Pallas kernels for 11%

profile of v1, /device:TPU:24, one launch (start us, length us, event | category | flops | bytes accessed | tf_op | source)
XLA Modules:
  0.0 186.0 jit_solution(5402173757898869509)
XLA Ops:
  6.5 0.8 convert_reduce_fusion
  7.3 0.1 broadcast_bitcast_fusion
  7.4 0.7 convert_element_type.26
  8.0 1.0 fusion
  9.1 0.8 reduce.1
  9.9 0.1 pad_maximum_fusion
  9.9 1.1 maximum_maximum_fusion.refs_1_
  11.1 1.3 collective-permute-start
  12.4 1.9 %collective-permute-start.10 = (bf16[1040,128]{1,0:T(8,128)(2,1)S(1)}, bf16[1040,128]{1,0:T(8,128)(2,1)S(1)}, u32[]{:S(2)}, u32[]{:S(2)}) collective-permute-start(bf16[1040,128]{1,0:T(8,128)(2,1)S(1)} %maximum_maximum_fusion.refs_1_), channel_id=1, source_target_pairs={{0,32},{1,33},{2,34},{3,35},{4,36},{5,37},{6,38},{7,39},{8,40},{9,... | collective-permute-start | bytes 798728 | tf_op jit(solution)/shard_map/ppermute | solution.py:30
  14.3 2.1 %collective-permute-start.11 = (bf16[1040,128]{1,0:T(8,128)(2,1)S(1)}, bf16[1040,128]{1,0:T(8,128)(2,1)S(1)}, u32[]{:S(2)}, u32[]{:S(2)}) collective-permute-start(bf16[1040,128]{1,0:T(8,128)(2,1)S(1)} %maximum_maximum_fusion.refs_1_), channel_id=1, source_target_pairs={{0,96},{1,97},{2,98},{3,99},{4,100},{5,101},{6,102},{7,103},{8,104... | collective-permute-start | bytes 798728 | tf_op jit(solution)/shard_map/ppermute | solution.py:30
  16.4 1.9 %collective-permute-start.7 = (bf16[1040,128]{1,0:T(8,128)(2,1)S(1)}, bf16[1040,128]{1,0:T(8,128)(2,1)S(1)}, u32[]{:S(2)}, u32[]{:S(2)}) collective-permute-start(bf16[1040,128]{1,0:T(8,128)(2,1)S(1)} %maximum_maximum_fusion.refs_1_), channel_id=1, source_target_pairs={{0,64},{1,65},{2,66},{3,67},{4,68},{5,69},{6,70},{7,71},{8,72},{9,... | collective-permute-start | bytes 798728 | tf_op jit(solution)/shard_map/ppermute | solution.py:30
  18.3 2.5 %collective-permute-done.refs_2_ = bf16[1040,128]{1,0:T(8,128)(2,1)S(1)} collective-permute-done((bf16[1040,128]{1,0:T(8,128)(2,1)S(1)}, bf16[1040,128]{1,0:T(8,128)(2,1)S(1)}, u32[]{:S(2)}, u32[]{:S(2)}) %collective-permute-start) | collective-permute-done | bytes 266272 | tf_op jit(solution)/shard_map/ppermute | solution.py:30
  20.8 1.9 %collective-permute-start.1 = (bf16[1040,128]{1,0:T(8,128)(2,1)S(1)}, bf16[1040,128]{1,0:T(8,128)(2,1)S(1)}, u32[]{:S(2)}, u32[]{:S(2)}) collective-permute-start(bf16[1040,128]{1,0:T(8,128)(2,1)S(1)} %collective-permute-done.refs_2_), channel_id=1, source_target_pairs={{0,32},{1,33},{2,34},{3,35},{4,36},{5,37},{6,38},{7,39},{8,40},{9,... | collective-permute-start | bytes 798728 | tf_op jit(solution)/shard_map/ppermute | solution.py:30
  22.7 0.0 collective-permute-done.14.refs_2_
  22.7 2.1 %collective-permute-start.2 = (bf16[1040,128]{1,0:T(8,128)(2,1)S(1)}, bf16[1040,128]{1,0:T(8,128)(2,1)S(1)}, u32[]{:S(2)}, u32[]{:S(2)}) collective-permute-start(bf16[1040,128]{1,0:T(8,128)(2,1)S(1)} %collective-permute-done.refs_2_), channel_id=1, source_target_pairs={{0,96},{1,97},{2,98},{3,99},{4,100},{5,101},{6,102},{7,103},{8,104... | collective-permute-start | bytes 798728 | tf_op jit(solution)/shard_map/ppermute | solution.py:30
  24.8 0.0 collective-permute-done.10.refs_2_
  24.8 6.2 %collective-permute-start.3 = (bf16[1040,128]{1,0:T(8,128)(2,1)S(1)}, bf16[1040,128]{1,0:T(8,128)(2,1)S(1)}, u32[]{:S(2)}, u32[]{:S(2)}) collective-permute-start(bf16[1040,128]{1,0:T(8,128)(2,1)S(1)} %collective-permute-done.refs_2_), channel_id=1, source_target_pairs={{0,64},{1,65},{2,66},{3,67},{4,68},{5,69},{6,70},{7,71},{8,72},{9,... | collective-permute-start | bytes 798728 | tf_op jit(solution)/shard_map/ppermute | solution.py:30
  31.1 0.5 collective-permute-start.13
  31.6 1.2 copy-done
  32.8 4.1 %attend_own.1 = (f32[4096,128]{1,0:T(8,128)S(1)}, f32[4096,128]{1,0:T(8,128)S(1)}, f32[4096,128]{1,0:T(8,128)S(1)}) custom-call(bf16[4096,128]{1,0:T(8,128)(2,1)S(1)} %bitcast.10, bf16[1040,128]{1,0:T(8,128)(2,1)S(1)} %maximum_maximum_fusion.refs_1_, bf16[1040,128]{1,0:T(8,128)(2,1)S(1)} %collective-permute-done.14.refs_2_), custom_call_target="tpu_custom_call" | custom-call | flops 5368709120 | bytes 1048576 | tf_op jit(solution)/shard_map/attend_own/pallas_call | solution.py:215
  36.9 0.1 collective-permute-start.8
  37.0 0.5 collective-permute-start.9
  37.5 0.1 collective-permute-start.4
  37.6 2.3 %collective-permute-done.2.refs_3_ = bf16[1040,128]{1,0:T(8,128)(2,1)S(1)} collective-permute-done((bf16[1040,128]{1,0:T(8,128)(2,1)S(1)}, bf16[1040,128]{1,0:T(8,128)(2,1)S(1)}, u32[]{:S(2)}, u32[]{:S(2)}) %collective-permute-start.2) | collective-permute-done | bytes 266272 | tf_op jit(solution)/shard_map/ppermute | solution.py:30
  39.9 1.9 %collective-permute-done.3.refs_4_ = bf16[1040,128]{1,0:T(8,128)(2,1)S(1)} collective-permute-done((bf16[1040,128]{1,0:T(8,128)(2,1)S(1)}, bf16[1040,128]{1,0:T(8,128)(2,1)S(1)}, u32[]{:S(2)}, u32[]{:S(2)}) %collective-permute-start.3) | collective-permute-done | bytes 266272 | tf_op jit(solution)/shard_map/ppermute | solution.py:30
  41.8 0.0 collective-permute-start.6
  41.8 7.8 %attend_near.1 = (f32[4096,128]{1,0:T(8,128)S(1)}, f32[4096,128]{1,0:T(8,128)S(1)}, f32[4096,128]{1,0:T(8,128)S(1)}) custom-call(bf16[4096,128]{1,0:T(8,128)(2,1)S(1)} %bitcast.11, bf16[1040,128]{1,0:T(8,128)(2,1)S(1)} %maximum_maximum_fusion.refs_1_, ...), custom_call_target="tpu_custom_call", output_to_operand_aliasing={{0}: (6, {}), {1}: (7, {}), {2}: (8, {})} | custom-call | flops 8589934592 | bytes 1048576 | tf_op jit(solution)/shard_map/attend_near/pallas_call | solution.py:215
  49.6 7.8 %attend_over.1 = (f32[4096,128]{1,0:T(8,128)S(1)}, f32[4096,128]{1,0:T(8,128)S(1)}, f32[4096,128]{1,0:T(8,128)S(1)}) custom-call(bf16[4096,128]{1,0:T(8,128)(2,1)S(1)} %bitcast.12, bf16[1040,128]{1,0:T(8,128)(2,1)S(1)} %maximum_maximum_fusion.refs_1_, ...), custom_call_target="tpu_custom_call", output_to_operand_aliasing={{0}: (6, {}), {1}: (7, {}), {2}: (8, {})} | custom-call | flops 8589934592 | bytes 1048576 | tf_op jit(solution)/shard_map/attend_over/pallas_call | solution.py:215
  57.4 12.3 %attend_rest.1 = (bf16[512,1024]{1,0:T(8,128)(2,1)S(1)}, f32[4096,128]{1,0:T(8,128)S(1)}, f32[4096,128]{1,0:T(8,128)S(1)}, f32[4096,128]{1,0:T(8,128)S(1)}) custom-call(bf16[4096,128]{1,0:T(8,128)(2,1)S(1)} %bitcast.13, bf16[1040,128]{1,0:T(8,128)(2,1)S(1)} %maximum_maximum_fusion.refs_1_, ...), custom_call_target="tpu_custom_call", output_to_operand_aliasing={{1}: (8, {}), {2}: (9, {}), {3}: (10, {})} | custom-call | flops 12884901888 | bytes 1048576 | tf_op jit(solution)/shard_map/attend_rest/pallas_call | solution.py:215
  69.7 17.1 %convolution_convert_fusion = bf16[512,8192]{1,0:T(8,128)(2,1)} fusion(bf16[512,1024]{1,0:T(8,128)(2,1)S(1)} %get-tuple-element.24, bf16[1024,8192]{1,0:T(8,128)(2,1)} %param.13), kind=kOutput, calls=%fused_computation | convolution fusion | flops 8594128896 | bytes 26214400 | tf_op jit(solution)/shard_map/dot_general | solution.py:260
  86.8 0.0 reduce-scatter.2.cloned.1.call-update
  86.8 92.4 %reduce-scatter.2.cloned.1.call-done = bf16[64,8192]{1,0:T(8,128)(2,1)} async-done(((bf16[512,8192]{1,0:T(8,128)(2,1)}), bf16[64,8192]{1,0:T(8,128)(2,1)}) %reduce-scatter.2.cloned.1.call-update) | async-done | bytes 1048592 | tf_op jit(solution)/shard_map/reduce_scatter | solution.py:259
  (17 shorter events, 0.0 us)
Async XLA Ops:
  6.5 172.6 %reduce-scatter.2.cloned.1.call-start = ((), (), s32[]{:S(2)}) async-start(), calls=%async_computation.1 | async-start | bytes 9437184 | tf_op jit(solution)/shard_map/reduce_scatter | solution.py:259
  11.1 9.7 %collective-permute-start = (bf16[1040,128]{1,0:T(8,128)(2,1)S(1)}, bf16[1040,128]{1,0:T(8,128)(2,1)S(1)}, u32[]{:S(2)}, u32[]{:S(2)}) collective-permute-start(bf16[1040,128]{1,0:T(8,128)(2,1)S(1)} %maximum_maximum_fusion.refs_1_), channel_id=1, source_target_pairs={{0,16},{1,17},{2,18},{3,19},{4,20},{5,21},{6,22},{7,23},{8,24},{9,... | collective-permute-start | bytes 798728 | tf_op jit(solution)/shard_map/ppermute | solution.py:30
  12.4 10.3 %collective-permute-start.14 = (bf16[1040,128]{1,0:T(8,128)(2,1)S(1)}, bf16[1040,128]{1,0:T(8,128)(2,1)S(1)}, u32[]{:S(2)}, u32[]{:S(2)}) collective-permute-start(bf16[1040,128]{1,0:T(8,128)(2,1)S(1)} %maximum_maximum_fusion.refs_1_), channel_id=1, source_target_pairs={{0,8},{1,9},{2,10},{3,11},{4,12},{5,13},{6,14},{7,15},{8,0},{9,1},... | collective-permute-start | bytes 798728 | tf_op jit(solution)/shard_map/ppermute | solution.py:30
  12.4 12.4 %collective-permute-start.10 = (bf16[1040,128]{1,0:T(8,128)(2,1)S(1)}, bf16[1040,128]{1,0:T(8,128)(2,1)S(1)}, u32[]{:S(2)}, u32[]{:S(2)}) collective-permute-start(bf16[1040,128]{1,0:T(8,128)(2,1)S(1)} %maximum_maximum_fusion.refs_1_), channel_id=1, source_target_pairs={{0,32},{1,33},{2,34},{3,35},{4,36},{5,37},{6,38},{7,39},{8,40},{9,... | collective-permute-start | bytes 798728 | tf_op jit(solution)/shard_map/ppermute | solution.py:30
  14.3 16.8 %collective-permute-start.11 = (bf16[1040,128]{1,0:T(8,128)(2,1)S(1)}, bf16[1040,128]{1,0:T(8,128)(2,1)S(1)}, u32[]{:S(2)}, u32[]{:S(2)}) collective-permute-start(bf16[1040,128]{1,0:T(8,128)(2,1)S(1)} %maximum_maximum_fusion.refs_1_), channel_id=1, source_target_pairs={{0,96},{1,97},{2,98},{3,99},{4,100},{5,101},{6,102},{7,103},{8,104... | collective-permute-start | bytes 798728 | tf_op jit(solution)/shard_map/ppermute | solution.py:30
  16.4 14.6 %collective-permute-start.7 = (bf16[1040,128]{1,0:T(8,128)(2,1)S(1)}, bf16[1040,128]{1,0:T(8,128)(2,1)S(1)}, u32[]{:S(2)}, u32[]{:S(2)}) collective-permute-start(bf16[1040,128]{1,0:T(8,128)(2,1)S(1)} %maximum_maximum_fusion.refs_1_), channel_id=1, source_target_pairs={{0,64},{1,65},{2,66},{3,67},{4,68},{5,69},{6,70},{7,71},{8,72},{9,... | collective-permute-start | bytes 798728 | tf_op jit(solution)/shard_map/ppermute | solution.py:30
  20.8 16.7 %collective-permute-start.1 = (bf16[1040,128]{1,0:T(8,128)(2,1)S(1)}, bf16[1040,128]{1,0:T(8,128)(2,1)S(1)}, u32[]{:S(2)}, u32[]{:S(2)}) collective-permute-start(bf16[1040,128]{1,0:T(8,128)(2,1)S(1)} %collective-permute-done.refs_2_), channel_id=1, source_target_pairs={{0,32},{1,33},{2,34},{3,35},{4,36},{5,37},{6,38},{7,39},{8,40},{9,... | collective-permute-start | bytes 798728 | tf_op jit(solution)/shard_map/ppermute | solution.py:30
  22.7 17.2 %collective-permute-start.2 = (bf16[1040,128]{1,0:T(8,128)(2,1)S(1)}, bf16[1040,128]{1,0:T(8,128)(2,1)S(1)}, u32[]{:S(2)}, u32[]{:S(2)}) collective-permute-start(bf16[1040,128]{1,0:T(8,128)(2,1)S(1)} %collective-permute-done.refs_2_), channel_id=1, source_target_pairs={{0,96},{1,97},{2,98},{3,99},{4,100},{5,101},{6,102},{7,103},{8,104... | collective-permute-start | bytes 798728 | tf_op jit(solution)/shard_map/ppermute | solution.py:30
  24.8 17.0 %collective-permute-start.3 = (bf16[1040,128]{1,0:T(8,128)(2,1)S(1)}, bf16[1040,128]{1,0:T(8,128)(2,1)S(1)}, u32[]{:S(2)}, u32[]{:S(2)}) collective-permute-start(bf16[1040,128]{1,0:T(8,128)(2,1)S(1)} %collective-permute-done.refs_2_), channel_id=1, source_target_pairs={{0,64},{1,65},{2,66},{3,67},{4,68},{5,69},{6,70},{7,71},{8,72},{9,... | collective-permute-start | bytes 798728 | tf_op jit(solution)/shard_map/ppermute | solution.py:30
  31.1 5.8 %collective-permute-start.12 = (bf16[1040,128]{1,0:T(8,128)(2,1)S(1)}, bf16[1040,128]{1,0:T(8,128)(2,1)S(1)}, u32[]{:S(2)}, u32[]{:S(2)}) collective-permute-start(bf16[1040,128]{1,0:T(8,128)(2,1)S(1)} %collective-permute-done.10.refs_2_), channel_id=1, source_target_pairs={{0,8},{1,9},{2,10},{3,11},{4,12},{5,13},{6,14},{7,15},{8,0},{9,1},... | collective-permute-start | bytes 798728 | tf_op jit(solution)/shard_map/ppermute | solution.py:30
  31.1 5.9 %collective-permute-start.13 = (bf16[1040,128]{1,0:T(8,128)(2,1)S(1)}, bf16[1040,128]{1,0:T(8,128)(2,1)S(1)}, u32[]{:S(2)}, u32[]{:S(2)}) collective-permute-start(bf16[1040,128]{1,0:T(8,128)(2,1)S(1)} %collective-permute-done.11.refs_3_), channel_id=1, source_target_pairs={{0,8},{1,9},{2,10},{3,11},{4,12},{5,13},{6,14},{7,15},{8,0},{9,1},... | collective-permute-start | bytes 798728 | tf_op jit(solution)/shard_map/ppermute | solution.py:30
  31.6 1.2 copy-start
  36.9 12.7 %collective-permute-start.8 = (bf16[1040,128]{1,0:T(8,128)(2,1)S(1)}, bf16[1040,128]{1,0:T(8,128)(2,1)S(1)}, u32[]{:S(2)}, u32[]{:S(2)}) collective-permute-start(bf16[1040,128]{1,0:T(8,128)(2,1)S(1)} %collective-permute-done.refs_2_), channel_id=1, source_target_pairs={{0,8},{1,9},{2,10},{3,11},{4,12},{5,13},{6,14},{7,15},{8,0},{9,1},... | collective-permute-start | bytes 798728 | tf_op jit(solution)/shard_map/ppermute | solution.py:30
  37.0 12.6 %collective-permute-start.9 = (bf16[1040,128]{1,0:T(8,128)(2,1)S(1)}, bf16[1040,128]{1,0:T(8,128)(2,1)S(1)}, u32[]{:S(2)}, u32[]{:S(2)}) collective-permute-start(bf16[1040,128]{1,0:T(8,128)(2,1)S(1)} %collective-permute-done.7.refs_3_), channel_id=1, source_target_pairs={{0,8},{1,9},{2,10},{3,11},{4,12},{5,13},{6,14},{7,15},{8,0},{9,1},... | collective-permute-start | bytes 798728 | tf_op jit(solution)/shard_map/ppermute | solution.py:30
  37.5 19.9 %collective-permute-start.4 = (bf16[1040,128]{1,0:T(8,128)(2,1)S(1)}, bf16[1040,128]{1,0:T(8,128)(2,1)S(1)}, u32[]{:S(2)}, u32[]{:S(2)}) collective-permute-start(bf16[1040,128]{1,0:T(8,128)(2,1)S(1)} %collective-permute-done.1.refs_2_), channel_id=1, source_target_pairs={{0,8},{1,9},{2,10},{3,11},{4,12},{5,13},{6,14},{7,15},{8,0},{9,1},... | collective-permute-start | bytes 798728 | tf_op jit(solution)/shard_map/ppermute | solution.py:30
  39.9 17.5 %collective-permute-start.5 = (bf16[1040,128]{1,0:T(8,128)(2,1)S(1)}, bf16[1040,128]{1,0:T(8,128)(2,1)S(1)}, u32[]{:S(2)}, u32[]{:S(2)}) collective-permute-start(bf16[1040,128]{1,0:T(8,128)(2,1)S(1)} %collective-permute-done.2.refs_3_), channel_id=1, source_target_pairs={{0,8},{1,9},{2,10},{3,11},{4,12},{5,13},{6,14},{7,15},{8,0},{9,1},... | collective-permute-start | bytes 798728 | tf_op jit(solution)/shard_map/ppermute | solution.py:30
  41.8 15.6 %collective-permute-start.6 = (bf16[1040,128]{1,0:T(8,128)(2,1)S(1)}, bf16[1040,128]{1,0:T(8,128)(2,1)S(1)}, u32[]{:S(2)}, u32[]{:S(2)}) collective-permute-start(bf16[1040,128]{1,0:T(8,128)(2,1)S(1)} %collective-permute-done.3.refs_4_), channel_id=1, source_target_pairs={{0,8},{1,9},{2,10},{3,11},{4,12},{5,13},{6,14},{7,15},{8,0},{9,1},... | collective-permute-start | bytes 798728 | tf_op jit(solution)/shard_map/ppermute | solution.py:30
Sparse Core Ops, SparseCore 0:
  86.9 92.1 reduce-scatter.1

commit v2 on v1

--- a/solution.py
+++ b/solution.py
@@ -1,3 +1,4 @@
+import functools
 import itertools
 import math
 
@@ -16,18 +17,50 @@
 NT = (((1,), (1,)), ((), ()))
 NN = (((1,), (0,)), ((), ()))
 META = 16
+PAYLOAD = 1024 + META
 
 
 def index_of(z, yh, c, yl, x):
     return ((z % 4) * 4 + (yh % 2) * 2 + c % 2) * 8 + (yl % 2) * 4 + x % 4
 
 
-def moved(array, step):
+def moved(array, target):
     pairs = []
-    for z, yh, c, yl, x in itertools.product(range(4), range(2), range(2), range(2), range(4)):
-        target = tuple(a + b for a, b in zip((z, yh, c, yl, x), step))
-        pairs.append((index_of(z, yh, c, yl, x), index_of(*target)))
+    for at in itertools.product(range(4), range(2), range(2), range(2), range(4)):
+        pairs.append((index_of(*at), index_of(*target(*at))))
     return lax.ppermute(array, AXES, pairs)
+
+
+def swapped(z, yh, c, yl, x):
+    return z, yh, 1 - c, yl, x
+
+
+def near(z, yh, c, yl, x):
+    return z + (1 if c == 0 else -1), yh, c, yl, x
+
+
+def across(z, yh, c, yl, x):
+    return (z, yh + 1, c, yl, x) if c == 0 else (z + 2, yh, c, yl, x)
+
+
+def diagonal(z, yh, c, yl, x):
+    return z + (1 if c == 0 else -1), yh + 1, c, yl, x
+
+
+def opposite(z, yh, c, yl, x):
+    return z + 2, yh + 1, c, yl, x
+
+
+def ahead(z, yh, c, yl, x):
+    return z, yh, c, yl, x + (1 if c == 0 else -1)
+
+
+def behind(z, yh, c, yl, x):
+    return z, yh, c, yl, x - (1 if c == 0 else -1)
+
+
+def beside(z, yh, c, yl, x):
+    return z, yh, c, yl + 1, x
 
 
 def attend_rows(q_ref, acc_ref, l_ref, m_ref, base, count, keys, vals, gains, first=False, visible=None):
@@ -89,8 +122,8 @@
     )
 
 
-def place_of(ref):
-    return jnp.max(ref[1026:1027, :].astype(F32)).astype(jnp.int32)
+def place_of(ref, offset=0):
+    return jnp.max(ref[offset + 1026 : offset + 1027, :].astype(F32)).astype(jnp.int32)
 
 
 def other_steps(q_ref, acc_ref, l_ref, m_ref, own_place, refs, kbuf, vbuf, gbuf, inv):
@@ -99,19 +132,20 @@
     highs = jnp.int32(count)
     lows = jnp.int32(0)
 
-    def put(slot, ref, half):
+    def put(slot, ref, offset, half):
         at = pl.ds(pl.multiple_of(slot * 256, 256), 256)
-        kbuf[at, :] = ref[pl.ds(pl.multiple_of(half * 256, 256), 256), :]
-        vbuf[at, :128] = ref[pl.ds(pl.multiple_of(512 + half * 256, 256), 256), :]
-        gain = jnp.where(half == 0, ref[1024:1025, :].astype(F32), ref[1025:1026, :].astype(F32))
-        gbuf[pl.ds(slot, 1), :] = gain * inv
-
-    for i, ref in enumerate(refs):
-        put(i, ref, 0)
-    for ref in refs:
-        is_low = (place_of(ref) < own_place).astype(jnp.int32)
+        source = pl.multiple_of(half * 256, 256)
+        kbuf[at, :] = ref[pl.ds(offset + source, 256), :]
+        vbuf[at, :128] = ref[pl.ds(offset + 512 + source, 256), :]
+        gains = ref[offset + 1024 : offset + 1026, :].astype(F32)
+        gbuf[pl.ds(slot, 1), :] = jnp.where(half == 0, gains[0:1], gains[1:2]) * inv
+
+    for i, (ref, offset) in enumerate(refs):
+        put(i, ref, offset, 0)
+    for ref, offset in refs:
+        is_low = (place_of(ref, offset) < own_place).astype(jnp.int32)
         slot = jnp.where(is_low == 1, 2 * count - 1 - lows, highs)
-        put(slot, ref, 1 - is_low)
+        put(slot, ref, offset, 1 - is_low)
         lows = lows + is_low
         highs = highs + 1 - is_low
 
@@ -167,66 +201,135 @@
     lax.fori_loop(0, count, step, 0)
 
 
-def group_kernel(inv, count, start, finish, *refs):
+def group_kernel(inv, sizes, start, finish, *refs):
     refs = list(refs)
     q_ref = refs.pop(0)
     own_ref = refs.pop(0)
-    others = [refs.pop(0) for _ in range(count)]
+    order_ref = refs.pop(0) if finish else None
+    others = []
+    for size in sizes:
+        ref = refs.pop(0)
+        others += [(ref, i * PAYLOAD) for i in range(size)]
     if not start:
         del refs[:3]
     att_ref = refs.pop(0) if finish else None
     acc_ref, l_ref, m_ref, kbuf, vbuf, gbuf = refs
     if start:
         own_steps(q_ref, acc_ref, l_ref, m_ref, own_ref, inv)
-    other_steps(q_ref, acc_ref, l_ref, m_ref, place_of(own_ref), others, kbuf, vbuf, gbuf, inv)
+    own_place = place_of(own_ref)
+    other_steps(q_ref, acc_ref, l_ref, m_ref, own_place, others, kbuf, vbuf, gbuf, inv)
     if finish:
         acc_ref[...] = acc_ref[...] / l_ref[...]
-        for h in range(8):
-            rows = pl.ds(h, 512, stride=8)
-            att_ref[:, h * 128 : (h + 1) * 128] = acc_ref[rows, :].astype(BF16)
-
-
-def attend(q, own, others, state, finish, inv, name):
-    count = len(others)
+        for block in range(8):
+            target = pl.ds(pl.multiple_of(order_ref[block] * 64, 64), 64)
+            for h in range(8):
+                rows = pl.ds(block * 512 + h, 64, stride=8)
+                att_ref[target, h * 128 : (h + 1) * 128] = acc_ref[rows, :].astype(BF16)
+
+
+def attend(q, own, others, state, order, inv, name):
+    sizes = [o.shape[0] // PAYLOAD for o in others]
+    count = sum(sizes)
     start = state is None
+    finish = order is not None
     vmem = pl.BlockSpec(memory_space=pltpu.VMEM)
     shapes = [jax.ShapeDtypeStruct((4096, 128), F32)] * 3
-    operands = [q, own, *others] + ([] if start else list(state))
-    scratch = [
-        pltpu.VMEM((2 * count * 256, 128), BF16),
-        pltpu.VMEM((2 * count * 256, 256), BF16),
-        pltpu.VMEM((2 * count, 128), F32),
-    ]
+    operands = [q, own] + ([order] if finish else []) + list(others)
+    specs = [vmem] * len(operands)
+    if finish:
+        specs[2] = pl.BlockSpec(memory_space=pltpu.SMEM)
+    outs = ([jax.ShapeDtypeStruct((512, 1024), BF16)] if finish else []) + shapes
     aliases = {}
-    if finish:
-        outs = [jax.ShapeDtypeStruct((512, 1024), BF16)]
-        scratch = [pltpu.VMEM(s.shape, s.dtype) for s in shapes] + scratch
-        if not start:
-            outs = outs + shapes
-            scratch = scratch[3:]
-            aliases = {2 + count + i: 1 + i for i in range(3)}
-    else:
-        outs = shapes
-        if not start:
-            aliases = {2 + count + i: i for i in range(3)}
+    if not start:
+        shift = len(outs) - 3
+        aliases = {len(operands) + i: shift + i for i in range(3)}
+        operands += list(state)
+        specs += [vmem] * 3
     tiles = 2 * count + (3 if start else 0)
-    import functools
-
     return pl.pallas_call(
-        functools.partial(group_kernel, inv, count, start, finish),
+        functools.partial(group_kernel, inv, sizes, start, finish),
         out_shape=outs,
-        in_specs=[vmem] * len(operands),
+        in_specs=specs,
         out_specs=[vmem] * len(outs),
-        scratch_shapes=scratch,
+        scratch_shapes=[
+            pltpu.VMEM((2 * count * 256, 128), BF16),
+            pltpu.VMEM((2 * count * 256, 256), BF16),
+            pltpu.VMEM((2 * count, 128), F32),
+        ],
         input_output_aliases=aliases,
-        compiler_params=pltpu.CompilerParams(vmem_limit_bytes=40 << 20),
+        compiler_params=pltpu.CompilerParams(vmem_limit_bytes=32 << 20),
         cost_estimate=pl.CostEstimate(
-            flops=tiles * 4 * 2048 * 256 * 128 * 4,
+            flops=tiles * 2048 * 256 * 128 * 16,
             transcendentals=tiles * 2048 * 256,
             bytes_accessed=1 << 20,
         ),
         name=name,
     )(*operands)
+
+
+def project_kernel(blocks, splits, a_ref, w_ref, *o_refs):
+    rows = jnp.concatenate([a_ref[b * 64 : (b + 1) * 64, :] for b in blocks], axis=0)
+    product = jnp.dot(rows, w_ref[...], preferred_element_type=F32).astype(BF16)
+    at = 0
+    for size, o_ref in zip(splits, o_refs):
+        o_ref[...] = product[at * 64 : (at + size) * 64, :]
+        at += size
+
+
+def project(att, weight, blocks, splits, first, columns, name):
+    tile = 1024
+    start = first // tile
+    return pl.pallas_call(
+        functools.partial(project_kernel, blocks, splits),
+        out_shape=[jax.ShapeDtypeStruct((s * 64, columns), BF16) for s in splits],
+        grid=(columns // tile,),
+        in_specs=[
+            pl.BlockSpec((512, 1024), lambda j: (0, 0)),
+            pl.BlockSpec((1024, tile), lambda j: (0, j + start)),
+        ],
+        out_specs=[pl.BlockSpec((s * 64, tile), lambda j: (0, j)) for s in splits],
+        compiler_params=pltpu.CompilerParams(vmem_limit_bytes=24 << 20),
+        cost_estimate=pl.CostEstimate(
+            flops=2 * len(blocks) * 64 * 1024 * columns,
+            transcendentals=0,
+            bytes_accessed=2 * 1024 * columns,
+        ),
+        name=name,
+    )(att, weight)
+
+
+def added(*arrays):
+    total = arrays[0].astype(F32)
+    for a in arrays[1:]:
+        total = total + a.astype(F32)
+    return total
+
+
+def scattered(att, weight, first_columns):
+    rest = weight.shape[1] - first_columns
+    x_far, x_behind = project(att, weight, (0, 1, 4, 5), (2, 2), 0, first_columns, "project_a")
+    got_far = moved(x_far, ahead)
+    got_front = moved(x_behind, behind)
+    (y_out,) = project(att, weight, (1, 3, 5, 7), (4,), first_columns, rest, "project_b")
+    got_y = moved(y_out, beside)
+    x_ahead, x_own = project(att, weight, (2, 3, 6, 7), (2, 2), 0, first_columns, "project_c")
+    (y_own,) = project(att, weight, (0, 2, 4, 6), (4,), first_columns, rest, "project_d")
+    got_back = moved(added(x_ahead, got_far).astype(BF16), ahead)
+    y_far, y_ahead, y_behind, y_mine = [
+        (y_own[i * 64 : (i + 1) * 64], got_y[i * 64 : (i + 1) * 64]) for i in range(4)
+    ]
+    y_got_far = moved(added(*y_far).astype(BF16), ahead)
+    y_got_front = moved(added(*y_behind).astype(BF16), behind)
+    y_got_back = moved(added(*y_ahead, y_got_far).astype(BF16), ahead)
+    x_out = added(x_own[64:], got_front[64:], got_back[64:]).astype(BF16)
+    x_last = moved(x_out, beside)
+    return jnp.concatenate(
+        [
+            added(x_own[:64], got_front[:64], got_back[:64], x_last).astype(BF16),
+            added(*y_mine, y_got_front, y_got_back).astype(BF16),
+        ],
+        axis=1,
+    )
 
 
 def body(query, keys, values, k_scale, v_scale, block_place, out_weight):
@@ -239,29 +342,28 @@
         [k_scale.reshape(2), block_place.astype(BF16), jnp.zeros((META - 4,), BF16)]
     )
     own = jnp.concatenate([k, v, jnp.broadcast_to(meta[:, None], (META, 128))], axis=0)
-    swap = (0, 0, 1, 0, 0)
-    partner = moved(own, swap)
-    up = moved(own, (1, 0, 0, 0, 0))
-    down = moved(own, (-1, 0, 0, 0, 0))
-    over = moved(own, (0, 1, 0, 0, 0))
-    far = moved(own, (2, 0, 0, 0, 0))
-    up2, down2 = moved(up, swap), moved(down, swap)
-    state = attend(q, own, [partner], None, False, inv, "attend_own")
-    state = attend(q, own, [up, down, up2, down2], state, False, inv, "attend_near")
-    over2, far2 = moved(over, swap), moved(far, swap)
-    oup = moved(over, (1, 0, 0, 0, 0))
-    odown = moved(over, (-1, 0, 0, 0, 0))
-    ofar = moved(over, (2, 0, 0, 0, 0))
-    state = attend(q, own, [over, far, over2, far2], state, False, inv, "attend_over")
-    rest = [oup, odown, ofar]
-    rest = rest + [moved(r, swap) for r in rest]
-    attended = attend(q, own, rest, state, True, inv, "attend_rest")[0]
-    return lax.psum_scatter(
-        jnp.dot(attended, out_weight, preferred_element_type=F32).astype(BF16),
-        "head",
-        scatter_dimension=0,
-        tiled=True,
-    )
+    partner = moved(own, swapped)
+    pair = jnp.concatenate([own, partner], axis=0)
+    one, two, three = moved(pair, near), moved(pair, across), moved(pair, diagonal)
+    four = moved(own, opposite)
+    state = attend(q, own, [partner], None, None, inv, "attend_own")
+    one, two, *state = lax.optimization_barrier((one, two, *state))
+    more = moved(jnp.concatenate([one, two], axis=0), swapped)
+    state = attend(q, own, [one, two], state, None, inv, "attend_near")
+    three, four, *state = lax.optimization_barrier((three, four, *state))
+    last = jnp.concatenate([three, four], axis=0)
+    final = moved(last, swapped)
+    state = attend(q, own, [more], state, None, inv, "attend_more")
+    core = lax.axis_index("ctx") % 2
+    place = lax.axis_index("head")
+    target = jnp.arange(8, dtype=jnp.int32)
+    along = (target % 4 - place % 4) % 4
+    side = (target // 4 - place // 4) % 2
+    forward = 1 + 2 * core
+    slot = jnp.where(along == 0, 3, jnp.where(along == 2, 0, jnp.where(along == forward, 1, 2)))
+    order = (slot * 2 + side).astype(jnp.int32)
+    attended = attend(q, own, [last, final], state, order, inv, "attend_rest")[0]
+    return scattered(attended, out_weight, 5120)
 
 
 def solution(mesh):

time: 188 us -> 152 us (0.81)
  waiting for transfers between devices: 99.1 us -> 59.7 us
  matrix products: 17.1 us -> 0 us
  between operations: 13.5 us -> 0.24 us
  starting transfers between devices: 18.7 us -> 29.5 us
  Pallas kernels: 31.9 us -> 42.5 us
  local copies, waits for them, and re-layouts: 1.31 us -> 9.05 us
  other arithmetic: 4.42 us -> 7.79 us
    reduce_scatter x1 -> x0, waiting for transfers between devices: 92.4 us -> none  [body(): lax.psum_scatter(jnp.dot(attended, out_weight, preferred_element_type=F32...]
    ppermute x15, waiting for transfers between devices: 6.75 us -> 59.7 us  [moved(): return lax.ppermute(array, AXES, pairs)]
    dot_general x1 -> x0, matrix products: 17.1 us -> none  [body(): jnp.dot(attended, out_weight, preferred_element_type=F32).astype(BF16)]
    ppermute x15, starting transfers between devices: 18.7 us -> 29.5 us  [moved(): return lax.ppermute(array, AXES, pairs)]
    pallas_call x4 -> x8, Pallas kernels: 31.9 us -> 42.5 us  [the longest x4 28.4 us: attend(): pl.pallas_call(functools.partial(group_kernel, inv, sizes, start, finish)...]
    unnamed x4 -> x25, local copies, waits for them, and re-layouts: 1.3 us -> 8.93 us
    concatenate x0 -> x3, other arithmetic: none -> 2.05 us  [the longest x1 1.04 us: scattered(): jnp.concatenate([added(x_own[:64], got_front[:64], got_back[:64], x_last)...]
  transfers between devices with their start and end apart: 16 -> 15, of which waited for: 4 -> 7; matrix products, arithmetic and copies ran while one was open for 0% -> 1% of each run, Pallas kernels for 11% -> 18%
where the time goes in v2:
time: 152 us; the launch traced here: 149 us
  waiting for transfers between devices  59.7 us (39%)
  Pallas kernels  42.5 us (28%)
  starting transfers between devices  29.5 us (19%)
  local copies, waits for them, and re-layouts  9.05 us (6%)
  other arithmetic  7.79 us (5%)
    ppermute x15, waiting for transfers between devices, moved(): return lax.ppermute(array, AXES, pairs)  59.7 us
    ppermute x15, starting transfers between devices, moved(): return lax.ppermute(array, AXES, pairs)  29.5 us
    pallas_call x4, Pallas kernels, attend(): pl.pallas_call(functools.partial(group_kernel, inv, sizes, start, finish)...  28.4 us
    pallas_call x4, Pallas kernels, project(): pl.pallas_call(functools.partial(project_kernel, blocks, splits), out_sha...  14.2 us
    unnamed x25, local copies, waits for them, and re-layouts  8.93 us
  transfers between devices with their start and end apart: 15, of which 7 were waited for; matrix products, arithmetic and copies ran while one was open for 1% of the time, Pallas kernels for 18%

profile of v2, /device:TPU:24, one launch (start us, length us, event | category | flops | bytes accessed | tf_op | source)
XLA Modules:
  0.0 148.9 jit_solution(6581052946307299245)
XLA Ops:
  1.6 1.0 fusion
  4.6 4.6 %collective-permute-start.2 = (bf16[1040,128]{1,0:T(8,128)(2,1)S(1)}, bf16[1040,128]{1,0:T(8,128)(2,1)S(1)}, u32[]{:S(2)}, u32[]{:S(2)}) collective-permute-start(bf16[1040,128]{1,0:T(8,128)(2,1)S(1)} %pad_maximum_fusion.3.refs_1_), channel_id=1, source_target_pairs={{0,80},{1,81},{2,82},{3,83},{4,84},{5,85},{6,86},{7,87},{8,88},{9,... | collective-permute-start | bytes 798728 | tf_op jit(solution)/shard_map/ppermute | solution.py:31
  10.2 1.1 collective-permute-start.3
  11.3 2.3 %collective-permute-start.4 = (bf16[2080,128]{1,0:T(8,128)(2,1)S(1)}, bf16[2080,128]{1,0:T(8,128)(2,1)S(1)}, u32[]{:S(2)}, u32[]{:S(2)}) collective-permute-start(bf16[2080,128]{1,0:T(8,128)(2,1)S(1)} %pad_maximum_fusion.2), channel_id=1, source_target_pairs={{0,16},{1,17},{2,18},{3,19},{4,20},{5,21},{6,22},{7,23},{8,72},{9,... | collective-permute-start | bytes 1597448 | tf_op jit(solution)/shard_map/ppermute | solution.py:31
  14.4 3.9 %attend_own.1 = (f32[4096,128]{1,0:T(8,128)S(1)}, f32[4096,128]{1,0:T(8,128)S(1)}, f32[4096,128]{1,0:T(8,128)S(1)}) custom-call(bf16[4096,128]{1,0:T(8,128)(2,1)S(1)} %bitcast.10, bf16[1040,128]{1,0:T(8,128)(2,1)S(1)} %pad_maximum_fusion.3.refs_1_, bf16[1040,128]{1,0:T(8,128)(2,1)S(1)} %collective-permute-done.refs_2_), custom_call_target="tpu_custom_call" | custom-call | flops 5368709120 | bytes 1048576 | tf_op jit(solution)/shard_map/attend_own/pallas_call | solution.py:249
  18.3 10.5 %collective-permute-done.3.refs_2_ = bf16[2080,128]{1,0:T(8,128)(2,1)S(1)} collective-permute-done((bf16[2080,128]{1,0:T(8,128)(2,1)S(1)}, bf16[2080,128]{1,0:T(8,128)(2,1)S(1)}, u32[]{:S(2)}, u32[]{:S(2)}) %collective-permute-start.3) | collective-permute-done | bytes 532512 | tf_op jit(solution)/shard_map/ppermute | solution.py:31
  30.4 6.7 %attend_near.1 = (f32[4096,128]{1,0:T(8,128)S(1)}, f32[4096,128]{1,0:T(8,128)S(1)}, f32[4096,128]{1,0:T(8,128)S(1)}) custom-call(bf16[4096,128]{1,0:T(8,128)(2,1)S(1)} %bitcast.11, bf16[1040,128]{1,0:T(8,128)(2,1)S(1)} %pad_maximum_fusion.3.refs_1_, ...), custom_call_target="tpu_custom_call", output_to_operand_aliasing={{0}: (4, {}), {1}: (5, {}), {2}: (6, {})} | custom-call | flops 8589934592 | bytes 1048576 | tf_op jit(solution)/shard_map/attend_near/pallas_call | solution.py:249
  37.5 6.7 %attend_more.1 = (f32[4096,128]{1,0:T(8,128)S(1)}, f32[4096,128]{1,0:T(8,128)S(1)}, f32[4096,128]{1,0:T(8,128)S(1)}) custom-call(bf16[4096,128]{1,0:T(8,128)(2,1)S(1)} %bitcast.12, bf16[1040,128]{1,0:T(8,128)(2,1)S(1)} %pad_maximum_fusion.3.refs_1_, ...), custom_call_target="tpu_custom_call", output_to_operand_aliasing={{0}: (3, {}), {1}: (4, {}), {2}: (5, {})} | custom-call | flops 8589934592 | bytes 1048576 | tf_op jit(solution)/shard_map/attend_more/pallas_call | solution.py:249
  44.1 1.3 copy-done.1
  45.5 1.3 copy-done.3
  46.8 1.4 copy-done.5
  48.2 1.6 %copy-done.2 = f32[4096,128]{1,0:T(8,128)S(1)} copy-done((f32[4096,128]{1,0:T(8,128)S(1)}, f32[4096,128]{1,0:T(8,128)}, u32[]{:S(2)}) %copy-start.2) | copy-done | bytes 2097176
  49.8 1.6 %copy-done.4 = f32[4096,128]{1,0:T(8,128)S(1)} copy-done((f32[4096,128]{1,0:T(8,128)S(1)}, f32[4096,128]{1,0:T(8,128)}, u32[]{:S(2)}) %copy-start.4) | copy-done | bytes 2097176
  51.4 1.6 %copy-done.6 = f32[4096,128]{1,0:T(8,128)S(1)} copy-done((f32[4096,128]{1,0:T(8,128)S(1)}, f32[4096,128]{1,0:T(8,128)}, u32[]{:S(2)}) %copy-start.6) | copy-done | bytes 2097176
  52.9 11.2 %attend_rest.1 = (bf16[512,1024]{1,0:T(8,128)(2,1)S(1)}, f32[4096,128]{1,0:T(8,128)S(1)}, f32[4096,128]{1,0:T(8,128)S(1)}, f32[4096,128]{1,0:T(8,128)S(1)}) custom-call(bf16[4096,128]{1,0:T(8,128)(2,1)S(1)} %bitcast.13, bf16[1040,128]{1,0:T(8,128)(2,1)S(1)} %pad_maximum_fusion.3.refs_1_, ...), custom_call_target="tpu_custom_call", output_to_operand_aliasing={{1}: (5, {}), {2}: (6, {}), {3}: (7, {})} | custom-call | flops 12884901888 | bytes 1048576 | tf_op jit(solution)/shard_map/attend_rest/pallas_call | solution.py:249
  64.2 4.4 %project_a.1 = (bf16[128,5120]{1,0:T(8,128)(2,1)S(1)}, bf16[128,5120]{1,0:T(8,128)(2,1)S(1)}) custom-call(bf16[512,1024]{1,0:T(8,128)(2,1)S(1)} %get-tuple-element.48.a_ref, bf16[1024,8192]{1,0:T(8,128)(2,1)S(1)} %bitcast.9), custom_call_target="tpu_custom_call" | custom-call | flops 2684354560 | bytes 10485760 | tf_op jit(solution)/shard_map/project_a/pallas_call | solution.py:282
  68.6 1.6 %collective-permute-start.8 = (bf16[128,5120]{1,0:T(8,128)(2,1)S(1)}, bf16[128,5120]{1,0:T(8,128)(2,1)S(1)}, u32[]{:S(2)}, u32[]{:S(2)}) collective-permute-start(bf16[128,5120]{1,0:T(8,128)(2,1)S(1)} %get-tuple-element.52), channel_id=1, source_target_pairs={{0,1},{1,2},{2,3},{3,0},{4,5},{5,6},{6,7},{7,4},{8,11},{9,8},{10,9... | collective-permute-start | bytes 3932168 | tf_op jit(solution)/shard_map/ppermute | solution.py:31
  70.2 1.7 %collective-permute-start.7 = (bf16[128,5120]{1,0:T(8,128)(2,1)S(1)}, bf16[128,5120]{1,0:T(8,128)(2,1)S(1)}, u32[]{:S(2)}, u32[]{:S(2)}) collective-permute-start(bf16[128,5120]{1,0:T(8,128)(2,1)S(1)} %get-tuple-element.50), channel_id=1, source_target_pairs={{0,3},{1,0},{2,1},{3,2},{4,7},{5,4},{6,5},{7,6},{8,9},{9,10},{10,1... | collective-permute-start | bytes 3932168 | tf_op jit(solution)/shard_map/ppermute | solution.py:31
  71.9 2.7 %project_b.1 = bf16[256,3072]{1,0:T(8,128)(2,1)S(1)} custom-call(bf16[512,1024]{1,0:T(8,128)(2,1)S(1)} %get-tuple-element.48.a_ref, bf16[1024,8192]{1,0:T(8,128)(2,1)S(1)} %bitcast.9), custom_call_target="tpu_custom_call" | custom-call | flops 1610612736 | bytes 6291456 | tf_op jit(solution)/shard_map/project_b/pallas_call | solution.py:282
  74.6 5.0 %collective-permute-start.11 = (bf16[256,3072]{1,0:T(8,128)(2,1)S(1)}, bf16[256,3072]{1,0:T(8,128)(2,1)S(1)}, u32[]{:S(2)}, u32[]{:S(2)}) collective-permute-start(bf16[256,3072]{1,0:T(8,128)(2,1)S(1)} %project_b.1), channel_id=1, source_target_pairs={{0,4},{1,5},{2,6},{3,7},{4,0},{5,1},{6,2},{7,3},{8,12},{9,13},{10,... | collective-permute-start | bytes 4718600 | tf_op jit(solution)/shard_map/ppermute | solution.py:31
  79.6 2.7 %project_d.1 = bf16[256,3072]{1,0:T(8,128)(2,1)S(1)} custom-call(bf16[512,1024]{1,0:T(8,128)(2,1)S(1)} %get-tuple-element.48.a_ref, bf16[1024,8192]{1,0:T(8,128)(2,1)S(1)} %bitcast.9), custom_call_target="tpu_custom_call" | custom-call | flops 1610612736 | bytes 6291456 | tf_op jit(solution)/shard_map/project_d/pallas_call | solution.py:282
  82.2 4.4 %project_c.1 = (bf16[128,5120]{1,0:T(8,128)(2,1)S(1)}, bf16[128,5120]{1,0:T(8,128)(2,1)S(1)}) custom-call(bf16[512,1024]{1,0:T(8,128)(2,1)S(1)} %get-tuple-element.48.a_ref, bf16[1024,8192]{1,0:T(8,128)(2,1)S(1)} %bitcast.9), custom_call_target="tpu_custom_call" | custom-call | flops 2684354560 | bytes 10485760 | tf_op jit(solution)/shard_map/project_c/pallas_call | solution.py:282
  86.7 12.8 %collective-permute-done.8 = bf16[128,5120]{1,0:T(8,128)(2,1)S(1)} collective-permute-done((bf16[128,5120]{1,0:T(8,128)(2,1)S(1)}, bf16[128,5120]{1,0:T(8,128)(2,1)S(1)}, u32[]{:S(2)}, u32[]{:S(2)}) %collective-permute-start.8) | collective-permute-done | bytes 1310752 | tf_op jit(solution)/shard_map/ppermute | solution.py:31
  99.8 1.7 %collective-permute-start.9 = (bf16[128,5120]{1,0:T(8,128)(2,1)S(1)}, bf16[128,5120]{1,0:T(8,128)(2,1)S(1)}, u32[]{:S(2)}, u32[]{:S(2)}) collective-permute-start(bf16[128,5120]{1,0:T(8,128)(2,1)S(1)} %add_convert_fusion), channel_id=1, source_target_pairs={{0,1},{1,2},{2,3},{3,0},{4,5},{5,6},{6,7},{7,4},{8,11},{9,8},{10,9... | collective-permute-start | bytes 3932168 | tf_op jit(solution)/shard_map/ppermute | solution.py:31
  101.4 12.4 %collective-permute-done.11 = bf16[256,3072]{1,0:T(8,128)(2,1)S(1)} collective-permute-done((bf16[256,3072]{1,0:T(8,128)(2,1)S(1)}, bf16[256,3072]{1,0:T(8,128)(2,1)S(1)}, u32[]{:S(2)}, u32[]{:S(2)}) %collective-permute-start.11) | collective-permute-done | bytes 1572896 | tf_op jit(solution)/shard_map/ppermute | solution.py:31
  114.6 2.8 %collective-permute-start.12 = (bf16[64,3072]{1,0:T(8,128)(2,1)S(1)}, bf16[64,3072]{1,0:T(8,128)(2,1)S(1)}, u32[]{:S(2)}, u32[]{:S(2)}) collective-permute-start(bf16[64,3072]{1,0:T(8,128)(2,1)S(1)} %get-tuple-element.53), channel_id=1, source_target_pairs={{0,3},{1,0},{2,1},{3,2},{4,7},{5,4},{6,5},{7,6},{8,9},{9,10},{10,1... | collective-permute-start | bytes 1179656 | tf_op jit(solution)/shard_map/ppermute | solution.py:31
  117.4 8.7 %collective-permute-done.13 = bf16[64,3072]{1,0:T(8,128)(2,1)S(1)} collective-permute-done((bf16[64,3072]{1,0:T(8,128)(2,1)S(1)}, bf16[64,3072]{1,0:T(8,128)(2,1)S(1)}, u32[]{:S(2)}, u32[]{:S(2)}) %collective-permute-start.13) | collective-permute-done | bytes 393248 | tf_op jit(solution)/shard_map/ppermute | solution.py:31
  126.2 1.1 collective-permute-start.14
  127.6 5.3 %collective-permute-start.10 = (bf16[64,5120]{1,0:T(8,128)(2,1)S(1)}, bf16[64,5120]{1,0:T(8,128)(2,1)S(1)}, u32[]{:S(2)}, u32[]{:S(2)}) collective-permute-start(bf16[64,5120]{1,0:T(8,128)(2,1)S(1)} %add_convert_fusion.2), channel_id=1, source_target_pairs={{0,4},{1,5},{2,6},{3,7},{4,0},{5,1},{6,2},{7,3},{8,12},{9,13},{10,... | collective-permute-start | bytes 1966088 | tf_op jit(solution)/shard_map/ppermute | solution.py:31
  132.9 2.5 %collective-permute-done.14 = bf16[64,3072]{1,0:T(8,128)(2,1)S(1)} collective-permute-done((bf16[64,3072]{1,0:T(8,128)(2,1)S(1)}, bf16[64,3072]{1,0:T(8,128)(2,1)S(1)}, u32[]{:S(2)}, u32[]{:S(2)}) %collective-permute-start.14) | collective-permute-done | bytes 393248 | tf_op jit(solution)/shard_map/ppermute | solution.py:31
  135.6 11.9 %collective-permute-done.10 = bf16[64,5120]{1,0:T(8,128)(2,1)S(1)} collective-permute-done((bf16[64,5120]{1,0:T(8,128)(2,1)S(1)}, bf16[64,5120]{1,0:T(8,128)(2,1)S(1)}, u32[]{:S(2)}, u32[]{:S(2)}) %collective-permute-start.10) | collective-permute-done | bytes 655392 | tf_op jit(solution)/shard_map/ppermute | solution.py:31
  147.8 1.0 pad_maximum_fusion.1
  (51 shorter events, 9.2 us)
Async XLA Ops:
  0.0 14.4 %copy-start = (bf16[512,8,128]{2,1,0:T(8,128)(2,1)S(1)}, bf16[512,8,128]{2,1,0:T(8,128)(2,1)}, u32[]{:S(2)}) copy-start(bf16[512,8,128]{2,1,0:T(8,128)(2,1)} %param.7) | copy-start | bytes 3145732
  4.5 4.7 %collective-permute-start = (bf16[1040,128]{1,0:T(8,128)(2,1)S(1)}, bf16[1040,128]{1,0:T(8,128)(2,1)S(1)}, u32[]{:S(2)}, u32[]{:S(2)}) collective-permute-start(bf16[1040,128]{1,0:T(8,128)(2,1)S(1)} %pad_maximum_fusion.3.refs_1_), channel_id=1, source_target_pairs={{0,8},{1,9},{2,10},{3,11},{4,12},{5,13},{6,14},{7,15},{8,0},{9,1},... | collective-permute-start | bytes 798728 | tf_op jit(solution)/shard_map/ppermute | solution.py:31
  4.6 32.4 %collective-permute-start.2 = (bf16[1040,128]{1,0:T(8,128)(2,1)S(1)}, bf16[1040,128]{1,0:T(8,128)(2,1)S(1)}, u32[]{:S(2)}, u32[]{:S(2)}) collective-permute-start(bf16[1040,128]{1,0:T(8,128)(2,1)S(1)} %pad_maximum_fusion.3.refs_1_), channel_id=1, source_target_pairs={{0,80},{1,81},{2,82},{3,83},{4,84},{5,85},{6,86},{7,87},{8,88},{9,... | collective-permute-start | bytes 798728 | tf_op jit(solution)/shard_map/ppermute | solution.py:31
  10.2 18.6 %collective-permute-start.3 = (bf16[2080,128]{1,0:T(8,128)(2,1)S(1)}, bf16[2080,128]{1,0:T(8,128)(2,1)S(1)}, u32[]{:S(2)}, u32[]{:S(2)}) collective-permute-start(bf16[2080,128]{1,0:T(8,128)(2,1)S(1)} %pad_maximum_fusion.2), channel_id=1, source_target_pairs={{0,32},{1,33},{2,34},{3,35},{4,36},{5,37},{6,38},{7,39},{8,104},{9... | collective-permute-start | bytes 1597448 | tf_op jit(solution)/shard_map/ppermute | solution.py:31
  11.3 18.4 %collective-permute-start.4 = (bf16[2080,128]{1,0:T(8,128)(2,1)S(1)}, bf16[2080,128]{1,0:T(8,128)(2,1)S(1)}, u32[]{:S(2)}, u32[]{:S(2)}) collective-permute-start(bf16[2080,128]{1,0:T(8,128)(2,1)S(1)} %pad_maximum_fusion.2), channel_id=1, source_target_pairs={{0,16},{1,17},{2,18},{3,19},{4,20},{5,21},{6,22},{7,23},{8,72},{9,... | collective-permute-start | bytes 1597448 | tf_op jit(solution)/shard_map/ppermute | solution.py:31
  13.6 23.5 %collective-permute-start.1 = (bf16[2080,128]{1,0:T(8,128)(2,1)S(1)}, bf16[2080,128]{1,0:T(8,128)(2,1)S(1)}, u32[]{:S(2)}, u32[]{:S(2)}) collective-permute-start(bf16[2080,128]{1,0:T(8,128)(2,1)S(1)} %pad_maximum_fusion.2), channel_id=1, source_target_pairs={{0,48},{1,49},{2,50},{3,51},{4,52},{5,53},{6,54},{7,55},{8,120},{9... | collective-permute-start | bytes 1597448 | tf_op jit(solution)/shard_map/ppermute | solution.py:31
  29.8 7.7 %collective-permute-start.6 = (bf16[4160,128]{1,0:T(8,128)(2,1)S(1)}, bf16[4160,128]{1,0:T(8,128)(2,1)S(1)}, u32[]{:S(2)}, u32[]{:S(2)}) collective-permute-start(bf16[4160,128]{1,0:T(8,128)(2,1)S(1)} %pad_maximum_fusion), channel_id=1, source_target_pairs={{0,8},{1,9},{2,10},{3,11},{4,12},{5,13},{6,14},{7,15},{8,0},{9,1},... | collective-permute-start | bytes 3194888 | tf_op jit(solution)/shard_map/ppermute | solution.py:31
  37.1 11.0 %collective-permute-start.5 = (bf16[3120,128]{1,0:T(8,128)(2,1)S(1)}, bf16[3120,128]{1,0:T(8,128)(2,1)S(1)}, u32[]{:S(2)}, u32[]{:S(2)}) collective-permute-start(bf16[3120,128]{1,0:T(8,128)(2,1)S(1)} %constant_dynamic-update-slice_fusion.refs_3_), channel_id=1, source_target_pairs={{0,8},{1,9},{2,10},{3,11},{4,12},{5,13},{6,14},{7,15},{8,0},{9,1},... | collective-permute-start | bytes 2396168 | tf_op jit(solution)/shard_map/ppermute | solution.py:31
  37.4 26.7 %slice-start = ((s8[16777216]{0:T(1024)(128)(4,1)}), s8[4194304]{0:T(1024)(128)(4,1)S(1)}, s32[]{:S(2)}) async-start(s8[16777216]{0:T(1024)(128)(4,1)} %bitcast.8), calls=%async_computation | async-start | bytes 8388608
  37.4 26.7 %slice-start.1 = ((s8[16777216]{0:T(1024)(128)(4,1)}), s8[4194304]{0:T(1024)(128)(4,1)S(1)}, s32[]{:S(2)}) async-start(s8[16777216]{0:T(1024)(128)(4,1)} %bitcast.8), calls=%async_computation.1 | async-start | bytes 8388608
  44.1 1.3 copy-start.1
  45.5 1.3 copy-start.3
  46.8 1.4 copy-start.5
  48.2 1.6 %copy-start.2 = (f32[4096,128]{1,0:T(8,128)S(1)}, f32[4096,128]{1,0:T(8,128)}, u32[]{:S(2)}) copy-start(f32[4096,128]{1,0:T(8,128)} %copy-done.1) | copy-start | bytes 6291460
  49.8 1.6 %copy-start.4 = (f32[4096,128]{1,0:T(8,128)S(1)}, f32[4096,128]{1,0:T(8,128)}, u32[]{:S(2)}) copy-start(f32[4096,128]{1,0:T(8,128)} %copy-done.3) | copy-start | bytes 6291460
  51.3 1.6 %copy-start.6 = (f32[4096,128]{1,0:T(8,128)S(1)}, f32[4096,128]{1,0:T(8,128)}, u32[]{:S(2)}) copy-start(f32[4096,128]{1,0:T(8,128)} %copy-done.5) | copy-start | bytes 6291460
  52.9 11.2 %slice-start.2 = ((s8[16777216]{0:T(1024)(128)(4,1)}), s8[4194304]{0:T(1024)(128)(4,1)S(1)}, s32[]{:S(2)}) async-start(s8[16777216]{0:T(1024)(128)(4,1)} %bitcast.8), calls=%async_computation.2 | async-start | bytes 8388608
  52.9 11.2 %slice-start.3 = ((s8[16777216]{0:T(1024)(128)(4,1)}), s8[4194304]{0:T(1024)(128)(4,1)S(1)}, s32[]{:S(2)}) async-start(s8[16777216]{0:T(1024)(128)(4,1)} %bitcast.8), calls=%async_computation.3 | async-start | bytes 8388608
  68.6 30.9 %collective-permute-start.8 = (bf16[128,5120]{1,0:T(8,128)(2,1)S(1)}, bf16[128,5120]{1,0:T(8,128)(2,1)S(1)}, u32[]{:S(2)}, u32[]{:S(2)}) collective-permute-start(bf16[128,5120]{1,0:T(8,128)(2,1)S(1)} %get-tuple-element.52), channel_id=1, source_target_pairs={{0,1},{1,2},{2,3},{3,0},{4,5},{5,6},{6,7},{7,4},{8,11},{9,8},{10,9... | collective-permute-start | bytes 3932168 | tf_op jit(solution)/shard_map/ppermute | solution.py:31
  70.2 57.2 %collective-permute-start.7 = (bf16[128,5120]{1,0:T(8,128)(2,1)S(1)}, bf16[128,5120]{1,0:T(8,128)(2,1)S(1)}, u32[]{:S(2)}, u32[]{:S(2)}) collective-permute-start(bf16[128,5120]{1,0:T(8,128)(2,1)S(1)} %get-tuple-element.50), channel_id=1, source_target_pairs={{0,3},{1,0},{2,1},{3,2},{4,7},{5,4},{6,5},{7,6},{8,9},{9,10},{10,1... | collective-permute-start | bytes 3932168 | tf_op jit(solution)/shard_map/ppermute | solution.py:31
  74.6 39.3 %collective-permute-start.11 = (bf16[256,3072]{1,0:T(8,128)(2,1)S(1)}, bf16[256,3072]{1,0:T(8,128)(2,1)S(1)}, u32[]{:S(2)}, u32[]{:S(2)}) collective-permute-start(bf16[256,3072]{1,0:T(8,128)(2,1)S(1)} %project_b.1), channel_id=1, source_target_pairs={{0,4},{1,5},{2,6},{3,7},{4,0},{5,1},{6,2},{7,3},{8,12},{9,13},{10,... | collective-permute-start | bytes 4718600 | tf_op jit(solution)/shard_map/ppermute | solution.py:31
  99.8 27.6 %collective-permute-start.9 = (bf16[128,5120]{1,0:T(8,128)(2,1)S(1)}, bf16[128,5120]{1,0:T(8,128)(2,1)S(1)}, u32[]{:S(2)}, u32[]{:S(2)}) collective-permute-start(bf16[128,5120]{1,0:T(8,128)(2,1)S(1)} %add_convert_fusion), channel_id=1, source_target_pairs={{0,1},{1,2},{2,3},{3,0},{4,5},{5,6},{6,7},{7,4},{8,11},{9,8},{10,9... | collective-permute-start | bytes 3932168 | tf_op jit(solution)/shard_map/ppermute | solution.py:31
  114.0 12.0 %collective-permute-start.13 = (bf16[64,3072]{1,0:T(8,128)(2,1)S(1)}, bf16[64,3072]{1,0:T(8,128)(2,1)S(1)}, u32[]{:S(2)}, u32[]{:S(2)}) collective-permute-start(bf16[64,3072]{1,0:T(8,128)(2,1)S(1)} %get-tuple-element.54), channel_id=1, source_target_pairs={{0,1},{1,2},{2,3},{3,0},{4,5},{5,6},{6,7},{7,4},{8,11},{9,8},{10,9... | collective-permute-start | bytes 1179656 | tf_op jit(solution)/shard_map/ppermute | solution.py:31
  114.6 18.3 %collective-permute-start.12 = (bf16[64,3072]{1,0:T(8,128)(2,1)S(1)}, bf16[64,3072]{1,0:T(8,128)(2,1)S(1)}, u32[]{:S(2)}, u32[]{:S(2)}) collective-permute-start(bf16[64,3072]{1,0:T(8,128)(2,1)S(1)} %get-tuple-element.53), channel_id=1, source_target_pairs={{0,3},{1,0},{2,1},{3,2},{4,7},{5,4},{6,5},{7,6},{8,9},{9,10},{10,1... | collective-permute-start | bytes 1179656 | tf_op jit(solution)/shard_map/ppermute | solution.py:31
  126.2 9.2 %collective-permute-start.14 = (bf16[64,3072]{1,0:T(8,128)(2,1)S(1)}, bf16[64,3072]{1,0:T(8,128)(2,1)S(1)}, u32[]{:S(2)}, u32[]{:S(2)}) collective-permute-start(bf16[64,3072]{1,0:T(8,128)(2,1)S(1)} %add_convert_fusion.4), channel_id=1, source_target_pairs={{0,1},{1,2},{2,3},{3,0},{4,5},{5,6},{6,7},{7,4},{8,11},{9,8},{10,9... | collective-permute-start | bytes 1179656 | tf_op jit(solution)/shard_map/ppermute | solution.py:31
  127.6 19.9 %collective-permute-start.10 = (bf16[64,5120]{1,0:T(8,128)(2,1)S(1)}, bf16[64,5120]{1,0:T(8,128)(2,1)S(1)}, u32[]{:S(2)}, u32[]{:S(2)}) collective-permute-start(bf16[64,5120]{1,0:T(8,128)(2,1)S(1)} %add_convert_fusion.2), channel_id=1, source_target_pairs={{0,4},{1,5},{2,6},{3,7},{4,0},{5,1},{6,2},{7,3},{8,12},{9,13},{10,... | collective-permute-start | bytes 1966088 | tf_op jit(solution)/shard_map/ppermute | solution.py:31

commit v3 on v2

--- a/solution.py
+++ b/solution.py
@@ -18,6 +18,8 @@
 NN = (((1,), (0,)), ((), ()))
 META = 16
 PAYLOAD = 1024 + META
+TILE = 512
+LIMIT = 20 << 20
 
 
 def index_of(z, yh, c, yl, x):
@@ -199,6 +201,32 @@
         return carry
 
     lax.fori_loop(0, count, step, 0)
+
+
+def pack_kernel(k_ref, v_ref, ks_ref, vs_ref, place_ref, o_ref):
+    o_ref[0:512, :] = k_ref[...]
+    for half in range(2):
+        rows = slice(half * 256, half * 256 + 256)
+        o_ref[512 + half * 256 : 768 + half * 256, :] = (
+            v_ref[rows, :].astype(F32) * vs_ref[half, 0].astype(F32)
+        ).astype(BF16)
+    row = lax.broadcasted_iota(jnp.int32, (META, 128), 0)
+    low, high = ks_ref[0, 0].astype(F32), ks_ref[1, 0].astype(F32)
+    place = place_ref[0].astype(F32)
+    meta = jnp.where(row == 0, low, jnp.where(row == 1, high, jnp.where(row == 2, place, 0.0)))
+    o_ref[1024:PAYLOAD, :] = meta.astype(BF16)
+
+
+def packed(keys, values, k_scale, v_scale, block_place):
+    vmem = pl.BlockSpec(memory_space=pltpu.VMEM)
+    smem = pl.BlockSpec(memory_space=pltpu.SMEM)
+    return pl.pallas_call(
+        pack_kernel,
+        out_shape=jax.ShapeDtypeStruct((PAYLOAD, 128), BF16),
+        in_specs=[vmem, vmem, smem, smem, smem],
+        out_specs=vmem,
+        name="pack",
+    )(keys, values, k_scale.astype(F32), v_scale.astype(F32), block_place)
 
 
 def group_kernel(inv, sizes, start, finish, *refs):
@@ -257,7 +285,7 @@
             pltpu.VMEM((2 * count, 128), F32),
         ],
         input_output_aliases=aliases,
-        compiler_params=pltpu.CompilerParams(vmem_limit_bytes=32 << 20),
+        compiler_params=pltpu.CompilerParams(vmem_limit_bytes=LIMIT),
         cost_estimate=pl.CostEstimate(
             flops=tiles * 2048 * 256 * 128 * 16,
             transcendentals=tiles * 2048 * 256,
@@ -267,28 +295,26 @@
     )(*operands)
 
 
-def project_kernel(blocks, splits, a_ref, w_ref, *o_refs):
+def project_kernel(blocks, splits, first, columns, a_ref, w_ref, *o_refs):
     rows = jnp.concatenate([a_ref[b * 64 : (b + 1) * 64, :] for b in blocks], axis=0)
-    product = jnp.dot(rows, w_ref[...], preferred_element_type=F32).astype(BF16)
-    at = 0
-    for size, o_ref in zip(splits, o_refs):
-        o_ref[...] = product[at * 64 : (at + size) * 64, :]
-        at += size
+    for c in range(0, columns, TILE):
+        product = jnp.dot(
+            rows, w_ref[:, first + c : first + c + TILE], preferred_element_type=F32
+        ).astype(BF16)
+        at = 0
+        for size, o_ref in zip(splits, o_refs):
+            o_ref[:, c : c + TILE] = product[at * 64 : (at + size) * 64, :]
+            at += size
 
 
 def project(att, weight, blocks, splits, first, columns, name):
-    tile = 1024
-    start = first // tile
+    vmem = pl.BlockSpec(memory_space=pltpu.VMEM)
     return pl.pallas_call(
-        functools.partial(project_kernel, blocks, splits),
+        functools.partial(project_kernel, blocks, splits, first, columns),
         out_shape=[jax.ShapeDtypeStruct((s * 64, columns), BF16) for s in splits],
-        grid=(columns // tile,),
-        in_specs=[
-            pl.BlockSpec((512, 1024), lambda j: (0, 0)),
-            pl.BlockSpec((1024, tile), lambda j: (0, j + start)),
-        ],
-        out_specs=[pl.BlockSpec((s * 64, tile), lambda j: (0, j)) for s in splits],
-        compiler_params=pltpu.CompilerParams(vmem_limit_bytes=24 << 20),
+        in_specs=[vmem] * 2,
+        out_specs=[vmem] * len(splits),
+        compiler_params=pltpu.CompilerParams(vmem_limit_bytes=LIMIT),
         cost_estimate=pl.CostEstimate(
             flops=2 * len(blocks) * 64 * 1024 * columns,
             transcendentals=0,
@@ -307,22 +333,26 @@
 
 def scattered(att, weight, first_columns):
     rest = weight.shape[1] - first_columns
-    x_far, x_behind = project(att, weight, (0, 1, 4, 5), (2, 2), 0, first_columns, "project_a")
+    (x_far,) = project(att, weight, (0, 1), (2,), 0, first_columns, "project_far")
     got_far = moved(x_far, ahead)
+    (y_out,) = project(att, weight, (1, 3, 5, 7), (4,), first_columns, rest, "project_y")
+    got_y = moved(y_out, beside)
+    (x_behind,) = project(att, weight, (4, 5), (2,), 0, first_columns, "project_behind")
     got_front = moved(x_behind, behind)
-    (y_out,) = project(att, weight, (1, 3, 5, 7), (4,), first_columns, rest, "project_b")
-    got_y = moved(y_out, beside)
     x_ahead, x_own = project(att, weight, (2, 3, 6, 7), (2, 2), 0, first_columns, "project_c")
     (y_own,) = project(att, weight, (0, 2, 4, 6), (4,), first_columns, rest, "project_d")
     got_back = moved(added(x_ahead, got_far).astype(BF16), ahead)
     y_far, y_ahead, y_behind, y_mine = [
         (y_own[i * 64 : (i + 1) * 64], got_y[i * 64 : (i + 1) * 64]) for i in range(4)
     ]
-    y_got_far = moved(added(*y_far).astype(BF16), ahead)
-    y_got_front = moved(added(*y_behind).astype(BF16), behind)
-    y_got_back = moved(added(*y_ahead, y_got_far).astype(BF16), ahead)
     x_out = added(x_own[64:], got_front[64:], got_back[64:]).astype(BF16)
     x_last = moved(x_out, beside)
+    y_far_sum, y_behind_sum, x_out = lax.optimization_barrier(
+        (added(*y_far).astype(BF16), added(*y_behind).astype(BF16), x_out)
+    )
+    y_got_far = moved(y_far_sum, ahead)
+    y_got_front = moved(y_behind_sum, behind)
+    y_got_back = moved(added(*y_ahead, y_got_far).astype(BF16), ahead)
     return jnp.concatenate(
         [
             added(x_own[:64], got_front[:64], got_back[:64], x_last).astype(BF16),
@@ -336,17 +366,14 @@
     inv = math.log2(math.e) / math.sqrt(128)
     q = query.reshape(4096, 128)
     k = keys.reshape(512, 128)
-    gain = jnp.repeat(v_scale.reshape(2).astype(F32), 256)[:, None]
-    v = (values.reshape(512, 128).astype(F32) * gain).astype(BF16)
-    meta = jnp.concatenate(
-        [k_scale.reshape(2), block_place.astype(BF16), jnp.zeros((META - 4,), BF16)]
-    )
-    own = jnp.concatenate([k, v, jnp.broadcast_to(meta[:, None], (META, 128))], axis=0)
+    own = packed(k, values.reshape(512, 128), k_scale, v_scale, block_place)
     partner = moved(own, swapped)
     pair = jnp.concatenate([own, partner], axis=0)
-    one, two, three = moved(pair, near), moved(pair, across), moved(pair, diagonal)
-    four = moved(own, opposite)
+    one, two = moved(pair, near), moved(pair, across)
     state = attend(q, own, [partner], None, None, inv, "attend_own")
+    pair, four_in, *state = lax.optimization_barrier((pair, own, *state))
+    three = moved(pair, diagonal)
+    four = moved(four_in, opposite)
     one, two, *state = lax.optimization_barrier((one, two, *state))
     more = moved(jnp.concatenate([one, two], axis=0), swapped)
     state = attend(q, own, [one, two], state, None, inv, "attend_near")

time: 152 us -> 133 us (0.88); the launches traced: 149 us -> 133 us
  local copies, waits for them, and re-layouts: 9.05 us -> 0.1 us
  starting transfers between devices: 29.5 us -> 25.9 us
  waiting for transfers between devices: 59.7 us -> 57 us
  other arithmetic: 7.79 us -> 6.02 us
    unnamed x25 -> x11, local copies, waits for them, and re-layouts: 8.93 us -> 0.06 us
    pallas_call x4, Pallas kernels: 28.4 us -> 32.4 us  [attend(): pl.pallas_call(functools.partial(group_kernel, inv, sizes, start, finish)...]
    ppermute x15, starting transfers between devices: 29.5 us -> 25.9 us  [moved(): return lax.ppermute(array, AXES, pairs)]
    pallas_call x4 -> x6, Pallas kernels: 14.2 us -> 11.2 us  [the longest x5 9.52 us: project(): pl.pallas_call(functools.partial(project_kernel, blocks, splits, first, c...]
    ppermute x15, waiting for transfers between devices: 59.7 us -> 57 us  [moved(): return lax.ppermute(array, AXES, pairs)]
  transfers between devices with their start and end apart: 15 -> 15, of which waited for: 7 -> 9; matrix products, arithmetic and copies ran while one was open for 1% -> 1% of each run, Pallas kernels for 18% -> 21%
where the time goes in v3:
time: 133 us
  waiting for transfers between devices  57 us (43%)
  Pallas kernels  43.7 us (33%)
  starting transfers between devices  25.9 us (19%)
  other arithmetic  6.02 us (5%)
    ppermute x15, waiting for transfers between devices, moved(): return lax.ppermute(array, AXES, pairs)  57 us
    pallas_call x4, Pallas kernels, attend(): pl.pallas_call(functools.partial(group_kernel, inv, sizes, start, finish)...  32.4 us
    ppermute x15, starting transfers between devices, moved(): return lax.ppermute(array, AXES, pairs)  25.9 us
    pallas_call x5, Pallas kernels, project(): pl.pallas_call(functools.partial(project_kernel, blocks, splits, first, c...  9.52 us
  transfers between devices with their start and end apart: 15, of which 9 were waited for; matrix products, arithmetic and copies ran while one was open for 1% of the time, Pallas kernels for 21%

profile of v3, /device:TPU:24, one launch (start us, length us, event | category | flops | bytes accessed | tf_op | source)
XLA Modules:
  0.0 132.9 jit_solution(10464598338001536073)
XLA Ops:
  0.0 1.3 convert_element_type.87.ks_ref
  1.3 1.2 convert_element_type.88.vs_ref
  2.5 1.7 %pack.1.refs_1_ = bf16[1040,128]{1,0:T(8,128)(2,1)} custom-call(bf16[512,128]{1,0:T(8,128)(2,1)} %bitcast.9, bf16[512,128]{1,0:T(8,128)(2,1)} %bitcast.10, f32[2,1]{1,0:T(2,128)} %convert_element_type.87.ks_ref, f32[2,1]{1,0:T(2,128)} %convert_element_type.88.vs_ref, s32[2]{0:T(128)} %place_ref.1), custom_call_target="tpu_custom_call" | custom-call | tf_op jit(solution)/shard_map/pack/pallas_call | solution.py:223
  4.2 1.7 %collective-permute-done.refs_2_ = bf16[1040,128]{1,0:T(8,128)(2,1)S(1)} collective-permute-done((bf16[1040,128]{1,0:T(8,128)(2,1)}, bf16[1040,128]{1,0:T(8,128)(2,1)S(1)}, u32[]{:S(2)}, u32[]{:S(2)}) %collective-permute-start) | collective-permute-done | bytes 266272 | tf_op jit(solution)/shard_map/ppermute | solution.py:33
  6.0 1.0 pad_maximum_fusion.2
  7.0 2.0 %collective-permute-start.3 = (bf16[2080,128]{1,0:T(8,128)(2,1)S(1)}, bf16[2080,128]{1,0:T(8,128)(2,1)S(1)}, u32[]{:S(2)}, u32[]{:S(2)}) collective-permute-start(bf16[2080,128]{1,0:T(8,128)(2,1)S(1)} %pad_maximum_fusion.2), channel_id=1, source_target_pairs={{0,32},{1,33},{2,34},{3,35},{4,36},{5,37},{6,38},{7,39},{8,104},{9... | collective-permute-start | bytes 1597448 | tf_op jit(solution)/shard_map/ppermute | solution.py:33
  9.0 1.2 collective-permute-start.4
  10.2 4.9 %attend_own.1 = (f32[4096,128]{1,0:T(8,128)S(1)}, f32[4096,128]{1,0:T(8,128)S(1)}, f32[4096,128]{1,0:T(8,128)S(1)}) custom-call(bf16[4096,128]{1,0:T(8,128)(2,1)S(1)} %bitcast.5, bf16[1040,128]{1,0:T(8,128)(2,1)} %pack.1.refs_1_, bf16[1040,128]{1,0:T(8,128)(2,1)S(1)} %collective-permute-done.refs_2_), custom_call_target="tpu_custom_call" | custom-call | flops 5368709120 | bytes 1048576 | tf_op jit(solution)/shard_map/attend_own/pallas_call | solution.py:277
  15.2 3.6 %collective-permute-start.1 = (bf16[2080,128]{1,0:T(8,128)(2,1)S(1)}, bf16[2080,128]{1,0:T(8,128)(2,1)S(1)}, u32[]{:S(2)}, u32[]{:S(2)}) collective-permute-start(bf16[2080,128]{1,0:T(8,128)(2,1)S(1)} %pad_maximum_fusion.2), channel_id=1, source_target_pairs={{0,48},{1,49},{2,50},{3,51},{4,52},{5,53},{6,54},{7,55},{8,120},{9... | collective-permute-start | bytes 1597448 | tf_op jit(solution)/shard_map/ppermute | solution.py:33
  18.8 2.4 %collective-permute-start.2 = (bf16[1040,128]{1,0:T(8,128)(2,1)}, bf16[1040,128]{1,0:T(8,128)(2,1)S(1)}, u32[]{:S(2)}, u32[]{:S(2)}) collective-permute-start(bf16[1040,128]{1,0:T(8,128)(2,1)} %pack.1.refs_1_), channel_id=1, source_target_pairs={{0,80},{1,81},{2,82},{3,83},{4,84},{5,85},{6,86},{7,87},{8,88},{9,... | collective-permute-start | bytes 798728 | tf_op jit(solution)/shard_map/ppermute | solution.py:33
  21.7 6.2 %collective-permute-start.6 = (bf16[4160,128]{1,0:T(8,128)(2,1)S(1)}, bf16[4160,128]{1,0:T(8,128)(2,1)S(1)}, u32[]{:S(2)}, u32[]{:S(2)}) collective-permute-start(bf16[4160,128]{1,0:T(8,128)(2,1)S(1)} %pad_maximum_fusion), channel_id=1, source_target_pairs={{0,8},{1,9},{2,10},{3,11},{4,12},{5,13},{6,14},{7,15},{8,0},{9,1},... | collective-permute-start | bytes 3194888 | tf_op jit(solution)/shard_map/ppermute | solution.py:33
  27.9 7.7 %attend_near.1 = (f32[4096,128]{1,0:T(8,128)S(1)}, f32[4096,128]{1,0:T(8,128)S(1)}, f32[4096,128]{1,0:T(8,128)S(1)}) custom-call(bf16[4096,128]{1,0:T(8,128)(2,1)S(1)} %bitcast.6, bf16[1040,128]{1,0:T(8,128)(2,1)} %pack.1.refs_1_, bf16[2080,128]{1,0:T(8,128)(2,1)S(1)} %collective-permute-done.3.refs_2_, ...), custom_call_target="tpu_custom_call", output_to_operand_aliasing={{0}: (4, {}), {1}: (5, {}), {2}: (6, {})} | custom-call | flops 8589934592 | bytes 1048576 | tf_op jit(solution)/shard_map/attend_near/pallas_call | solution.py:277
  35.7 4.2 %collective-permute-done.2 = bf16[1040,128]{1,0:T(8,128)(2,1)S(1)} collective-permute-done((bf16[1040,128]{1,0:T(8,128)(2,1)}, bf16[1040,128]{1,0:T(8,128)(2,1)S(1)}, u32[]{:S(2)}, u32[]{:S(2)}) %collective-permute-start.2) | collective-permute-done | bytes 266272 | tf_op jit(solution)/shard_map/ppermute | solution.py:33
  40.3 7.9 %attend_more.1 = (f32[4096,128]{1,0:T(8,128)S(1)}, f32[4096,128]{1,0:T(8,128)S(1)}, f32[4096,128]{1,0:T(8,128)S(1)}) custom-call(bf16[4096,128]{1,0:T(8,128)(2,1)S(1)} %bitcast.7, bf16[1040,128]{1,0:T(8,128)(2,1)} %pack.1.refs_1_, bf16[4160,128]{1,0:T(8,128)(2,1)S(1)} %collective-permute-done.6.refs_2_, ...), custom_call_target="tpu_custom_call", output_to_operand_aliasing={{0}: (3, {}), {1}: (4, {}), {2}: (5, {})} | custom-call | flops 8589934592 | bytes 1048576 | tf_op jit(solution)/shard_map/attend_more/pallas_call | solution.py:277
  48.2 11.9 %attend_rest.1 = (bf16[512,1024]{1,0:T(8,128)(2,1)S(1)}, f32[4096,128]{1,0:T(8,128)S(1)}, f32[4096,128]{1,0:T(8,128)S(1)}, f32[4096,128]{1,0:T(8,128)S(1)}) custom-call(bf16[4096,128]{1,0:T(8,128)(2,1)S(1)} %bitcast.8, bf16[1040,128]{1,0:T(8,128)(2,1)} %pack.1.refs_1_, ...), custom_call_target="tpu_custom_call", output_to_operand_aliasing={{1}: (5, {}), {2}: (6, {}), {3}: (7, {})} | custom-call | flops 12884901888 | bytes 1048576 | tf_op jit(solution)/shard_map/attend_rest/pallas_call | solution.py:277
  60.1 1.5 %project_far.1 = bf16[128,5120]{1,0:T(8,128)(2,1)S(1)} custom-call(bf16[512,1024]{1,0:T(8,128)(2,1)S(1)} %get-tuple-element.58.a_ref, bf16[1024,8192]{1,0:T(8,128)(2,1)S(1)} %bitcast.4), custom_call_target="tpu_custom_call" | custom-call | flops 1342177280 | bytes 10485760 | tf_op jit(solution)/shard_map/project_far/pallas_call | solution.py:312
  61.7 1.6 %collective-permute-start.8 = (bf16[128,5120]{1,0:T(8,128)(2,1)S(1)}, bf16[128,5120]{1,0:T(8,128)(2,1)S(1)}, u32[]{:S(2)}, u32[]{:S(2)}) collective-permute-start(bf16[128,5120]{1,0:T(8,128)(2,1)S(1)} %project_far.1), channel_id=1, source_target_pairs={{0,1},{1,2},{2,3},{3,0},{4,5},{5,6},{6,7},{7,4},{8,11},{9,8},{10,9... | collective-permute-start | bytes 3932168 | tf_op jit(solution)/shard_map/ppermute | solution.py:33
  63.2 1.5 %project_behind.1 = bf16[128,5120]{1,0:T(8,128)(2,1)S(1)} custom-call(bf16[512,1024]{1,0:T(8,128)(2,1)S(1)} %get-tuple-element.58.a_ref, bf16[1024,8192]{1,0:T(8,128)(2,1)S(1)} %bitcast.4), custom_call_target="tpu_custom_call" | custom-call | flops 1342177280 | bytes 10485760 | tf_op jit(solution)/shard_map/project_behind/pallas_call | solution.py:312
  64.8 2.0 %collective-permute-start.7 = (bf16[128,5120]{1,0:T(8,128)(2,1)S(1)}, bf16[128,5120]{1,0:T(8,128)(2,1)S(1)}, u32[]{:S(2)}, u32[]{:S(2)}) collective-permute-start(bf16[128,5120]{1,0:T(8,128)(2,1)S(1)} %project_behind.1), channel_id=1, source_target_pairs={{0,3},{1,0},{2,1},{3,2},{4,7},{5,4},{6,5},{7,6},{8,9},{9,10},{10,1... | collective-permute-start | bytes 3932168 | tf_op jit(solution)/shard_map/ppermute | solution.py:33
  66.8 1.8 %project_y.1 = bf16[256,3072]{1,0:T(8,128)(2,1)S(1)} custom-call(bf16[512,1024]{1,0:T(8,128)(2,1)S(1)} %get-tuple-element.58.a_ref, bf16[1024,8192]{1,0:T(8,128)(2,1)S(1)} %bitcast.4), custom_call_target="tpu_custom_call" | custom-call | flops 1610612736 | bytes 6291456 | tf_op jit(solution)/shard_map/project_y/pallas_call | solution.py:312
  68.6 0.8 collective-permute-start.11
  69.4 2.9 %project_c.1 = (bf16[128,5120]{1,0:T(8,128)(2,1)S(1)}, bf16[128,5120]{1,0:T(8,128)(2,1)S(1)}) custom-call(bf16[512,1024]{1,0:T(8,128)(2,1)S(1)} %get-tuple-element.58.a_ref, bf16[1024,8192]{1,0:T(8,128)(2,1)S(1)} %bitcast.4), custom_call_target="tpu_custom_call" | custom-call | flops 2684354560 | bytes 10485760 | tf_op jit(solution)/shard_map/project_c/pallas_call | solution.py:312
  72.3 18.4 %collective-permute-done.8 = bf16[128,5120]{1,0:T(8,128)(2,1)S(1)} collective-permute-done((bf16[128,5120]{1,0:T(8,128)(2,1)S(1)}, bf16[128,5120]{1,0:T(8,128)(2,1)S(1)}, u32[]{:S(2)}, u32[]{:S(2)}) %collective-permute-start.8) | collective-permute-done | bytes 1310752 | tf_op jit(solution)/shard_map/ppermute | solution.py:33
  91.1 1.6 %collective-permute-start.9 = (bf16[128,5120]{1,0:T(8,128)(2,1)S(1)}, bf16[128,5120]{1,0:T(8,128)(2,1)S(1)}, u32[]{:S(2)}, u32[]{:S(2)}) collective-permute-start(bf16[128,5120]{1,0:T(8,128)(2,1)S(1)} %add_convert_fusion), channel_id=1, source_target_pairs={{0,1},{1,2},{2,3},{3,0},{4,5},{5,6},{6,7},{7,4},{8,11},{9,8},{10,9... | collective-permute-start | bytes 3932168 | tf_op jit(solution)/shard_map/ppermute | solution.py:33
  92.6 1.8 %project_d.1 = bf16[256,3072]{1,0:T(8,128)(2,1)S(1)} custom-call(bf16[512,1024]{1,0:T(8,128)(2,1)S(1)} %get-tuple-element.58.a_ref, bf16[1024,8192]{1,0:T(8,128)(2,1)S(1)} %bitcast.4), custom_call_target="tpu_custom_call" | custom-call | flops 1610612736 | bytes 6291456 | tf_op jit(solution)/shard_map/project_d/pallas_call | solution.py:312
  94.4 10.3 %collective-permute-done.11 = bf16[256,3072]{1,0:T(8,128)(2,1)S(1)} collective-permute-done((bf16[256,3072]{1,0:T(8,128)(2,1)S(1)}, bf16[256,3072]{1,0:T(8,128)(2,1)S(1)}, u32[]{:S(2)}, u32[]{:S(2)}) %collective-permute-start.11) | collective-permute-done | bytes 1572896 | tf_op jit(solution)/shard_map/ppermute | solution.py:33
  104.9 5.3 %collective-permute-done.9 = bf16[128,5120]{1,0:T(8,128)(2,1)S(1)} collective-permute-done((bf16[128,5120]{1,0:T(8,128)(2,1)S(1)}, bf16[128,5120]{1,0:T(8,128)(2,1)S(1)}, u32[]{:S(2)}, u32[]{:S(2)}) %collective-permute-start.9) | collective-permute-done | bytes 1310752 | tf_op jit(solution)/shard_map/ppermute | solution.py:33
  111.3 3.1 %collective-permute-start.12 = (bf16[64,3072]{1,0:T(8,128)(2,1)S(1)}, bf16[64,3072]{1,0:T(8,128)(2,1)S(1)}, u32[]{:S(2)}, u32[]{:S(2)}) collective-permute-start(bf16[64,3072]{1,0:T(8,128)(2,1)S(1)} %get-tuple-element.61), channel_id=1, source_target_pairs={{0,3},{1,0},{2,1},{3,2},{4,7},{5,4},{6,5},{7,6},{8,9},{9,10},{10,1... | collective-permute-start | bytes 1179656 | tf_op jit(solution)/shard_map/ppermute | solution.py:33
  114.5 8.0 %collective-permute-done.13 = bf16[64,3072]{1,0:T(8,128)(2,1)S(1)} collective-permute-done((bf16[64,3072]{1,0:T(8,128)(2,1)S(1)}, bf16[64,3072]{1,0:T(8,128)(2,1)S(1)}, u32[]{:S(2)}, u32[]{:S(2)}) %collective-permute-start.13) | collective-permute-done | bytes 393248 | tf_op jit(solution)/shard_map/ppermute | solution.py:33
  122.7 4.9 %collective-permute-done.10 = bf16[64,5120]{1,0:T(8,128)(2,1)S(1)} collective-permute-done((bf16[64,5120]{1,0:T(8,128)(2,1)S(1)}, bf16[64,5120]{1,0:T(8,128)(2,1)S(1)}, u32[]{:S(2)}, u32[]{:S(2)}) %collective-permute-start.10) | collective-permute-done | bytes 655392 | tf_op jit(solution)/shard_map/ppermute | solution.py:33
  128.0 3.7 %collective-permute-done.14 = bf16[64,3072]{1,0:T(8,128)(2,1)S(1)} collective-permute-done((bf16[64,3072]{1,0:T(8,128)(2,1)S(1)}, bf16[64,3072]{1,0:T(8,128)(2,1)S(1)}, u32[]{:S(2)}, u32[]{:S(2)}) %collective-permute-start.14) | collective-permute-done | bytes 393248 | tf_op jit(solution)/shard_map/ppermute | solution.py:33
  131.9 1.0 pad_maximum_fusion.1
  (33 shorter events, 3.3 us)
Async XLA Ops:
  0.0 10.2 %copy-start = (bf16[512,8,128]{2,1,0:T(8,128)(2,1)S(1)}, bf16[512,8,128]{2,1,0:T(8,128)(2,1)}, u32[]{:S(2)}) copy-start(bf16[512,8,128]{2,1,0:T(8,128)(2,1)} %param.7) | copy-start | bytes 3145732
  4.2 1.8 %collective-permute-start = (bf16[1040,128]{1,0:T(8,128)(2,1)}, bf16[1040,128]{1,0:T(8,128)(2,1)S(1)}, u32[]{:S(2)}, u32[]{:S(2)}) collective-permute-start(bf16[1040,128]{1,0:T(8,128)(2,1)} %pack.1.refs_1_), channel_id=1, source_target_pairs={{0,8},{1,9},{2,10},{3,11},{4,12},{5,13},{6,14},{7,15},{8,0},{9,1},... | collective-permute-start | bytes 798728 | tf_op jit(solution)/shard_map/ppermute | solution.py:33
  7.0 14.7 %collective-permute-start.3 = (bf16[2080,128]{1,0:T(8,128)(2,1)S(1)}, bf16[2080,128]{1,0:T(8,128)(2,1)S(1)}, u32[]{:S(2)}, u32[]{:S(2)}) collective-permute-start(bf16[2080,128]{1,0:T(8,128)(2,1)S(1)} %pad_maximum_fusion.2), channel_id=1, source_target_pairs={{0,32},{1,33},{2,34},{3,35},{4,36},{5,37},{6,38},{7,39},{8,104},{9... | collective-permute-start | bytes 1597448 | tf_op jit(solution)/shard_map/ppermute | solution.py:33
  9.0 12.7 %collective-permute-start.4 = (bf16[2080,128]{1,0:T(8,128)(2,1)S(1)}, bf16[2080,128]{1,0:T(8,128)(2,1)S(1)}, u32[]{:S(2)}, u32[]{:S(2)}) collective-permute-start(bf16[2080,128]{1,0:T(8,128)(2,1)S(1)} %pad_maximum_fusion.2), channel_id=1, source_target_pairs={{0,16},{1,17},{2,18},{3,19},{4,20},{5,21},{6,22},{7,23},{8,72},{9,... | collective-permute-start | bytes 1597448 | tf_op jit(solution)/shard_map/ppermute | solution.py:33
  15.2 24.7 %collective-permute-start.1 = (bf16[2080,128]{1,0:T(8,128)(2,1)S(1)}, bf16[2080,128]{1,0:T(8,128)(2,1)S(1)}, u32[]{:S(2)}, u32[]{:S(2)}) collective-permute-start(bf16[2080,128]{1,0:T(8,128)(2,1)S(1)} %pad_maximum_fusion.2), channel_id=1, source_target_pairs={{0,48},{1,49},{2,50},{3,51},{4,52},{5,53},{6,54},{7,55},{8,120},{9... | collective-permute-start | bytes 1597448 | tf_op jit(solution)/shard_map/ppermute | solution.py:33
  18.8 21.1 %collective-permute-start.2 = (bf16[1040,128]{1,0:T(8,128)(2,1)}, bf16[1040,128]{1,0:T(8,128)(2,1)S(1)}, u32[]{:S(2)}, u32[]{:S(2)}) collective-permute-start(bf16[1040,128]{1,0:T(8,128)(2,1)} %pack.1.refs_1_), channel_id=1, source_target_pairs={{0,80},{1,81},{2,82},{3,83},{4,84},{5,85},{6,86},{7,87},{8,88},{9,... | collective-permute-start | bytes 798728 | tf_op jit(solution)/shard_map/ppermute | solution.py:33
  21.7 18.5 %collective-permute-start.6 = (bf16[4160,128]{1,0:T(8,128)(2,1)S(1)}, bf16[4160,128]{1,0:T(8,128)(2,1)S(1)}, u32[]{:S(2)}, u32[]{:S(2)}) collective-permute-start(bf16[4160,128]{1,0:T(8,128)(2,1)S(1)} %pad_maximum_fusion), channel_id=1, source_target_pairs={{0,8},{1,9},{2,10},{3,11},{4,12},{5,13},{6,14},{7,15},{8,0},{9,1},... | collective-permute-start | bytes 3194888 | tf_op jit(solution)/shard_map/ppermute | solution.py:33
  40.0 8.2 %collective-permute-start.5 = (bf16[3120,128]{1,0:T(8,128)(2,1)S(1)}, bf16[3120,128]{1,0:T(8,128)(2,1)S(1)}, u32[]{:S(2)}, u32[]{:S(2)}) collective-permute-start(bf16[3120,128]{1,0:T(8,128)(2,1)S(1)} %constant_dynamic-update-slice_fusion.refs_3_), channel_id=1, source_target_pairs={{0,8},{1,9},{2,10},{3,11},{4,12},{5,13},{6,14},{7,15},{8,0},{9,1},... | collective-permute-start | bytes 2396168 | tf_op jit(solution)/shard_map/ppermute | solution.py:33
  40.2 19.8 %slice-start = ((s8[16777216]{0:T(1024)(128)(4,1)}), s8[4194304]{0:T(1024)(128)(4,1)S(1)}, s32[]{:S(2)}) async-start(s8[16777216]{0:T(1024)(128)(4,1)} %bitcast.3), calls=%async_computation | async-start | bytes 8388608
  40.3 19.8 %slice-start.1 = ((s8[16777216]{0:T(1024)(128)(4,1)}), s8[4194304]{0:T(1024)(128)(4,1)S(1)}, s32[]{:S(2)}) async-start(s8[16777216]{0:T(1024)(128)(4,1)} %bitcast.3), calls=%async_computation.1 | async-start | bytes 8388608
  48.2 12.0 %slice-start.2 = ((s8[16777216]{0:T(1024)(128)(4,1)}), s8[4194304]{0:T(1024)(128)(4,1)S(1)}, s32[]{:S(2)}) async-start(s8[16777216]{0:T(1024)(128)(4,1)} %bitcast.3), calls=%async_computation.2 | async-start | bytes 8388608
  48.2 12.0 %slice-start.3 = ((s8[16777216]{0:T(1024)(128)(4,1)}), s8[4194304]{0:T(1024)(128)(4,1)S(1)}, s32[]{:S(2)}) async-start(s8[16777216]{0:T(1024)(128)(4,1)} %bitcast.3), calls=%async_computation.3 | async-start | bytes 8388608
  61.7 29.1 %collective-permute-start.8 = (bf16[128,5120]{1,0:T(8,128)(2,1)S(1)}, bf16[128,5120]{1,0:T(8,128)(2,1)S(1)}, u32[]{:S(2)}, u32[]{:S(2)}) collective-permute-start(bf16[128,5120]{1,0:T(8,128)(2,1)S(1)} %project_far.1), channel_id=1, source_target_pairs={{0,1},{1,2},{2,3},{3,0},{4,5},{5,6},{6,7},{7,4},{8,11},{9,8},{10,9... | collective-permute-start | bytes 3932168 | tf_op jit(solution)/shard_map/ppermute | solution.py:33
  64.8 40.1 %collective-permute-start.7 = (bf16[128,5120]{1,0:T(8,128)(2,1)S(1)}, bf16[128,5120]{1,0:T(8,128)(2,1)S(1)}, u32[]{:S(2)}, u32[]{:S(2)}) collective-permute-start(bf16[128,5120]{1,0:T(8,128)(2,1)S(1)} %project_behind.1), channel_id=1, source_target_pairs={{0,3},{1,0},{2,1},{3,2},{4,7},{5,4},{6,5},{7,6},{8,9},{9,10},{10,1... | collective-permute-start | bytes 3932168 | tf_op jit(solution)/shard_map/ppermute | solution.py:33
  68.6 36.1 %collective-permute-start.11 = (bf16[256,3072]{1,0:T(8,128)(2,1)S(1)}, bf16[256,3072]{1,0:T(8,128)(2,1)S(1)}, u32[]{:S(2)}, u32[]{:S(2)}) collective-permute-start(bf16[256,3072]{1,0:T(8,128)(2,1)S(1)} %project_y.1), channel_id=1, source_target_pairs={{0,4},{1,5},{2,6},{3,7},{4,0},{5,1},{6,2},{7,3},{8,12},{9,13},{10,... | collective-permute-start | bytes 4718600 | tf_op jit(solution)/shard_map/ppermute | solution.py:33
  91.1 19.1 %collective-permute-start.9 = (bf16[128,5120]{1,0:T(8,128)(2,1)S(1)}, bf16[128,5120]{1,0:T(8,128)(2,1)S(1)}, u32[]{:S(2)}, u32[]{:S(2)}) collective-permute-start(bf16[128,5120]{1,0:T(8,128)(2,1)S(1)} %add_convert_fusion), channel_id=1, source_target_pairs={{0,1},{1,2},{2,3},{3,0},{4,5},{5,6},{6,7},{7,4},{8,11},{9,8},{10,9... | collective-permute-start | bytes 3932168 | tf_op jit(solution)/shard_map/ppermute | solution.py:33
  110.4 12.1 %collective-permute-start.13 = (bf16[64,3072]{1,0:T(8,128)(2,1)S(1)}, bf16[64,3072]{1,0:T(8,128)(2,1)S(1)}, u32[]{:S(2)}, u32[]{:S(2)}) collective-permute-start(bf16[64,3072]{1,0:T(8,128)(2,1)S(1)} %get-tuple-element.62), channel_id=1, source_target_pairs={{0,1},{1,2},{2,3},{3,0},{4,5},{5,6},{6,7},{7,4},{8,11},{9,8},{10,9... | collective-permute-start | bytes 1179656 | tf_op jit(solution)/shard_map/ppermute | solution.py:33
  110.5 17.1 %collective-permute-start.10 = (bf16[64,5120]{1,0:T(8,128)(2,1)S(1)}, bf16[64,5120]{1,0:T(8,128)(2,1)S(1)}, u32[]{:S(2)}, u32[]{:S(2)}) collective-permute-start(bf16[64,5120]{1,0:T(8,128)(2,1)S(1)} %add_convert_fusion.2), channel_id=1, source_target_pairs={{0,4},{1,5},{2,6},{3,7},{4,0},{5,1},{6,2},{7,3},{8,12},{9,13},{10,... | collective-permute-start | bytes 1966088 | tf_op jit(solution)/shard_map/ppermute | solution.py:33
  111.3 16.6 %collective-permute-start.12 = (bf16[64,3072]{1,0:T(8,128)(2,1)S(1)}, bf16[64,3072]{1,0:T(8,128)(2,1)S(1)}, u32[]{:S(2)}, u32[]{:S(2)}) collective-permute-start(bf16[64,3072]{1,0:T(8,128)(2,1)S(1)} %get-tuple-element.61), channel_id=1, source_target_pairs={{0,3},{1,0},{2,1},{3,2},{4,7},{5,4},{6,5},{7,6},{8,9},{9,10},{10,1... | collective-permute-start | bytes 1179656 | tf_op jit(solution)/shard_map/ppermute | solution.py:33
  122.6 9.1 %collective-permute-start.14 = (bf16[64,3072]{1,0:T(8,128)(2,1)S(1)}, bf16[64,3072]{1,0:T(8,128)(2,1)S(1)}, u32[]{:S(2)}, u32[]{:S(2)}) collective-permute-start(bf16[64,3072]{1,0:T(8,128)(2,1)S(1)} %add_convert_fusion.4), channel_id=1, source_target_pairs={{0,1},{1,2},{2,3},{3,0},{4,5},{5,6},{6,7},{7,4},{8,11},{9,8},{10,9... | collective-permute-start | bytes 1179656 | tf_op jit(solution)/shard_map/ppermute | solution.py:33

commit v4 on v3

--- a/solution.py
+++ b/solution.py
@@ -18,7 +18,7 @@
 NN = (((1,), (0,)), ((), ()))
 META = 16
 PAYLOAD = 1024 + META
-TILE = 512
+TILE = 256
 LIMIT = 20 << 20
 
 
@@ -152,21 +152,19 @@
         highs = highs + 1 - is_low
 
     def step(i, carry):
-        first = 2 * i
-        mixed = (first + 1) == highs
-        base = jnp.where(first + 1 < highs, 2048, 0)
-        at = pl.multiple_of(i * 512, 512)
-        g0 = gbuf[pl.ds(first, 1), :]
-        g1 = gbuf[pl.ds(first + 1, 1), :]
+        mixed = 2 * i + 1 == highs
 
         @pl.when(jnp.logical_not(mixed))
         def _():
+            at = pl.multiple_of(i * 512, 512)
+            g0 = gbuf[pl.ds(2 * i, 1), :]
+            g1 = gbuf[pl.ds(2 * i + 1, 1), :]
             attend_rows(
                 q_ref,
                 acc_ref,
                 l_ref,
                 m_ref,
-                base,
+                pl.multiple_of(jnp.where(2 * i + 1 < highs, 2048, 0), 2048),
                 16,
                 kbuf[pl.ds(at, 512), :],
                 vbuf[pl.ds(at, 512), :],
@@ -175,28 +173,23 @@
 
         @pl.when(mixed)
         def _():
-            attend_rows(
-                q_ref,
-                acc_ref,
-                l_ref,
-                m_ref,
-                2048,
-                16,
-                kbuf[pl.ds(at, 256), :],
-                vbuf[pl.ds(at, 256), :],
-                jnp.concatenate([g0, g0], axis=1),
-            )
-            attend_rows(
-                q_ref,
-                acc_ref,
-                l_ref,
-                m_ref,
-                0,
-                16,
-                kbuf[pl.ds(at + 256, 256), :],
-                vbuf[pl.ds(at + 256, 256), :],
-                jnp.concatenate([g1, g1], axis=1),
-            )
+            def single(slot, inner):
+                at = pl.multiple_of(slot * 256, 256)
+                gain = gbuf[pl.ds(slot, 1), :]
+                attend_rows(
+                    q_ref,
+                    acc_ref,
+                    l_ref,
+                    m_ref,
+                    pl.multiple_of(jnp.where(slot < highs, 2048, 0), 2048),
+                    16,
+                    kbuf[pl.ds(at, 256), :],
+                    vbuf[pl.ds(at, 256), :],
+                    jnp.concatenate([gain, gain], axis=1),
+                )
+                return inner
+
+            lax.fori_loop(2 * i, 2 * i + 2, single, 0)
 
         return carry
 
@@ -208,10 +201,10 @@
     for half in range(2):
         rows = slice(half * 256, half * 256 + 256)
         o_ref[512 + half * 256 : 768 + half * 256, :] = (
-            v_ref[rows, :].astype(F32) * vs_ref[half, 0].astype(F32)
+            v_ref[rows, :].astype(F32) * vs_ref[half : half + 1, :].astype(F32)
         ).astype(BF16)
     row = lax.broadcasted_iota(jnp.int32, (META, 128), 0)
-    low, high = ks_ref[0, 0].astype(F32), ks_ref[1, 0].astype(F32)
+    low, high = ks_ref[0:1, :].astype(F32), ks_ref[1:2, :].astype(F32)
     place = place_ref[0].astype(F32)
     meta = jnp.where(row == 0, low, jnp.where(row == 1, high, jnp.where(row == 2, place, 0.0)))
     o_ref[1024:PAYLOAD, :] = meta.astype(BF16)
@@ -223,10 +216,10 @@
     return pl.pallas_call(
         pack_kernel,
         out_shape=jax.ShapeDtypeStruct((PAYLOAD, 128), BF16),
-        in_specs=[vmem, vmem, smem, smem, smem],
+        in_specs=[vmem, vmem, vmem, vmem, smem],
         out_specs=vmem,
         name="pack",
-    )(keys, values, k_scale.astype(F32), v_scale.astype(F32), block_place)
+    )(keys, values, k_scale, v_scale, block_place)
 
 
 def group_kernel(inv, sizes, start, finish, *refs):
@@ -245,7 +238,10 @@
     if start:
         own_steps(q_ref, acc_ref, l_ref, m_ref, own_ref, inv)
     own_place = place_of(own_ref)
-    other_steps(q_ref, acc_ref, l_ref, m_ref, own_place, others, kbuf, vbuf, gbuf, inv)
+    if others:
+        other_steps(
+            q_ref, acc_ref, l_ref, m_ref, own_place, others, kbuf, vbuf, gbuf, inv
+        )
     if finish:
         acc_ref[...] = acc_ref[...] / l_ref[...]
         for block in range(8):
@@ -280,9 +276,9 @@
         in_specs=specs,
         out_specs=[vmem] * len(outs),
         scratch_shapes=[
-            pltpu.VMEM((2 * count * 256, 128), BF16),
-            pltpu.VMEM((2 * count * 256, 256), BF16),
-            pltpu.VMEM((2 * count, 128), F32),
+            pltpu.VMEM((max(count, 1) * 512, 128), BF16),
+            pltpu.VMEM((max(count, 1) * 512, 256), BF16),
+            pltpu.VMEM((max(count, 1) * 2, 128), F32),
         ],
         input_output_aliases=aliases,
         compiler_params=pltpu.CompilerParams(vmem_limit_bytes=LIMIT),
@@ -337,8 +333,10 @@
     got_far = moved(x_far, ahead)
     (y_out,) = project(att, weight, (1, 3, 5, 7), (4,), first_columns, rest, "project_y")
     got_y = moved(y_out, beside)
+    att, x_far, y_out = lax.optimization_barrier((att, x_far, y_out))
     (x_behind,) = project(att, weight, (4, 5), (2,), 0, first_columns, "project_behind")
     got_front = moved(x_behind, behind)
+    att, x_behind = lax.optimization_barrier((att, x_behind))
     x_ahead, x_own = project(att, weight, (2, 3, 6, 7), (2, 2), 0, first_columns, "project_c")
     (y_own,) = project(att, weight, (0, 2, 4, 6), (4,), first_columns, rest, "project_d")
     got_back = moved(added(x_ahead, got_far).astype(BF16), ahead)
@@ -367,20 +365,6 @@
     q = query.reshape(4096, 128)
     k = keys.reshape(512, 128)
     own = packed(k, values.reshape(512, 128), k_scale, v_scale, block_place)
-    partner = moved(own, swapped)
-    pair = jnp.concatenate([own, partner], axis=0)
-    one, two = moved(pair, near), moved(pair, across)
-    state = attend(q, own, [partner], None, None, inv, "attend_own")
-    pair, four_in, *state = lax.optimization_barrier((pair, own, *state))
-    three = moved(pair, diagonal)
-    four = moved(four_in, opposite)
-    one, two, *state = lax.optimization_barrier((one, two, *state))
-    more = moved(jnp.concatenate([one, two], axis=0), swapped)
-    state = attend(q, own, [one, two], state, None, inv, "attend_near")
-    three, four, *state = lax.optimization_barrier((three, four, *state))
-    last = jnp.concatenate([three, four], axis=0)
-    final = moved(last, swapped)
-    state = attend(q, own, [more], state, None, inv, "attend_more")
     core = lax.axis_index("ctx") % 2
     place = lax.axis_index("head")
     target = jnp.arange(8, dtype=jnp.int32)
@@ -389,8 +373,24 @@
     forward = 1 + 2 * core
     slot = jnp.where(along == 0, 3, jnp.where(along == 2, 0, jnp.where(along == forward, 1, 2)))
     order = (slot * 2 + side).astype(jnp.int32)
-    attended = attend(q, own, [last, final], state, order, inv, "attend_rest")[0]
-    return scattered(attended, out_weight, 5120)
+    own, order = lax.optimization_barrier((own, order))
+    partner = moved(own, swapped)
+    pair = jnp.concatenate([own, partner], axis=0)
+    one, two = moved(pair, near), moved(pair, across)
+    state = attend(q, own, [], None, None, inv, "attend_own")
+    pair, mine, *state = lax.optimization_barrier((pair, own, *state))
+    three, four = moved(pair, diagonal), moved(mine, opposite)
+    state = attend(q, own, [partner], state, None, inv, "attend_partner")
+    one, two, *state = lax.optimization_barrier((one, two, *state))
+    more = moved(jnp.concatenate([one, two], axis=0), swapped)
+    state = attend(q, own, [one, two], state, None, inv, "attend_near")
+    state = attend(q, own, [more], state, None, inv, "attend_more")
+    three, four, *state = lax.optimization_barrier((three, four, *state))
+    last = jnp.concatenate([three, four], axis=0)
+    final = moved(last, swapped)
+    state = attend(q, own, [last], state, None, inv, "attend_last")
+    attended = attend(q, own, [final], state, order, inv, "attend_rest")[0]
+    return scattered(attended, out_weight, 4864)
 
 
 def solution(mesh):

time: 133 us -> 128 us (0.962)
  starting transfers between devices: 25.9 us -> 21.9 us
  other arithmetic: 6.02 us -> 2.53 us
  local copies, waits for them, and re-layouts: 0.1 us -> 3.29 us
  Pallas kernels: 43.7 us -> 40.7 us
  waiting for transfers between devices: 57 us -> 59 us
    ppermute x15, starting transfers between devices: 25.9 us -> 21.9 us  [moved(): return lax.ppermute(array, AXES, pairs)]
    unnamed x11 -> x18, local copies, waits for them, and re-layouts: 0.06 us -> 3.22 us
    pallas_call x4 -> x6, Pallas kernels: 32.4 us -> 29.4 us  [attend(): pl.pallas_call(functools.partial(group_kernel, inv, sizes, start, finish)...]
    convert_element_type x2 -> x0, other arithmetic: 2.51 us -> none  [the longest x1 1.31 us: packed(): k_scale.astype(F32)]
    ppermute x15, waiting for transfers between devices: 57 us -> 59 us  [moved(): return lax.ppermute(array, AXES, pairs)]
  transfers between devices with their start and end apart: 15 -> 15, of which waited for: 9 -> 8; matrix products, arithmetic and copies ran while one was open for 1% -> 2% of each run, Pallas kernels for 21% -> 24%
where the time goes in v4:
time: 128 us
  waiting for transfers between devices  59 us (46%)
  Pallas kernels  40.7 us (32%)
  starting transfers between devices  21.9 us (17%)
  local copies, waits for them, and re-layouts  3.29 us (3%)
  other arithmetic  2.53 us (2%)
    ppermute x15, waiting for transfers between devices, moved(): return lax.ppermute(array, AXES, pairs)  59 us
    pallas_call x6, Pallas kernels, attend(): pl.pallas_call(functools.partial(group_kernel, inv, sizes, start, finish)...  29.4 us
    ppermute x15, starting transfers between devices, moved(): return lax.ppermute(array, AXES, pairs)  21.9 us
    pallas_call x5, Pallas kernels, project(): pl.pallas_call(functools.partial(project_kernel, blocks, splits, first, c...  9.58 us
    unnamed x18, local copies, waits for them, and re-layouts  3.22 us
  transfers between devices with their start and end apart: 15, of which 8 were waited for; matrix products, arithmetic and copies ran while one was open for 2% of the time, Pallas kernels for 24%

profile of v4, /device:TPU:24, one launch (start us, length us, event | category | flops | bytes accessed | tf_op | source)
XLA Modules:
  0.0 127.7 jit_solution(11466544684690084909)
XLA Ops:
  0.0 1.7 %pack.1.refs_1_ = bf16[1040,128]{1,0:T(8,128)(2,1)} custom-call(bf16[512,128]{1,0:T(8,128)(2,1)} %bitcast.11, bf16[512,128]{1,0:T(8,128)(2,1)} %bitcast.12, bf16[2,1]{1,0:T(2,128)(2,1)} %ks_ref.1, bf16[2,1]{1,0:T(2,128)(2,1)} %vs_ref.1, s32[2]{0:T(128)} %place_ref.1), custom_call_target="tpu_custom_call" | custom-call | tf_op jit(solution)/shard_map/pack/pallas_call | solution.py:216
  1.8 1.0 constant_dynamic-update-slice_fusion.1
  2.7 0.8 collective-permute-done.refs_2_
  3.6 2.0 %collective-permute-start.3 = (bf16[2080,128]{1,0:T(8,128)(2,1)S(1)}, bf16[2080,128]{1,0:T(8,128)(2,1)S(1)}, u32[]{:S(2)}, u32[]{:S(2)}) collective-permute-start(bf16[2080,128]{1,0:T(8,128)(2,1)S(1)} %constant_dynamic-update-slice_fusion), channel_id=1, source_target_pairs={{0,32},{1,33},{2,34},{3,35},{4,36},{5,37},{6,38},{7,39},{8,104},{9... | collective-permute-start | bytes 1597448 | tf_op jit(solution)/shard_map/ppermute | solution.py:33
  5.5 1.2 collective-permute-start.4
  6.8 0.9 copy-done
  7.7 1.2 copy-done.2
  9.0 2.2 %attend_own.1 = (f32[4096,128]{1,0:T(8,128)S(1)}, f32[4096,128]{1,0:T(8,128)S(1)}, f32[4096,128]{1,0:T(8,128)S(1)}) custom-call(bf16[4096,128]{1,0:T(8,128)(2,1)S(1)} %bitcast.5, bf16[1040,128]{1,0:T(8,128)(2,1)S(1)} %copy-done), custom_call_target="tpu_custom_call" | custom-call | flops 3221225472 | bytes 1048576 | tf_op jit(solution)/shard_map/attend_own/pallas_call | solution.py:273
  11.2 2.2 %attend_partner.1 = (f32[4096,128]{1,0:T(8,128)S(1)}, f32[4096,128]{1,0:T(8,128)S(1)}, f32[4096,128]{1,0:T(8,128)S(1)}) custom-call(bf16[4096,128]{1,0:T(8,128)(2,1)S(1)} %bitcast.6, bf16[1040,128]{1,0:T(8,128)(2,1)S(1)} %copy-done.1, bf16[1040,128]{1,0:T(8,128)(2,1)S(1)} %collective-permute-done.refs_2_, ...), custom_call_target="tpu_custom_call", output_to_operand_aliasing={{0}: (3, {}), {1}: (4, {}), {2}: (5, {})} | custom-call | flops 2147483648 | bytes 1048576 | tf_op jit(solution)/shard_map/attend_partner/pallas_call | solution.py:273
  13.4 4.8 %collective-permute-done.3.refs_2_ = bf16[2080,128]{1,0:T(8,128)(2,1)S(1)} collective-permute-done((bf16[2080,128]{1,0:T(8,128)(2,1)S(1)}, bf16[2080,128]{1,0:T(8,128)(2,1)S(1)}, u32[]{:S(2)}, u32[]{:S(2)}) %collective-permute-start.3) | collective-permute-done | bytes 532512 | tf_op jit(solution)/shard_map/ppermute | solution.py:33
  18.3 3.8 %collective-permute-start.5 = (bf16[4160,128]{1,0:T(8,128)(2,1)S(1)}, bf16[4160,128]{1,0:T(8,128)(2,1)S(1)}, u32[]{:S(2)}, u32[]{:S(2)}) collective-permute-start(bf16[4160,128]{1,0:T(8,128)(2,1)S(1)} %pad_maximum_fusion), channel_id=1, source_target_pairs={{0,8},{1,9},{2,10},{3,11},{4,12},{5,13},{6,14},{7,15},{8,0},{9,1},... | collective-permute-start | bytes 3194888 | tf_op jit(solution)/shard_map/ppermute | solution.py:33
  22.0 4.8 %collective-permute-start.2 = (bf16[1040,128]{1,0:T(8,128)(2,1)S(1)}, bf16[1040,128]{1,0:T(8,128)(2,1)S(1)}, u32[]{:S(2)}, u32[]{:S(2)}) collective-permute-start(bf16[1040,128]{1,0:T(8,128)(2,1)S(1)} %copy-done.1), channel_id=1, source_target_pairs={{0,80},{1,81},{2,82},{3,83},{4,84},{5,85},{6,86},{7,87},{8,88},{9,... | collective-permute-start | bytes 798728 | tf_op jit(solution)/shard_map/ppermute | solution.py:33
  26.9 6.7 %attend_near.1 = (f32[4096,128]{1,0:T(8,128)S(1)}, f32[4096,128]{1,0:T(8,128)S(1)}, f32[4096,128]{1,0:T(8,128)S(1)}) custom-call(bf16[4096,128]{1,0:T(8,128)(2,1)S(1)} %bitcast.7, bf16[1040,128]{1,0:T(8,128)(2,1)S(1)} %copy-done.1, bf16[2080,128]{1,0:T(8,128)(2,1)S(1)} %collective-permute-done.3.refs_2_, ...), custom_call_target="tpu_custom_call", output_to_operand_aliasing={{0}: (4, {}), {1}: (5, {}), {2}: (6, {})} | custom-call | flops 8589934592 | bytes 1048576 | tf_op jit(solution)/shard_map/attend_near/pallas_call | solution.py:273
  33.6 6.7 %attend_more.1 = (f32[4096,128]{1,0:T(8,128)S(1)}, f32[4096,128]{1,0:T(8,128)S(1)}, f32[4096,128]{1,0:T(8,128)S(1)}) custom-call(bf16[4096,128]{1,0:T(8,128)(2,1)S(1)} %bitcast.8, bf16[1040,128]{1,0:T(8,128)(2,1)S(1)} %copy-done.1, bf16[4160,128]{1,0:T(8,128)(2,1)S(1)} %collective-permute-done.5.refs_2_, ...), custom_call_target="tpu_custom_call", output_to_operand_aliasing={{0}: (3, {}), {1}: (4, {}), {2}: (5, {})} | custom-call | flops 8589934592 | bytes 1048576 | tf_op jit(solution)/shard_map/attend_more/pallas_call | solution.py:273
  40.4 3.3 %collective-permute-done.2 = bf16[1040,128]{1,0:T(8,128)(2,1)S(1)} collective-permute-done((bf16[1040,128]{1,0:T(8,128)(2,1)S(1)}, bf16[1040,128]{1,0:T(8,128)(2,1)S(1)}, u32[]{:S(2)}, u32[]{:S(2)}) %collective-permute-start.2) | collective-permute-done | bytes 266272 | tf_op jit(solution)/shard_map/ppermute | solution.py:33
  44.1 5.1 %attend_last.1 = (f32[4096,128]{1,0:T(8,128)S(1)}, f32[4096,128]{1,0:T(8,128)S(1)}, f32[4096,128]{1,0:T(8,128)S(1)}) custom-call(bf16[4096,128]{1,0:T(8,128)(2,1)S(1)} %bitcast.9, bf16[1040,128]{1,0:T(8,128)(2,1)S(1)} %copy-done.1, ...), custom_call_target="tpu_custom_call", output_to_operand_aliasing={{0}: (3, {}), {1}: (4, {}), {2}: (5, {})} | custom-call | flops 6442450944 | bytes 1048576 | tf_op jit(solution)/shard_map/attend_last/pallas_call | solution.py:273
  49.3 6.4 %attend_rest.1 = (bf16[512,1024]{1,0:T(8,128)(2,1)S(1)}, f32[4096,128]{1,0:T(8,128)S(1)}, f32[4096,128]{1,0:T(8,128)S(1)}, f32[4096,128]{1,0:T(8,128)S(1)}) custom-call(bf16[4096,128]{1,0:T(8,128)(2,1)S(1)} %bitcast.10, bf16[1040,128]{1,0:T(8,128)(2,1)S(1)} %copy-done.1, ...), custom_call_target="tpu_custom_call", output_to_operand_aliasing={{1}: (4, {}), {2}: (5, {}), {3}: (6, {})} | custom-call | flops 6442450944 | bytes 1048576 | tf_op jit(solution)/shard_map/attend_rest/pallas_call | solution.py:273
  55.7 1.5 %project_far.1 = bf16[128,4864]{1,0:T(8,128)(2,1)S(1)} custom-call(bf16[512,1024]{1,0:T(8,128)(2,1)S(1)} %get-tuple-element.78.a_ref, bf16[1024,8192]{1,0:T(8,128)(2,1)S(1)} %bitcast.4), custom_call_target="tpu_custom_call" | custom-call | flops 1275068416 | bytes 9961472 | tf_op jit(solution)/shard_map/project_far/pallas_call | solution.py:308
  57.2 1.6 %collective-permute-start.8 = (bf16[128,4864]{1,0:T(8,128)(2,1)S(1)}, bf16[128,4864]{1,0:T(8,128)(2,1)S(1)}, u32[]{:S(2)}, u32[]{:S(2)}) collective-permute-start(bf16[128,4864]{1,0:T(8,128)(2,1)S(1)} %project_far.1), channel_id=1, source_target_pairs={{0,1},{1,2},{2,3},{3,0},{4,5},{5,6},{6,7},{7,4},{8,11},{9,8},{10,9... | collective-permute-start | bytes 3735560 | tf_op jit(solution)/shard_map/ppermute | solution.py:33
  58.7 1.9 %project_y.1 = bf16[256,3328]{1,0:T(8,128)(2,1)S(1)} custom-call(bf16[512,1024]{1,0:T(8,128)(2,1)S(1)} %get-tuple-element.78.a_ref, bf16[1024,8192]{1,0:T(8,128)(2,1)S(1)} %bitcast.4), custom_call_target="tpu_custom_call" | custom-call | flops 1744830464 | bytes 6815744 | tf_op jit(solution)/shard_map/project_y/pallas_call | solution.py:308
  60.7 1.5 %project_behind.1 = bf16[128,4864]{1,0:T(8,128)(2,1)S(1)} custom-call(bf16[512,1024]{1,0:T(8,128)(2,1)S(1)} %get-tuple-element.78.a_ref, bf16[1024,8192]{1,0:T(8,128)(2,1)S(1)} %bitcast.4), custom_call_target="tpu_custom_call" | custom-call | flops 1275068416 | bytes 9961472 | tf_op jit(solution)/shard_map/project_behind/pallas_call | solution.py:308
  62.2 1.8 %collective-permute-start.7 = (bf16[128,4864]{1,0:T(8,128)(2,1)S(1)}, bf16[128,4864]{1,0:T(8,128)(2,1)S(1)}, u32[]{:S(2)}, u32[]{:S(2)}) collective-permute-start(bf16[128,4864]{1,0:T(8,128)(2,1)S(1)} %project_behind.1), channel_id=1, source_target_pairs={{0,3},{1,0},{2,1},{3,2},{4,7},{5,4},{6,5},{7,6},{8,9},{9,10},{10,1... | collective-permute-start | bytes 3735560 | tf_op jit(solution)/shard_map/ppermute | solution.py:33
  64.7 2.7 %project_c.1 = (bf16[128,4864]{1,0:T(8,128)(2,1)S(1)}, bf16[128,4864]{1,0:T(8,128)(2,1)S(1)}) custom-call(bf16[512,1024]{1,0:T(8,128)(2,1)S(1)} %get-tuple-element.78.a_ref, bf16[1024,8192]{1,0:T(8,128)(2,1)S(1)} %bitcast.4), custom_call_target="tpu_custom_call" | custom-call | flops 2550136832 | bytes 9961472 | tf_op jit(solution)/shard_map/project_c/pallas_call | solution.py:308
  67.5 15.3 %collective-permute-done.8 = bf16[128,4864]{1,0:T(8,128)(2,1)S(1)} collective-permute-done((bf16[128,4864]{1,0:T(8,128)(2,1)S(1)}, bf16[128,4864]{1,0:T(8,128)(2,1)S(1)}, u32[]{:S(2)}, u32[]{:S(2)}) %collective-permute-start.8) | collective-permute-done | bytes 1245216 | tf_op jit(solution)/shard_map/ppermute | solution.py:33
  83.0 1.6 %collective-permute-start.9 = (bf16[128,4864]{1,0:T(8,128)(2,1)S(1)}, bf16[128,4864]{1,0:T(8,128)(2,1)S(1)}, u32[]{:S(2)}, u32[]{:S(2)}) collective-permute-start(bf16[128,4864]{1,0:T(8,128)(2,1)S(1)} %add_convert_fusion), channel_id=1, source_target_pairs={{0,1},{1,2},{2,3},{3,0},{4,5},{5,6},{6,7},{7,4},{8,11},{9,8},{10,9... | collective-permute-start | bytes 3735560 | tf_op jit(solution)/shard_map/ppermute | solution.py:33
  84.6 1.9 %project_d.1 = bf16[256,3328]{1,0:T(8,128)(2,1)S(1)} custom-call(bf16[512,1024]{1,0:T(8,128)(2,1)S(1)} %get-tuple-element.78.a_ref, bf16[1024,8192]{1,0:T(8,128)(2,1)S(1)} %bitcast.4), custom_call_target="tpu_custom_call" | custom-call | flops 1744830464 | bytes 6815744 | tf_op jit(solution)/shard_map/project_d/pallas_call | solution.py:308
  86.6 17.0 %collective-permute-done.11 = bf16[256,3328]{1,0:T(8,128)(2,1)S(1)} collective-permute-done((bf16[256,3328]{1,0:T(8,128)(2,1)S(1)}, bf16[256,3328]{1,0:T(8,128)(2,1)S(1)}, u32[]{:S(2)}, u32[]{:S(2)}) %collective-permute-start.11) | collective-permute-done | bytes 1703968 | tf_op jit(solution)/shard_map/ppermute | solution.py:33
  105.0 3.1 %collective-permute-start.12 = (bf16[64,3328]{1,0:T(8,128)(2,1)S(1)}, bf16[64,3328]{1,0:T(8,128)(2,1)S(1)}, u32[]{:S(2)}, u32[]{:S(2)}) collective-permute-start(bf16[64,3328]{1,0:T(8,128)(2,1)S(1)} %get-tuple-element.81), channel_id=1, source_target_pairs={{0,3},{1,0},{2,1},{3,2},{4,7},{5,4},{6,5},{7,6},{8,9},{9,10},{10,1... | collective-permute-start | bytes 1277960 | tf_op jit(solution)/shard_map/ppermute | solution.py:33
  108.1 8.8 %collective-permute-done.13 = bf16[64,3328]{1,0:T(8,128)(2,1)S(1)} collective-permute-done((bf16[64,3328]{1,0:T(8,128)(2,1)S(1)}, bf16[64,3328]{1,0:T(8,128)(2,1)S(1)}, u32[]{:S(2)}, u32[]{:S(2)}) %collective-permute-start.13) | collective-permute-done | bytes 426016 | tf_op jit(solution)/shard_map/ppermute | solution.py:33
  117.2 3.6 %collective-permute-done.10 = bf16[64,4864]{1,0:T(8,128)(2,1)S(1)} collective-permute-done((bf16[64,4864]{1,0:T(8,128)(2,1)S(1)}, bf16[64,4864]{1,0:T(8,128)(2,1)S(1)}, u32[]{:S(2)}, u32[]{:S(2)}) %collective-permute-start.10) | collective-permute-done | bytes 622624 | tf_op jit(solution)/shard_map/ppermute | solution.py:33
  121.1 5.4 %collective-permute-done.14 = bf16[64,3328]{1,0:T(8,128)(2,1)S(1)} collective-permute-done((bf16[64,3328]{1,0:T(8,128)(2,1)S(1)}, bf16[64,3328]{1,0:T(8,128)(2,1)S(1)}, u32[]{:S(2)}, u32[]{:S(2)}) %collective-permute-start.14) | collective-permute-done | bytes 426016 | tf_op jit(solution)/shard_map/ppermute | solution.py:33
  126.7 1.0 pad_maximum_fusion.1
  (40 shorter events, 3.7 us)
Async XLA Ops:
  1.8 1.8 %collective-permute-start = (bf16[1040,128]{1,0:T(8,128)(2,1)}, bf16[1040,128]{1,0:T(8,128)(2,1)S(1)}, u32[]{:S(2)}, u32[]{:S(2)}) collective-permute-start(bf16[1040,128]{1,0:T(8,128)(2,1)} %pack.1.refs_1_), channel_id=1, source_target_pairs={{0,8},{1,9},{2,10},{3,11},{4,12},{5,13},{6,14},{7,15},{8,0},{9,1},... | collective-permute-start | bytes 798728 | tf_op jit(solution)/shard_map/ppermute | solution.py:33
  3.6 14.7 %collective-permute-start.3 = (bf16[2080,128]{1,0:T(8,128)(2,1)S(1)}, bf16[2080,128]{1,0:T(8,128)(2,1)S(1)}, u32[]{:S(2)}, u32[]{:S(2)}) collective-permute-start(bf16[2080,128]{1,0:T(8,128)(2,1)S(1)} %constant_dynamic-update-slice_fusion), channel_id=1, source_target_pairs={{0,32},{1,33},{2,34},{3,35},{4,36},{5,37},{6,38},{7,39},{8,104},{9... | collective-permute-start | bytes 1597448 | tf_op jit(solution)/shard_map/ppermute | solution.py:33
  5.5 12.7 %collective-permute-start.4 = (bf16[2080,128]{1,0:T(8,128)(2,1)S(1)}, bf16[2080,128]{1,0:T(8,128)(2,1)S(1)}, u32[]{:S(2)}, u32[]{:S(2)}) collective-permute-start(bf16[2080,128]{1,0:T(8,128)(2,1)S(1)} %constant_dynamic-update-slice_fusion), channel_id=1, source_target_pairs={{0,16},{1,17},{2,18},{3,19},{4,20},{5,21},{6,22},{7,23},{8,72},{9,... | collective-permute-start | bytes 1597448 | tf_op jit(solution)/shard_map/ppermute | solution.py:33
  6.8 1.0 copy-start
  7.7 1.2 copy-start.2
  9.0 2.2 %copy-start.1 = (bf16[1040,128]{1,0:T(8,128)(2,1)S(1)}, bf16[1040,128]{1,0:T(8,128)(2,1)}, u32[]{:S(2)}) copy-start(bf16[1040,128]{1,0:T(8,128)(2,1)} %pack.1.refs_1_) | copy-start | bytes 798724
  18.3 15.3 %collective-permute-start.5 = (bf16[4160,128]{1,0:T(8,128)(2,1)S(1)}, bf16[4160,128]{1,0:T(8,128)(2,1)S(1)}, u32[]{:S(2)}, u32[]{:S(2)}) collective-permute-start(bf16[4160,128]{1,0:T(8,128)(2,1)S(1)} %pad_maximum_fusion), channel_id=1, source_target_pairs={{0,8},{1,9},{2,10},{3,11},{4,12},{5,13},{6,14},{7,15},{8,0},{9,1},... | collective-permute-start | bytes 3194888 | tf_op jit(solution)/shard_map/ppermute | solution.py:33
  22.0 21.6 %collective-permute-start.1 = (bf16[2080,128]{1,0:T(8,128)(2,1)S(1)}, bf16[2080,128]{1,0:T(8,128)(2,1)S(1)}, u32[]{:S(2)}, u32[]{:S(2)}) collective-permute-start(bf16[2080,128]{1,0:T(8,128)(2,1)S(1)} %constant_dynamic-update-slice_fusion), channel_id=1, source_target_pairs={{0,48},{1,49},{2,50},{3,51},{4,52},{5,53},{6,54},{7,55},{8,120},{9... | collective-permute-start | bytes 1597448 | tf_op jit(solution)/shard_map/ppermute | solution.py:33
  22.0 21.6 %collective-permute-start.2 = (bf16[1040,128]{1,0:T(8,128)(2,1)S(1)}, bf16[1040,128]{1,0:T(8,128)(2,1)S(1)}, u32[]{:S(2)}, u32[]{:S(2)}) collective-permute-start(bf16[1040,128]{1,0:T(8,128)(2,1)S(1)} %copy-done.1), channel_id=1, source_target_pairs={{0,80},{1,81},{2,82},{3,83},{4,84},{5,85},{6,86},{7,87},{8,88},{9,... | collective-permute-start | bytes 798728 | tf_op jit(solution)/shard_map/ppermute | solution.py:33
  33.6 10.5 %copy-start.3 = (bf16[512,8,128]{2,1,0:T(8,128)(2,1)S(1)}, bf16[512,8,128]{2,1,0:T(8,128)(2,1)}, u32[]{:S(2)}) copy-start(bf16[512,8,128]{2,1,0:T(8,128)(2,1)} %param.7) | copy-start | bytes 3145732
  43.8 5.5 %collective-permute-start.6 = (bf16[3120,128]{1,0:T(8,128)(2,1)S(1)}, bf16[3120,128]{1,0:T(8,128)(2,1)S(1)}, u32[]{:S(2)}, u32[]{:S(2)}) collective-permute-start(bf16[3120,128]{1,0:T(8,128)(2,1)S(1)} %constant_dynamic-update-slice_fusion.2.refs_2_), channel_id=1, source_target_pairs={{0,8},{1,9},{2,10},{3,11},{4,12},{5,13},{6,14},{7,15},{8,0},{9,1},... | collective-permute-start | bytes 2396168 | tf_op jit(solution)/shard_map/ppermute | solution.py:33
  44.1 11.6 %slice-start = ((s8[16777216]{0:T(1024)(128)(4,1)}), s8[4194304]{0:T(1024)(128)(4,1)S(1)}, s32[]{:S(2)}) async-start(s8[16777216]{0:T(1024)(128)(4,1)} %bitcast.3), calls=%async_computation | async-start | bytes 8388608
  44.1 11.6 %slice-start.1 = ((s8[16777216]{0:T(1024)(128)(4,1)}), s8[4194304]{0:T(1024)(128)(4,1)S(1)}, s32[]{:S(2)}) async-start(s8[16777216]{0:T(1024)(128)(4,1)} %bitcast.3), calls=%async_computation.1 | async-start | bytes 8388608
  49.3 6.4 %slice-start.2 = ((s8[16777216]{0:T(1024)(128)(4,1)}), s8[4194304]{0:T(1024)(128)(4,1)S(1)}, s32[]{:S(2)}) async-start(s8[16777216]{0:T(1024)(128)(4,1)} %bitcast.3), calls=%async_computation.2 | async-start | bytes 8388608
  49.3 6.4 %slice-start.3 = ((s8[16777216]{0:T(1024)(128)(4,1)}), s8[4194304]{0:T(1024)(128)(4,1)S(1)}, s32[]{:S(2)}) async-start(s8[16777216]{0:T(1024)(128)(4,1)} %bitcast.3), calls=%async_computation.3 | async-start | bytes 8388608
  57.2 25.6 %collective-permute-start.8 = (bf16[128,4864]{1,0:T(8,128)(2,1)S(1)}, bf16[128,4864]{1,0:T(8,128)(2,1)S(1)}, u32[]{:S(2)}, u32[]{:S(2)}) collective-permute-start(bf16[128,4864]{1,0:T(8,128)(2,1)S(1)} %project_far.1), channel_id=1, source_target_pairs={{0,1},{1,2},{2,3},{3,0},{4,5},{5,6},{6,7},{7,4},{8,11},{9,8},{10,9... | collective-permute-start | bytes 3735560 | tf_op jit(solution)/shard_map/ppermute | solution.py:33
  62.2 41.6 %collective-permute-start.7 = (bf16[128,4864]{1,0:T(8,128)(2,1)S(1)}, bf16[128,4864]{1,0:T(8,128)(2,1)S(1)}, u32[]{:S(2)}, u32[]{:S(2)}) collective-permute-start(bf16[128,4864]{1,0:T(8,128)(2,1)S(1)} %project_behind.1), channel_id=1, source_target_pairs={{0,3},{1,0},{2,1},{3,2},{4,7},{5,4},{6,5},{7,6},{8,9},{9,10},{10,1... | collective-permute-start | bytes 3735560 | tf_op jit(solution)/shard_map/ppermute | solution.py:33
  64.0 39.6 %collective-permute-start.11 = (bf16[256,3328]{1,0:T(8,128)(2,1)S(1)}, bf16[256,3328]{1,0:T(8,128)(2,1)S(1)}, u32[]{:S(2)}, u32[]{:S(2)}) collective-permute-start(bf16[256,3328]{1,0:T(8,128)(2,1)S(1)} %project_y.1), channel_id=1, source_target_pairs={{0,4},{1,5},{2,6},{3,7},{4,0},{5,1},{6,2},{7,3},{8,12},{9,13},{10,... | collective-permute-start | bytes 5111816 | tf_op jit(solution)/shard_map/ppermute | solution.py:33
  83.0 20.7 %collective-permute-start.9 = (bf16[128,4864]{1,0:T(8,128)(2,1)S(1)}, bf16[128,4864]{1,0:T(8,128)(2,1)S(1)}, u32[]{:S(2)}, u32[]{:S(2)}) collective-permute-start(bf16[128,4864]{1,0:T(8,128)(2,1)S(1)} %add_convert_fusion), channel_id=1, source_target_pairs={{0,1},{1,2},{2,3},{3,0},{4,5},{5,6},{6,7},{7,4},{8,11},{9,8},{10,9... | collective-permute-start | bytes 3735560 | tf_op jit(solution)/shard_map/ppermute | solution.py:33
  104.0 12.9 %collective-permute-start.13 = (bf16[64,3328]{1,0:T(8,128)(2,1)S(1)}, bf16[64,3328]{1,0:T(8,128)(2,1)S(1)}, u32[]{:S(2)}, u32[]{:S(2)}) collective-permute-start(bf16[64,3328]{1,0:T(8,128)(2,1)S(1)} %get-tuple-element.82), channel_id=1, source_target_pairs={{0,1},{1,2},{2,3},{3,0},{4,5},{5,6},{6,7},{7,4},{8,11},{9,8},{10,9... | collective-permute-start | bytes 1277960 | tf_op jit(solution)/shard_map/ppermute | solution.py:33
  104.2 16.5 %collective-permute-start.10 = (bf16[64,4864]{1,0:T(8,128)(2,1)S(1)}, bf16[64,4864]{1,0:T(8,128)(2,1)S(1)}, u32[]{:S(2)}, u32[]{:S(2)}) collective-permute-start(bf16[64,4864]{1,0:T(8,128)(2,1)S(1)} %add_convert_fusion.2), channel_id=1, source_target_pairs={{0,4},{1,5},{2,6},{3,7},{4,0},{5,1},{6,2},{7,3},{8,12},{9,13},{10,... | collective-permute-start | bytes 1867784 | tf_op jit(solution)/shard_map/ppermute | solution.py:33
  105.0 16.1 %collective-permute-start.12 = (bf16[64,3328]{1,0:T(8,128)(2,1)S(1)}, bf16[64,3328]{1,0:T(8,128)(2,1)S(1)}, u32[]{:S(2)}, u32[]{:S(2)}) collective-permute-start(bf16[64,3328]{1,0:T(8,128)(2,1)S(1)} %get-tuple-element.81), channel_id=1, source_target_pairs={{0,3},{1,0},{2,1},{3,2},{4,7},{5,4},{6,5},{7,6},{8,9},{9,10},{10,1... | collective-permute-start | bytes 1277960 | tf_op jit(solution)/shard_map/ppermute | solution.py:33
  117.1 9.4 %collective-permute-start.14 = (bf16[64,3328]{1,0:T(8,128)(2,1)S(1)}, bf16[64,3328]{1,0:T(8,128)(2,1)S(1)}, u32[]{:S(2)}, u32[]{:S(2)}) collective-permute-start(bf16[64,3328]{1,0:T(8,128)(2,1)S(1)} %add_convert_fusion.4), channel_id=1, source_target_pairs={{0,1},{1,2},{2,3},{3,0},{4,5},{5,6},{6,7},{7,4},{8,11},{9,8},{10,9... | collective-permute-start | bytes 1277960 | tf_op jit(solution)/shard_map/ppermute | solution.py:33

commit v5 on v4

--- a/solution.py
+++ b/solution.py
@@ -334,10 +334,11 @@
     (y_out,) = project(att, weight, (1, 3, 5, 7), (4,), first_columns, rest, "project_y")
     got_y = moved(y_out, beside)
     att, x_far, y_out = lax.optimization_barrier((att, x_far, y_out))
+    x_ahead, x_own = project(att, weight, (2, 3, 6, 7), (2, 2), 0, first_columns, "project_c")
+    att, x_ahead, x_own = lax.optimization_barrier((att, x_ahead, x_own))
     (x_behind,) = project(att, weight, (4, 5), (2,), 0, first_columns, "project_behind")
     got_front = moved(x_behind, behind)
     att, x_behind = lax.optimization_barrier((att, x_behind))
-    x_ahead, x_own = project(att, weight, (2, 3, 6, 7), (2, 2), 0, first_columns, "project_c")
     (y_own,) = project(att, weight, (0, 2, 4, 6), (4,), first_columns, rest, "project_d")
     got_back = moved(added(x_ahead, got_far).astype(BF16), ahead)
     y_far, y_ahead, y_behind, y_mine = [

time: 128 us -> 126 us (0.984)
  waiting for transfers between devices: 59 us -> 57.6 us
    ppermute x15, waiting for transfers between devices: 59 us -> 57.6 us  [moved(): return lax.ppermute(array, AXES, pairs)]
  transfers between devices with their start and end apart: 15 -> 15, of which waited for: 8 -> 9; matrix products, arithmetic and copies ran while one was open for 2% -> 2% of each run, Pallas kernels for 24% -> 24%
where the time goes in v5:
time: 126 us
  waiting for transfers between devices  57.6 us (46%)
  Pallas kernels  40.3 us (32%)
  starting transfers between devices  22.3 us (18%)
  local copies, waits for them, and re-layouts  3.29 us (3%)
  other arithmetic  2.53 us (2%)
    ppermute x15, waiting for transfers between devices, moved(): return lax.ppermute(array, AXES, pairs)  57.6 us
    pallas_call x6, Pallas kernels, attend(): pl.pallas_call(functools.partial(group_kernel, inv, sizes, start, finish)...  29 us
    ppermute x15, starting transfers between devices, moved(): return lax.ppermute(array, AXES, pairs)  22.3 us
    pallas_call x5, Pallas kernels, project(): pl.pallas_call(functools.partial(project_kernel, blocks, splits, first, c...  9.57 us
    unnamed x18, local copies, waits for them, and re-layouts  3.22 us
  transfers between devices with their start and end apart: 15, of which 9 were waited for; matrix products, arithmetic and copies ran while one was open for 2% of the time, Pallas kernels for 24%

profile of v5, /device:TPU:24, one launch (start us, length us, event | category | flops | bytes accessed | tf_op | source)
XLA Modules:
  0.0 126.3 jit_solution(1543351909682819157)
XLA Ops:
  0.0 1.7 %pack.1.refs_1_ = bf16[1040,128]{1,0:T(8,128)(2,1)} custom-call(bf16[512,128]{1,0:T(8,128)(2,1)} %bitcast.11, bf16[512,128]{1,0:T(8,128)(2,1)} %bitcast.12, bf16[2,1]{1,0:T(2,128)(2,1)} %ks_ref.1, bf16[2,1]{1,0:T(2,128)(2,1)} %vs_ref.1, s32[2]{0:T(128)} %place_ref.1), custom_call_target="tpu_custom_call" | custom-call | tf_op jit(solution)/shard_map/pack/pallas_call | solution.py:216
  1.8 1.0 constant_dynamic-update-slice_fusion.1
  3.6 2.0 %collective-permute-start.3 = (bf16[2080,128]{1,0:T(8,128)(2,1)S(1)}, bf16[2080,128]{1,0:T(8,128)(2,1)S(1)}, u32[]{:S(2)}, u32[]{:S(2)}) collective-permute-start(bf16[2080,128]{1,0:T(8,128)(2,1)S(1)} %constant_dynamic-update-slice_fusion), channel_id=1, source_target_pairs={{0,32},{1,33},{2,34},{3,35},{4,36},{5,37},{6,38},{7,39},{8,104},{9... | collective-permute-start | bytes 1597448 | tf_op jit(solution)/shard_map/ppermute | solution.py:33
  5.5 1.2 collective-permute-start.4
  6.8 0.9 copy-done
  7.7 1.2 copy-done.2
  9.0 2.2 %attend_own.1 = (f32[4096,128]{1,0:T(8,128)S(1)}, f32[4096,128]{1,0:T(8,128)S(1)}, f32[4096,128]{1,0:T(8,128)S(1)}) custom-call(bf16[4096,128]{1,0:T(8,128)(2,1)S(1)} %bitcast.5, bf16[1040,128]{1,0:T(8,128)(2,1)S(1)} %copy-done), custom_call_target="tpu_custom_call" | custom-call | flops 3221225472 | bytes 1048576 | tf_op jit(solution)/shard_map/attend_own/pallas_call | solution.py:273
  11.2 2.1 %attend_partner.1 = (f32[4096,128]{1,0:T(8,128)S(1)}, f32[4096,128]{1,0:T(8,128)S(1)}, f32[4096,128]{1,0:T(8,128)S(1)}) custom-call(bf16[4096,128]{1,0:T(8,128)(2,1)S(1)} %bitcast.6, bf16[1040,128]{1,0:T(8,128)(2,1)S(1)} %copy-done.1, bf16[1040,128]{1,0:T(8,128)(2,1)S(1)} %collective-permute-done.refs_2_, ...), custom_call_target="tpu_custom_call", output_to_operand_aliasing={{0}: (3, {}), {1}: (4, {}), {2}: (5, {})} | custom-call | flops 2147483648 | bytes 1048576 | tf_op jit(solution)/shard_map/attend_partner/pallas_call | solution.py:273
  13.3 4.9 %collective-permute-done.3.refs_2_ = bf16[2080,128]{1,0:T(8,128)(2,1)S(1)} collective-permute-done((bf16[2080,128]{1,0:T(8,128)(2,1)S(1)}, bf16[2080,128]{1,0:T(8,128)(2,1)S(1)}, u32[]{:S(2)}, u32[]{:S(2)}) %collective-permute-start.3) | collective-permute-done | bytes 532512 | tf_op jit(solution)/shard_map/ppermute | solution.py:33
  18.3 3.8 %collective-permute-start.5 = (bf16[4160,128]{1,0:T(8,128)(2,1)S(1)}, bf16[4160,128]{1,0:T(8,128)(2,1)S(1)}, u32[]{:S(2)}, u32[]{:S(2)}) collective-permute-start(bf16[4160,128]{1,0:T(8,128)(2,1)S(1)} %pad_maximum_fusion), channel_id=1, source_target_pairs={{0,8},{1,9},{2,10},{3,11},{4,12},{5,13},{6,14},{7,15},{8,0},{9,1},... | collective-permute-start | bytes 3194888 | tf_op jit(solution)/shard_map/ppermute | solution.py:33
  22.0 4.8 %collective-permute-start.2 = (bf16[1040,128]{1,0:T(8,128)(2,1)S(1)}, bf16[1040,128]{1,0:T(8,128)(2,1)S(1)}, u32[]{:S(2)}, u32[]{:S(2)}) collective-permute-start(bf16[1040,128]{1,0:T(8,128)(2,1)S(1)} %copy-done.1), channel_id=1, source_target_pairs={{0,80},{1,81},{2,82},{3,83},{4,84},{5,85},{6,86},{7,87},{8,88},{9,... | collective-permute-start | bytes 798728 | tf_op jit(solution)/shard_map/ppermute | solution.py:33
  26.9 6.5 %attend_near.1 = (f32[4096,128]{1,0:T(8,128)S(1)}, f32[4096,128]{1,0:T(8,128)S(1)}, f32[4096,128]{1,0:T(8,128)S(1)}) custom-call(bf16[4096,128]{1,0:T(8,128)(2,1)S(1)} %bitcast.7, bf16[1040,128]{1,0:T(8,128)(2,1)S(1)} %copy-done.1, bf16[2080,128]{1,0:T(8,128)(2,1)S(1)} %collective-permute-done.3.refs_2_, ...), custom_call_target="tpu_custom_call", output_to_operand_aliasing={{0}: (4, {}), {1}: (5, {}), {2}: (6, {})} | custom-call | flops 8589934592 | bytes 1048576 | tf_op jit(solution)/shard_map/attend_near/pallas_call | solution.py:273
  33.4 6.5 %attend_more.1 = (f32[4096,128]{1,0:T(8,128)S(1)}, f32[4096,128]{1,0:T(8,128)S(1)}, f32[4096,128]{1,0:T(8,128)S(1)}) custom-call(bf16[4096,128]{1,0:T(8,128)(2,1)S(1)} %bitcast.8, bf16[1040,128]{1,0:T(8,128)(2,1)S(1)} %copy-done.1, bf16[4160,128]{1,0:T(8,128)(2,1)S(1)} %collective-permute-done.5.refs_2_, ...), custom_call_target="tpu_custom_call", output_to_operand_aliasing={{0}: (3, {}), {1}: (4, {}), {2}: (5, {})} | custom-call | flops 8589934592 | bytes 1048576 | tf_op jit(solution)/shard_map/attend_more/pallas_call | solution.py:273
  39.9 3.8 %collective-permute-done.2 = bf16[1040,128]{1,0:T(8,128)(2,1)S(1)} collective-permute-done((bf16[1040,128]{1,0:T(8,128)(2,1)S(1)}, bf16[1040,128]{1,0:T(8,128)(2,1)S(1)}, u32[]{:S(2)}, u32[]{:S(2)}) %collective-permute-start.2) | collective-permute-done | bytes 266272 | tf_op jit(solution)/shard_map/ppermute | solution.py:33
  44.1 5.2 %attend_last.1 = (f32[4096,128]{1,0:T(8,128)S(1)}, f32[4096,128]{1,0:T(8,128)S(1)}, f32[4096,128]{1,0:T(8,128)S(1)}) custom-call(bf16[4096,128]{1,0:T(8,128)(2,1)S(1)} %bitcast.9, bf16[1040,128]{1,0:T(8,128)(2,1)S(1)} %copy-done.1, ...), custom_call_target="tpu_custom_call", output_to_operand_aliasing={{0}: (3, {}), {1}: (4, {}), {2}: (5, {})} | custom-call | flops 6442450944 | bytes 1048576 | tf_op jit(solution)/shard_map/attend_last/pallas_call | solution.py:273
  49.4 6.4 %attend_rest.1 = (bf16[512,1024]{1,0:T(8,128)(2,1)S(1)}, f32[4096,128]{1,0:T(8,128)S(1)}, f32[4096,128]{1,0:T(8,128)S(1)}, f32[4096,128]{1,0:T(8,128)S(1)}) custom-call(bf16[4096,128]{1,0:T(8,128)(2,1)S(1)} %bitcast.10, bf16[1040,128]{1,0:T(8,128)(2,1)S(1)} %copy-done.1, ...), custom_call_target="tpu_custom_call", output_to_operand_aliasing={{1}: (4, {}), {2}: (5, {}), {3}: (6, {})} | custom-call | flops 6442450944 | bytes 1048576 | tf_op jit(solution)/shard_map/attend_rest/pallas_call | solution.py:273
  55.9 1.5 %project_far.1 = bf16[128,4864]{1,0:T(8,128)(2,1)S(1)} custom-call(bf16[512,1024]{1,0:T(8,128)(2,1)S(1)} %get-tuple-element.86.a_ref, bf16[1024,8192]{1,0:T(8,128)(2,1)S(1)} %bitcast.4), custom_call_target="tpu_custom_call" | custom-call | flops 1275068416 | bytes 9961472 | tf_op jit(solution)/shard_map/project_far/pallas_call | solution.py:308
  57.3 1.6 %collective-permute-start.8 = (bf16[128,4864]{1,0:T(8,128)(2,1)S(1)}, bf16[128,4864]{1,0:T(8,128)(2,1)S(1)}, u32[]{:S(2)}, u32[]{:S(2)}) collective-permute-start(bf16[128,4864]{1,0:T(8,128)(2,1)S(1)} %project_far.1), channel_id=1, source_target_pairs={{0,1},{1,2},{2,3},{3,0},{4,5},{5,6},{6,7},{7,4},{8,11},{9,8},{10,9... | collective-permute-start | bytes 3735560 | tf_op jit(solution)/shard_map/ppermute | solution.py:33
  58.9 1.9 %project_y.1 = bf16[256,3328]{1,0:T(8,128)(2,1)S(1)} custom-call(bf16[512,1024]{1,0:T(8,128)(2,1)S(1)} %get-tuple-element.86.a_ref, bf16[1024,8192]{1,0:T(8,128)(2,1)S(1)} %bitcast.4), custom_call_target="tpu_custom_call" | custom-call | flops 1744830464 | bytes 6815744 | tf_op jit(solution)/shard_map/project_y/pallas_call | solution.py:308
  60.8 1.1 collective-permute-start.11
  61.9 2.7 %project_c.1 = (bf16[128,4864]{1,0:T(8,128)(2,1)S(1)}, bf16[128,4864]{1,0:T(8,128)(2,1)S(1)}) custom-call(bf16[512,1024]{1,0:T(8,128)(2,1)S(1)} %get-tuple-element.86.a_ref, bf16[1024,8192]{1,0:T(8,128)(2,1)S(1)} %bitcast.4), custom_call_target="tpu_custom_call" | custom-call | flops 2550136832 | bytes 9961472 | tf_op jit(solution)/shard_map/project_c/pallas_call | solution.py:308
  64.7 1.5 %project_behind.1 = bf16[128,4864]{1,0:T(8,128)(2,1)S(1)} custom-call(bf16[512,1024]{1,0:T(8,128)(2,1)S(1)} %get-tuple-element.86.a_ref, bf16[1024,8192]{1,0:T(8,128)(2,1)S(1)} %bitcast.4), custom_call_target="tpu_custom_call" | custom-call | flops 1275068416 | bytes 9961472 | tf_op jit(solution)/shard_map/project_behind/pallas_call | solution.py:308
  66.2 1.8 %collective-permute-start.7 = (bf16[128,4864]{1,0:T(8,128)(2,1)S(1)}, bf16[128,4864]{1,0:T(8,128)(2,1)S(1)}, u32[]{:S(2)}, u32[]{:S(2)}) collective-permute-start(bf16[128,4864]{1,0:T(8,128)(2,1)S(1)} %project_behind.1), channel_id=1, source_target_pairs={{0,3},{1,0},{2,1},{3,2},{4,7},{5,4},{6,5},{7,6},{8,9},{9,10},{10,1... | collective-permute-start | bytes 3735560 | tf_op jit(solution)/shard_map/ppermute | solution.py:33
  68.0 12.1 %collective-permute-done.8 = bf16[128,4864]{1,0:T(8,128)(2,1)S(1)} collective-permute-done((bf16[128,4864]{1,0:T(8,128)(2,1)S(1)}, bf16[128,4864]{1,0:T(8,128)(2,1)S(1)}, u32[]{:S(2)}, u32[]{:S(2)}) %collective-permute-start.8) | collective-permute-done | bytes 1245216 | tf_op jit(solution)/shard_map/ppermute | solution.py:33
  80.4 1.6 %collective-permute-start.9 = (bf16[128,4864]{1,0:T(8,128)(2,1)S(1)}, bf16[128,4864]{1,0:T(8,128)(2,1)S(1)}, u32[]{:S(2)}, u32[]{:S(2)}) collective-permute-start(bf16[128,4864]{1,0:T(8,128)(2,1)S(1)} %add_convert_fusion), channel_id=1, source_target_pairs={{0,1},{1,2},{2,3},{3,0},{4,5},{5,6},{6,7},{7,4},{8,11},{9,8},{10,9... | collective-permute-start | bytes 3735560 | tf_op jit(solution)/shard_map/ppermute | solution.py:33
  82.0 1.9 %project_d.1 = bf16[256,3328]{1,0:T(8,128)(2,1)S(1)} custom-call(bf16[512,1024]{1,0:T(8,128)(2,1)S(1)} %get-tuple-element.86.a_ref, bf16[1024,8192]{1,0:T(8,128)(2,1)S(1)} %bitcast.4), custom_call_target="tpu_custom_call" | custom-call | flops 1744830464 | bytes 6815744 | tf_op jit(solution)/shard_map/project_d/pallas_call | solution.py:308
  83.9 17.2 %collective-permute-done.11 = bf16[256,3328]{1,0:T(8,128)(2,1)S(1)} collective-permute-done((bf16[256,3328]{1,0:T(8,128)(2,1)S(1)}, bf16[256,3328]{1,0:T(8,128)(2,1)S(1)}, u32[]{:S(2)}, u32[]{:S(2)}) %collective-permute-start.11) | collective-permute-done | bytes 1703968 | tf_op jit(solution)/shard_map/ppermute | solution.py:33
  103.5 2.9 %collective-permute-start.12 = (bf16[64,3328]{1,0:T(8,128)(2,1)S(1)}, bf16[64,3328]{1,0:T(8,128)(2,1)S(1)}, u32[]{:S(2)}, u32[]{:S(2)}) collective-permute-start(bf16[64,3328]{1,0:T(8,128)(2,1)S(1)} %get-tuple-element.87), channel_id=1, source_target_pairs={{0,3},{1,0},{2,1},{3,2},{4,7},{5,4},{6,5},{7,6},{8,9},{9,10},{10,1... | collective-permute-start | bytes 1277960 | tf_op jit(solution)/shard_map/ppermute | solution.py:33
  106.5 9.0 %collective-permute-done.13 = bf16[64,3328]{1,0:T(8,128)(2,1)S(1)} collective-permute-done((bf16[64,3328]{1,0:T(8,128)(2,1)S(1)}, bf16[64,3328]{1,0:T(8,128)(2,1)S(1)}, u32[]{:S(2)}, u32[]{:S(2)}) %collective-permute-start.13) | collective-permute-done | bytes 426016 | tf_op jit(solution)/shard_map/ppermute | solution.py:33
  115.7 3.8 %collective-permute-done.10 = bf16[64,4864]{1,0:T(8,128)(2,1)S(1)} collective-permute-done((bf16[64,4864]{1,0:T(8,128)(2,1)S(1)}, bf16[64,4864]{1,0:T(8,128)(2,1)S(1)}, u32[]{:S(2)}, u32[]{:S(2)}) %collective-permute-start.10) | collective-permute-done | bytes 622624 | tf_op jit(solution)/shard_map/ppermute | solution.py:33
  119.9 5.2 %collective-permute-done.14 = bf16[64,3328]{1,0:T(8,128)(2,1)S(1)} collective-permute-done((bf16[64,3328]{1,0:T(8,128)(2,1)S(1)}, bf16[64,3328]{1,0:T(8,128)(2,1)S(1)}, u32[]{:S(2)}, u32[]{:S(2)}) %collective-permute-start.14) | collective-permute-done | bytes 426016 | tf_op jit(solution)/shard_map/ppermute | solution.py:33
  125.3 1.0 pad_maximum_fusion.1
  (40 shorter events, 4.8 us)
Async XLA Ops:
  1.8 1.8 %collective-permute-start = (bf16[1040,128]{1,0:T(8,128)(2,1)}, bf16[1040,128]{1,0:T(8,128)(2,1)S(1)}, u32[]{:S(2)}, u32[]{:S(2)}) collective-permute-start(bf16[1040,128]{1,0:T(8,128)(2,1)} %pack.1.refs_1_), channel_id=1, source_target_pairs={{0,8},{1,9},{2,10},{3,11},{4,12},{5,13},{6,14},{7,15},{8,0},{9,1},... | collective-permute-start | bytes 798728 | tf_op jit(solution)/shard_map/ppermute | solution.py:33
  3.6 14.7 %collective-permute-start.3 = (bf16[2080,128]{1,0:T(8,128)(2,1)S(1)}, bf16[2080,128]{1,0:T(8,128)(2,1)S(1)}, u32[]{:S(2)}, u32[]{:S(2)}) collective-permute-start(bf16[2080,128]{1,0:T(8,128)(2,1)S(1)} %constant_dynamic-update-slice_fusion), channel_id=1, source_target_pairs={{0,32},{1,33},{2,34},{3,35},{4,36},{5,37},{6,38},{7,39},{8,104},{9... | collective-permute-start | bytes 1597448 | tf_op jit(solution)/shard_map/ppermute | solution.py:33
  5.5 12.7 %collective-permute-start.4 = (bf16[2080,128]{1,0:T(8,128)(2,1)S(1)}, bf16[2080,128]{1,0:T(8,128)(2,1)S(1)}, u32[]{:S(2)}, u32[]{:S(2)}) collective-permute-start(bf16[2080,128]{1,0:T(8,128)(2,1)S(1)} %constant_dynamic-update-slice_fusion), channel_id=1, source_target_pairs={{0,16},{1,17},{2,18},{3,19},{4,20},{5,21},{6,22},{7,23},{8,72},{9,... | collective-permute-start | bytes 1597448 | tf_op jit(solution)/shard_map/ppermute | solution.py:33
  6.8 1.0 copy-start
  7.7 1.2 copy-start.2
  9.0 2.2 %copy-start.1 = (bf16[1040,128]{1,0:T(8,128)(2,1)S(1)}, bf16[1040,128]{1,0:T(8,128)(2,1)}, u32[]{:S(2)}) copy-start(bf16[1040,128]{1,0:T(8,128)(2,1)} %pack.1.refs_1_) | copy-start | bytes 798724
  18.3 15.1 %collective-permute-start.5 = (bf16[4160,128]{1,0:T(8,128)(2,1)S(1)}, bf16[4160,128]{1,0:T(8,128)(2,1)S(1)}, u32[]{:S(2)}, u32[]{:S(2)}) collective-permute-start(bf16[4160,128]{1,0:T(8,128)(2,1)S(1)} %pad_maximum_fusion), channel_id=1, source_target_pairs={{0,8},{1,9},{2,10},{3,11},{4,12},{5,13},{6,14},{7,15},{8,0},{9,1},... | collective-permute-start | bytes 3194888 | tf_op jit(solution)/shard_map/ppermute | solution.py:33
  22.0 21.6 %collective-permute-start.1 = (bf16[2080,128]{1,0:T(8,128)(2,1)S(1)}, bf16[2080,128]{1,0:T(8,128)(2,1)S(1)}, u32[]{:S(2)}, u32[]{:S(2)}) collective-permute-start(bf16[2080,128]{1,0:T(8,128)(2,1)S(1)} %constant_dynamic-update-slice_fusion), channel_id=1, source_target_pairs={{0,48},{1,49},{2,50},{3,51},{4,52},{5,53},{6,54},{7,55},{8,120},{9... | collective-permute-start | bytes 1597448 | tf_op jit(solution)/shard_map/ppermute | solution.py:33
  22.0 21.6 %collective-permute-start.2 = (bf16[1040,128]{1,0:T(8,128)(2,1)S(1)}, bf16[1040,128]{1,0:T(8,128)(2,1)S(1)}, u32[]{:S(2)}, u32[]{:S(2)}) collective-permute-start(bf16[1040,128]{1,0:T(8,128)(2,1)S(1)} %copy-done.1), channel_id=1, source_target_pairs={{0,80},{1,81},{2,82},{3,83},{4,84},{5,85},{6,86},{7,87},{8,88},{9,... | collective-permute-start | bytes 798728 | tf_op jit(solution)/shard_map/ppermute | solution.py:33
  33.4 10.7 %copy-start.3 = (bf16[512,8,128]{2,1,0:T(8,128)(2,1)S(1)}, bf16[512,8,128]{2,1,0:T(8,128)(2,1)}, u32[]{:S(2)}) copy-start(bf16[512,8,128]{2,1,0:T(8,128)(2,1)} %param.7) | copy-start | bytes 3145732
  43.8 5.6 %collective-permute-start.6 = (bf16[3120,128]{1,0:T(8,128)(2,1)S(1)}, bf16[3120,128]{1,0:T(8,128)(2,1)S(1)}, u32[]{:S(2)}, u32[]{:S(2)}) collective-permute-start(bf16[3120,128]{1,0:T(8,128)(2,1)S(1)} %constant_dynamic-update-slice_fusion.2.refs_2_), channel_id=1, source_target_pairs={{0,8},{1,9},{2,10},{3,11},{4,12},{5,13},{6,14},{7,15},{8,0},{9,1},... | collective-permute-start | bytes 2396168 | tf_op jit(solution)/shard_map/ppermute | solution.py:33
  44.1 11.7 %slice-start = ((s8[16777216]{0:T(1024)(128)(4,1)}), s8[4194304]{0:T(1024)(128)(4,1)S(1)}, s32[]{:S(2)}) async-start(s8[16777216]{0:T(1024)(128)(4,1)} %bitcast.3), calls=%async_computation | async-start | bytes 8388608
  44.1 11.7 %slice-start.1 = ((s8[16777216]{0:T(1024)(128)(4,1)}), s8[4194304]{0:T(1024)(128)(4,1)S(1)}, s32[]{:S(2)}) async-start(s8[16777216]{0:T(1024)(128)(4,1)} %bitcast.3), calls=%async_computation.1 | async-start | bytes 8388608
  49.4 6.5 %slice-start.2 = ((s8[16777216]{0:T(1024)(128)(4,1)}), s8[4194304]{0:T(1024)(128)(4,1)S(1)}, s32[]{:S(2)}) async-start(s8[16777216]{0:T(1024)(128)(4,1)} %bitcast.3), calls=%async_computation.2 | async-start | bytes 8388608
  49.4 6.5 %slice-start.3 = ((s8[16777216]{0:T(1024)(128)(4,1)}), s8[4194304]{0:T(1024)(128)(4,1)S(1)}, s32[]{:S(2)}) async-start(s8[16777216]{0:T(1024)(128)(4,1)} %bitcast.3), calls=%async_computation.3 | async-start | bytes 8388608
  57.3 22.8 %collective-permute-start.8 = (bf16[128,4864]{1,0:T(8,128)(2,1)S(1)}, bf16[128,4864]{1,0:T(8,128)(2,1)S(1)}, u32[]{:S(2)}, u32[]{:S(2)}) collective-permute-start(bf16[128,4864]{1,0:T(8,128)(2,1)S(1)} %project_far.1), channel_id=1, source_target_pairs={{0,1},{1,2},{2,3},{3,0},{4,5},{5,6},{6,7},{7,4},{8,11},{9,8},{10,9... | collective-permute-start | bytes 3735560 | tf_op jit(solution)/shard_map/ppermute | solution.py:33
  60.8 40.3 %collective-permute-start.11 = (bf16[256,3328]{1,0:T(8,128)(2,1)S(1)}, bf16[256,3328]{1,0:T(8,128)(2,1)S(1)}, u32[]{:S(2)}, u32[]{:S(2)}) collective-permute-start(bf16[256,3328]{1,0:T(8,128)(2,1)S(1)} %project_y.1), channel_id=1, source_target_pairs={{0,4},{1,5},{2,6},{3,7},{4,0},{5,1},{6,2},{7,3},{8,12},{9,13},{10,... | collective-permute-start | bytes 5111816 | tf_op jit(solution)/shard_map/ppermute | solution.py:33
  66.2 35.2 %collective-permute-start.7 = (bf16[128,4864]{1,0:T(8,128)(2,1)S(1)}, bf16[128,4864]{1,0:T(8,128)(2,1)S(1)}, u32[]{:S(2)}, u32[]{:S(2)}) collective-permute-start(bf16[128,4864]{1,0:T(8,128)(2,1)S(1)} %project_behind.1), channel_id=1, source_target_pairs={{0,3},{1,0},{2,1},{3,2},{4,7},{5,4},{6,5},{7,6},{8,9},{9,10},{10,1... | collective-permute-start | bytes 3735560 | tf_op jit(solution)/shard_map/ppermute | solution.py:33
  80.4 21.8 %collective-permute-start.9 = (bf16[128,4864]{1,0:T(8,128)(2,1)S(1)}, bf16[128,4864]{1,0:T(8,128)(2,1)S(1)}, u32[]{:S(2)}, u32[]{:S(2)}) collective-permute-start(bf16[128,4864]{1,0:T(8,128)(2,1)S(1)} %add_convert_fusion), channel_id=1, source_target_pairs={{0,1},{1,2},{2,3},{3,0},{4,5},{5,6},{6,7},{7,4},{8,11},{9,8},{10,9... | collective-permute-start | bytes 3735560 | tf_op jit(solution)/shard_map/ppermute | solution.py:33
  102.4 13.0 %collective-permute-start.13 = (bf16[64,3328]{1,0:T(8,128)(2,1)S(1)}, bf16[64,3328]{1,0:T(8,128)(2,1)S(1)}, u32[]{:S(2)}, u32[]{:S(2)}) collective-permute-start(bf16[64,3328]{1,0:T(8,128)(2,1)S(1)} %get-tuple-element.88), channel_id=1, source_target_pairs={{0,1},{1,2},{2,3},{3,0},{4,5},{5,6},{6,7},{7,4},{8,11},{9,8},{10,9... | collective-permute-start | bytes 1277960 | tf_op jit(solution)/shard_map/ppermute | solution.py:33
  102.8 16.7 %collective-permute-start.10 = (bf16[64,4864]{1,0:T(8,128)(2,1)S(1)}, bf16[64,4864]{1,0:T(8,128)(2,1)S(1)}, u32[]{:S(2)}, u32[]{:S(2)}) collective-permute-start(bf16[64,4864]{1,0:T(8,128)(2,1)S(1)} %add_convert_fusion.2), channel_id=1, source_target_pairs={{0,4},{1,5},{2,6},{3,7},{4,0},{5,1},{6,2},{7,3},{8,12},{9,13},{10,... | collective-permute-start | bytes 1867784 | tf_op jit(solution)/shard_map/ppermute | solution.py:33
  103.5 16.3 %collective-permute-start.12 = (bf16[64,3328]{1,0:T(8,128)(2,1)S(1)}, bf16[64,3328]{1,0:T(8,128)(2,1)S(1)}, u32[]{:S(2)}, u32[]{:S(2)}) collective-permute-start(bf16[64,3328]{1,0:T(8,128)(2,1)S(1)} %get-tuple-element.87), channel_id=1, source_target_pairs={{0,3},{1,0},{2,1},{3,2},{4,7},{5,4},{6,5},{7,6},{8,9},{9,10},{10,1... | collective-permute-start | bytes 1277960 | tf_op jit(solution)/shard_map/ppermute | solution.py:33
  115.6 9.4 %collective-permute-start.14 = (bf16[64,3328]{1,0:T(8,128)(2,1)S(1)}, bf16[64,3328]{1,0:T(8,128)(2,1)S(1)}, u32[]{:S(2)}, u32[]{:S(2)}) collective-permute-start(bf16[64,3328]{1,0:T(8,128)(2,1)S(1)} %add_convert_fusion.4), channel_id=1, source_target_pairs={{0,1},{1,2},{2,3},{3,0},{4,5},{5,6},{6,7},{7,4},{8,11},{9,8},{10,9... | collective-permute-start | bytes 1277960 | tf_op jit(solution)/shard_map/ppermute | solution.py:33

commit v6 on v5

--- a/solution.py
+++ b/solution.py
@@ -327,6 +327,15 @@
     return total
 
 
+def finish_kernel(cut, xo_ref, xf_ref, xb_ref, xl_ref, yo_ref, yy_ref, yf_ref, yb_ref, o_ref):
+    o_ref[:, :cut] = added(xo_ref[0:64, :], xf_ref[0:64, :], xb_ref[0:64, :], xl_ref[...]).astype(
+        BF16
+    )
+    o_ref[:, cut:] = added(yo_ref[192:256, :], yy_ref[192:256, :], yf_ref[...], yb_ref[...]).astype(
+        BF16
+    )
+
+
 def scattered(att, weight, first_columns):
     rest = weight.shape[1] - first_columns
     (x_far,) = project(att, weight, (0, 1), (2,), 0, first_columns, "project_far")
@@ -341,8 +350,8 @@
     att, x_behind = lax.optimization_barrier((att, x_behind))
     (y_own,) = project(att, weight, (0, 2, 4, 6), (4,), first_columns, rest, "project_d")
     got_back = moved(added(x_ahead, got_far).astype(BF16), ahead)
-    y_far, y_ahead, y_behind, y_mine = [
-        (y_own[i * 64 : (i + 1) * 64], got_y[i * 64 : (i + 1) * 64]) for i in range(4)
+    y_far, y_ahead, y_behind = [
+        (y_own[i * 64 : (i + 1) * 64], got_y[i * 64 : (i + 1) * 64]) for i in range(3)
     ]
     x_out = added(x_own[64:], got_front[64:], got_back[64:]).astype(BF16)
     x_last = moved(x_out, beside)
@@ -352,13 +361,15 @@
     y_got_far = moved(y_far_sum, ahead)
     y_got_front = moved(y_behind_sum, behind)
     y_got_back = moved(added(*y_ahead, y_got_far).astype(BF16), ahead)
-    return jnp.concatenate(
-        [
-            added(x_own[:64], got_front[:64], got_back[:64], x_last).astype(BF16),
-            added(*y_mine, y_got_front, y_got_back).astype(BF16),
-        ],
-        axis=1,
-    )
+    vmem = pl.BlockSpec(memory_space=pltpu.VMEM)
+    return pl.pallas_call(
+        functools.partial(finish_kernel, first_columns),
+        out_shape=jax.ShapeDtypeStruct((64, first_columns + rest), BF16),
+        in_specs=[vmem] * 8,
+        out_specs=vmem,
+        compiler_params=pltpu.CompilerParams(vmem_limit_bytes=LIMIT),
+        name="finish",
+    )(x_own, got_front, got_back, x_last, y_own, got_y, y_got_front, y_got_back)
 
 
 def body(query, keys, values, k_scale, v_scale, block_place, out_weight):

time: 126 us -> 128 us (1.016)
  Pallas kernels: 40.3 us -> 43 us
  other arithmetic: 2.53 us -> 0.94 us
    pallas_call x0 -> x1, Pallas kernels: none -> 1.48 us  [scattered(): pl.pallas_call(functools.partial(finish_kernel, first_columns), out_shape...]
  transfers between devices with their start and end apart: 15 -> 15, of which waited for: 9 -> 9; matrix products, arithmetic and copies ran while one was open for 2% -> 1% of each run, Pallas kernels for 24% -> 25%
where the time goes in v6:
time: 128 us; the launch traced here: 127 us
  waiting for transfers between devices  57.5 us (45%)
  Pallas kernels  43 us (34%)
  starting transfers between devices  22.3 us (17%)
  local copies, waits for them, and re-layouts  3.29 us (3%)
    ppermute x15, waiting for transfers between devices, moved(): return lax.ppermute(array, AXES, pairs)  57.5 us
    pallas_call x6, Pallas kernels, attend(): pl.pallas_call(functools.partial(group_kernel, inv, sizes, start, finish)...  30.2 us
    ppermute x15, starting transfers between devices, moved(): return lax.ppermute(array, AXES, pairs)  22.3 us
    pallas_call x5, Pallas kernels, project(): pl.pallas_call(functools.partial(project_kernel, blocks, splits, first, c...  9.57 us
    unnamed x18, local copies, waits for them, and re-layouts  3.22 us
  transfers between devices with their start and end apart: 15, of which 9 were waited for; matrix products, arithmetic and copies ran while one was open for 1% of the time, Pallas kernels for 25%

profile of v6, /device:TPU:24, one launch (start us, length us, event | category | flops | bytes accessed | tf_op | source)
XLA Modules:
  0.0 127.3 jit_solution(7909841515723539863)
XLA Ops:
  0.0 1.7 %pack.1.refs_1_ = bf16[1040,128]{1,0:T(8,128)(2,1)} custom-call(bf16[512,128]{1,0:T(8,128)(2,1)} %bitcast.11, bf16[512,128]{1,0:T(8,128)(2,1)} %bitcast.12, bf16[2,1]{1,0:T(2,128)(2,1)} %ks_ref.1, bf16[2,1]{1,0:T(2,128)(2,1)} %vs_ref.1, s32[2]{0:T(128)} %place_ref.1), custom_call_target="tpu_custom_call" | custom-call | tf_op jit(solution)/shard_map/pack/pallas_call | solution.py:216
  1.8 1.0 constant_dynamic-update-slice_fusion.1
  3.6 2.0 %collective-permute-start.3 = (bf16[2080,128]{1,0:T(8,128)(2,1)S(1)}, bf16[2080,128]{1,0:T(8,128)(2,1)S(1)}, u32[]{:S(2)}, u32[]{:S(2)}) collective-permute-start(bf16[2080,128]{1,0:T(8,128)(2,1)S(1)} %constant_dynamic-update-slice_fusion), channel_id=1, source_target_pairs={{0,32},{1,33},{2,34},{3,35},{4,36},{5,37},{6,38},{7,39},{8,104},{9... | collective-permute-start | bytes 1597448 | tf_op jit(solution)/shard_map/ppermute | solution.py:33
  5.5 1.2 collective-permute-start.4
  6.8 0.9 copy-done
  7.7 1.2 copy-done.2
  9.0 2.2 %attend_own.1 = (f32[4096,128]{1,0:T(8,128)S(1)}, f32[4096,128]{1,0:T(8,128)S(1)}, f32[4096,128]{1,0:T(8,128)S(1)}) custom-call(bf16[4096,128]{1,0:T(8,128)(2,1)S(1)} %bitcast.5, bf16[1040,128]{1,0:T(8,128)(2,1)S(1)} %copy-done), custom_call_target="tpu_custom_call" | custom-call | flops 3221225472 | bytes 1048576 | tf_op jit(solution)/shard_map/attend_own/pallas_call | solution.py:273
  11.2 2.2 %attend_partner.1 = (f32[4096,128]{1,0:T(8,128)S(1)}, f32[4096,128]{1,0:T(8,128)S(1)}, f32[4096,128]{1,0:T(8,128)S(1)}) custom-call(bf16[4096,128]{1,0:T(8,128)(2,1)S(1)} %bitcast.6, bf16[1040,128]{1,0:T(8,128)(2,1)S(1)} %copy-done.1, bf16[1040,128]{1,0:T(8,128)(2,1)S(1)} %collective-permute-done.refs_2_, ...), custom_call_target="tpu_custom_call", output_to_operand_aliasing={{0}: (3, {}), {1}: (4, {}), {2}: (5, {})} | custom-call | flops 2147483648 | bytes 1048576 | tf_op jit(solution)/shard_map/attend_partner/pallas_call | solution.py:273
  13.4 4.8 %collective-permute-done.3.refs_2_ = bf16[2080,128]{1,0:T(8,128)(2,1)S(1)} collective-permute-done((bf16[2080,128]{1,0:T(8,128)(2,1)S(1)}, bf16[2080,128]{1,0:T(8,128)(2,1)S(1)}, u32[]{:S(2)}, u32[]{:S(2)}) %collective-permute-start.3) | collective-permute-done | bytes 532512 | tf_op jit(solution)/shard_map/ppermute | solution.py:33
  18.3 3.8 %collective-permute-start.5 = (bf16[4160,128]{1,0:T(8,128)(2,1)S(1)}, bf16[4160,128]{1,0:T(8,128)(2,1)S(1)}, u32[]{:S(2)}, u32[]{:S(2)}) collective-permute-start(bf16[4160,128]{1,0:T(8,128)(2,1)S(1)} %pad_maximum_fusion), channel_id=1, source_target_pairs={{0,8},{1,9},{2,10},{3,11},{4,12},{5,13},{6,14},{7,15},{8,0},{9,1},... | collective-permute-start | bytes 3194888 | tf_op jit(solution)/shard_map/ppermute | solution.py:33
  22.0 4.8 %collective-permute-start.2 = (bf16[1040,128]{1,0:T(8,128)(2,1)S(1)}, bf16[1040,128]{1,0:T(8,128)(2,1)S(1)}, u32[]{:S(2)}, u32[]{:S(2)}) collective-permute-start(bf16[1040,128]{1,0:T(8,128)(2,1)S(1)} %copy-done.1), channel_id=1, source_target_pairs={{0,80},{1,81},{2,82},{3,83},{4,84},{5,85},{6,86},{7,87},{8,88},{9,... | collective-permute-start | bytes 798728 | tf_op jit(solution)/shard_map/ppermute | solution.py:33
  26.9 6.7 %attend_near.1 = (f32[4096,128]{1,0:T(8,128)S(1)}, f32[4096,128]{1,0:T(8,128)S(1)}, f32[4096,128]{1,0:T(8,128)S(1)}) custom-call(bf16[4096,128]{1,0:T(8,128)(2,1)S(1)} %bitcast.7, bf16[1040,128]{1,0:T(8,128)(2,1)S(1)} %copy-done.1, bf16[2080,128]{1,0:T(8,128)(2,1)S(1)} %collective-permute-done.3.refs_2_, ...), custom_call_target="tpu_custom_call", output_to_operand_aliasing={{0}: (4, {}), {1}: (5, {}), {2}: (6, {})} | custom-call | flops 8589934592 | bytes 1048576 | tf_op jit(solution)/shard_map/attend_near/pallas_call | solution.py:273
  33.6 6.7 %attend_more.1 = (f32[4096,128]{1,0:T(8,128)S(1)}, f32[4096,128]{1,0:T(8,128)S(1)}, f32[4096,128]{1,0:T(8,128)S(1)}) custom-call(bf16[4096,128]{1,0:T(8,128)(2,1)S(1)} %bitcast.8, bf16[1040,128]{1,0:T(8,128)(2,1)S(1)} %copy-done.1, bf16[4160,128]{1,0:T(8,128)(2,1)S(1)} %collective-permute-done.5.refs_2_, ...), custom_call_target="tpu_custom_call", output_to_operand_aliasing={{0}: (3, {}), {1}: (4, {}), {2}: (5, {})} | custom-call | flops 8589934592 | bytes 1048576 | tf_op jit(solution)/shard_map/attend_more/pallas_call | solution.py:273
  40.4 3.3 %collective-permute-done.2 = bf16[1040,128]{1,0:T(8,128)(2,1)S(1)} collective-permute-done((bf16[1040,128]{1,0:T(8,128)(2,1)S(1)}, bf16[1040,128]{1,0:T(8,128)(2,1)S(1)}, u32[]{:S(2)}, u32[]{:S(2)}) %collective-permute-start.2) | collective-permute-done | bytes 266272 | tf_op jit(solution)/shard_map/ppermute | solution.py:33
  44.1 5.6 %attend_last.1 = (f32[4096,128]{1,0:T(8,128)S(1)}, f32[4096,128]{1,0:T(8,128)S(1)}, f32[4096,128]{1,0:T(8,128)S(1)}) custom-call(bf16[4096,128]{1,0:T(8,128)(2,1)S(1)} %bitcast.9, bf16[1040,128]{1,0:T(8,128)(2,1)S(1)} %copy-done.1, ...), custom_call_target="tpu_custom_call", output_to_operand_aliasing={{0}: (3, {}), {1}: (4, {}), {2}: (5, {})} | custom-call | flops 6442450944 | bytes 1048576 | tf_op jit(solution)/shard_map/attend_last/pallas_call | solution.py:273
  49.7 6.8 %attend_rest.1 = (bf16[512,1024]{1,0:T(8,128)(2,1)S(1)}, f32[4096,128]{1,0:T(8,128)S(1)}, f32[4096,128]{1,0:T(8,128)S(1)}, f32[4096,128]{1,0:T(8,128)S(1)}) custom-call(bf16[4096,128]{1,0:T(8,128)(2,1)S(1)} %bitcast.10, bf16[1040,128]{1,0:T(8,128)(2,1)S(1)} %copy-done.1, ...), custom_call_target="tpu_custom_call", output_to_operand_aliasing={{1}: (4, {}), {2}: (5, {}), {3}: (6, {})} | custom-call | flops 6442450944 | bytes 1048576 | tf_op jit(solution)/shard_map/attend_rest/pallas_call | solution.py:273
  56.5 1.5 %project_far.1 = bf16[128,4864]{1,0:T(8,128)(2,1)S(1)} custom-call(bf16[512,1024]{1,0:T(8,128)(2,1)S(1)} %get-tuple-element.86.a_ref, bf16[1024,8192]{1,0:T(8,128)(2,1)S(1)} %bitcast.4), custom_call_target="tpu_custom_call" | custom-call | flops 1275068416 | bytes 9961472 | tf_op jit(solution)/shard_map/project_far/pallas_call | solution.py:308
  58.0 1.6 %collective-permute-start.8 = (bf16[128,4864]{1,0:T(8,128)(2,1)S(1)}, bf16[128,4864]{1,0:T(8,128)(2,1)S(1)}, u32[]{:S(2)}, u32[]{:S(2)}) collective-permute-start(bf16[128,4864]{1,0:T(8,128)(2,1)S(1)} %project_far.1), channel_id=1, source_target_pairs={{0,1},{1,2},{2,3},{3,0},{4,5},{5,6},{6,7},{7,4},{8,11},{9,8},{10,9... | collective-permute-start | bytes 3735560 | tf_op jit(solution)/shard_map/ppermute | solution.py:33
  59.6 1.9 %project_y.1 = bf16[256,3328]{1,0:T(8,128)(2,1)S(1)} custom-call(bf16[512,1024]{1,0:T(8,128)(2,1)S(1)} %get-tuple-element.86.a_ref, bf16[1024,8192]{1,0:T(8,128)(2,1)S(1)} %bitcast.4), custom_call_target="tpu_custom_call" | custom-call | flops 1744830464 | bytes 6815744 | tf_op jit(solution)/shard_map/project_y/pallas_call | solution.py:308
  61.5 1.1 collective-permute-start.11
  62.6 2.7 %project_c.1 = (bf16[128,4864]{1,0:T(8,128)(2,1)S(1)}, bf16[128,4864]{1,0:T(8,128)(2,1)S(1)}) custom-call(bf16[512,1024]{1,0:T(8,128)(2,1)S(1)} %get-tuple-element.86.a_ref, bf16[1024,8192]{1,0:T(8,128)(2,1)S(1)} %bitcast.4), custom_call_target="tpu_custom_call" | custom-call | flops 2550136832 | bytes 9961472 | tf_op jit(solution)/shard_map/project_c/pallas_call | solution.py:308
  65.3 1.5 %project_behind.1 = bf16[128,4864]{1,0:T(8,128)(2,1)S(1)} custom-call(bf16[512,1024]{1,0:T(8,128)(2,1)S(1)} %get-tuple-element.86.a_ref, bf16[1024,8192]{1,0:T(8,128)(2,1)S(1)} %bitcast.4), custom_call_target="tpu_custom_call" | custom-call | flops 1275068416 | bytes 9961472 | tf_op jit(solution)/shard_map/project_behind/pallas_call | solution.py:308
  66.8 1.8 %collective-permute-start.7 = (bf16[128,4864]{1,0:T(8,128)(2,1)S(1)}, bf16[128,4864]{1,0:T(8,128)(2,1)S(1)}, u32[]{:S(2)}, u32[]{:S(2)}) collective-permute-start(bf16[128,4864]{1,0:T(8,128)(2,1)S(1)} %project_behind.1), channel_id=1, source_target_pairs={{0,3},{1,0},{2,1},{3,2},{4,7},{5,4},{6,5},{7,6},{8,9},{9,10},{10,1... | collective-permute-start | bytes 3735560 | tf_op jit(solution)/shard_map/ppermute | solution.py:33
  68.7 12.2 %collective-permute-done.8 = bf16[128,4864]{1,0:T(8,128)(2,1)S(1)} collective-permute-done((bf16[128,4864]{1,0:T(8,128)(2,1)S(1)}, bf16[128,4864]{1,0:T(8,128)(2,1)S(1)}, u32[]{:S(2)}, u32[]{:S(2)}) %collective-permute-start.8) | collective-permute-done | bytes 1245216 | tf_op jit(solution)/shard_map/ppermute | solution.py:33
  81.2 1.6 %collective-permute-start.9 = (bf16[128,4864]{1,0:T(8,128)(2,1)S(1)}, bf16[128,4864]{1,0:T(8,128)(2,1)S(1)}, u32[]{:S(2)}, u32[]{:S(2)}) collective-permute-start(bf16[128,4864]{1,0:T(8,128)(2,1)S(1)} %add_convert_fusion), channel_id=1, source_target_pairs={{0,1},{1,2},{2,3},{3,0},{4,5},{5,6},{6,7},{7,4},{8,11},{9,8},{10,9... | collective-permute-start | bytes 3735560 | tf_op jit(solution)/shard_map/ppermute | solution.py:33
  82.7 1.9 %project_d.1.yo_ref = bf16[256,3328]{1,0:T(8,128)(2,1)S(1)} custom-call(bf16[512,1024]{1,0:T(8,128)(2,1)S(1)} %get-tuple-element.86.a_ref, bf16[1024,8192]{1,0:T(8,128)(2,1)S(1)} %bitcast.4), custom_call_target="tpu_custom_call" | custom-call | flops 1744830464 | bytes 6815744 | tf_op jit(solution)/shard_map/project_d/pallas_call | solution.py:308
  84.7 17.2 %collective-permute-done.11.yy_ref = bf16[256,3328]{1,0:T(8,128)(2,1)S(1)} collective-permute-done((bf16[256,3328]{1,0:T(8,128)(2,1)S(1)}, bf16[256,3328]{1,0:T(8,128)(2,1)S(1)}, u32[]{:S(2)}, u32[]{:S(2)}) %collective-permute-start.11) | collective-permute-done | bytes 1703968 | tf_op jit(solution)/shard_map/ppermute | solution.py:33
  104.2 3.0 %collective-permute-start.12 = (bf16[64,3328]{1,0:T(8,128)(2,1)S(1)}, bf16[64,3328]{1,0:T(8,128)(2,1)S(1)}, u32[]{:S(2)}, u32[]{:S(2)}) collective-permute-start(bf16[64,3328]{1,0:T(8,128)(2,1)S(1)} %get-tuple-element.87), channel_id=1, source_target_pairs={{0,3},{1,0},{2,1},{3,2},{4,7},{5,4},{6,5},{7,6},{8,9},{9,10},{10,1... | collective-permute-start | bytes 1277960 | tf_op jit(solution)/shard_map/ppermute | solution.py:33
  107.2 9.1 %collective-permute-done.13 = bf16[64,3328]{1,0:T(8,128)(2,1)S(1)} collective-permute-done((bf16[64,3328]{1,0:T(8,128)(2,1)S(1)}, bf16[64,3328]{1,0:T(8,128)(2,1)S(1)}, u32[]{:S(2)}, u32[]{:S(2)}) %collective-permute-start.13) | collective-permute-done | bytes 426016 | tf_op jit(solution)/shard_map/ppermute | solution.py:33
  116.5 3.7 %collective-permute-done.10.xl_ref = bf16[64,4864]{1,0:T(8,128)(2,1)S(1)} collective-permute-done((bf16[64,4864]{1,0:T(8,128)(2,1)S(1)}, bf16[64,4864]{1,0:T(8,128)(2,1)S(1)}, u32[]{:S(2)}, u32[]{:S(2)}) %collective-permute-start.10) | collective-permute-done | bytes 622624 | tf_op jit(solution)/shard_map/ppermute | solution.py:33
  120.2 5.6 %collective-permute-done.14.yb_ref = bf16[64,3328]{1,0:T(8,128)(2,1)S(1)} collective-permute-done((bf16[64,3328]{1,0:T(8,128)(2,1)S(1)}, bf16[64,3328]{1,0:T(8,128)(2,1)S(1)}, u32[]{:S(2)}, u32[]{:S(2)}) %collective-permute-start.14) | collective-permute-done | bytes 426016 | tf_op jit(solution)/shard_map/ppermute | solution.py:33
  125.8 1.5 %finish.1 = bf16[64,8192]{1,0:T(8,128)(2,1)} custom-call(bf16[128,4864]{1,0:T(8,128)(2,1)S(1)} %get-tuple-element.83.xo_ref, bf16[128,4864]{1,0:T(8,128)(2,1)S(1)} %collective-permute-done.7.xf_ref, bf16[128,4864]{1,0:T(8,128)(2,1)S(1)} %collective-permute-done.9.xb_ref, bf16[64,4864]{1,0:T(8,128)(2,1)S(1)} %collective-permute-done.10.xl_ref, ...), custom_call_target="tpu_custom_call" | custom-call | tf_op jit(solution)/shard_map/finish/pallas_call | solution.py:365
  (38 shorter events, 4.2 us)
Async XLA Ops:
  1.8 1.8 %collective-permute-start = (bf16[1040,128]{1,0:T(8,128)(2,1)}, bf16[1040,128]{1,0:T(8,128)(2,1)S(1)}, u32[]{:S(2)}, u32[]{:S(2)}) collective-permute-start(bf16[1040,128]{1,0:T(8,128)(2,1)} %pack.1.refs_1_), channel_id=1, source_target_pairs={{0,8},{1,9},{2,10},{3,11},{4,12},{5,13},{6,14},{7,15},{8,0},{9,1},... | collective-permute-start | bytes 798728 | tf_op jit(solution)/shard_map/ppermute | solution.py:33
  3.6 14.7 %collective-permute-start.3 = (bf16[2080,128]{1,0:T(8,128)(2,1)S(1)}, bf16[2080,128]{1,0:T(8,128)(2,1)S(1)}, u32[]{:S(2)}, u32[]{:S(2)}) collective-permute-start(bf16[2080,128]{1,0:T(8,128)(2,1)S(1)} %constant_dynamic-update-slice_fusion), channel_id=1, source_target_pairs={{0,32},{1,33},{2,34},{3,35},{4,36},{5,37},{6,38},{7,39},{8,104},{9... | collective-permute-start | bytes 1597448 | tf_op jit(solution)/shard_map/ppermute | solution.py:33
  5.5 12.7 %collective-permute-start.4 = (bf16[2080,128]{1,0:T(8,128)(2,1)S(1)}, bf16[2080,128]{1,0:T(8,128)(2,1)S(1)}, u32[]{:S(2)}, u32[]{:S(2)}) collective-permute-start(bf16[2080,128]{1,0:T(8,128)(2,1)S(1)} %constant_dynamic-update-slice_fusion), channel_id=1, source_target_pairs={{0,16},{1,17},{2,18},{3,19},{4,20},{5,21},{6,22},{7,23},{8,72},{9,... | collective-permute-start | bytes 1597448 | tf_op jit(solution)/shard_map/ppermute | solution.py:33
  6.8 1.0 copy-start
  7.7 1.2 copy-start.2
  9.0 2.2 %copy-start.1 = (bf16[1040,128]{1,0:T(8,128)(2,1)S(1)}, bf16[1040,128]{1,0:T(8,128)(2,1)}, u32[]{:S(2)}) copy-start(bf16[1040,128]{1,0:T(8,128)(2,1)} %pack.1.refs_1_) | copy-start | bytes 798724
  18.3 15.3 %collective-permute-start.5 = (bf16[4160,128]{1,0:T(8,128)(2,1)S(1)}, bf16[4160,128]{1,0:T(8,128)(2,1)S(1)}, u32[]{:S(2)}, u32[]{:S(2)}) collective-permute-start(bf16[4160,128]{1,0:T(8,128)(2,1)S(1)} %pad_maximum_fusion), channel_id=1, source_target_pairs={{0,8},{1,9},{2,10},{3,11},{4,12},{5,13},{6,14},{7,15},{8,0},{9,1},... | collective-permute-start | bytes 3194888 | tf_op jit(solution)/shard_map/ppermute | solution.py:33
  22.0 21.6 %collective-permute-start.1 = (bf16[2080,128]{1,0:T(8,128)(2,1)S(1)}, bf16[2080,128]{1,0:T(8,128)(2,1)S(1)}, u32[]{:S(2)}, u32[]{:S(2)}) collective-permute-start(bf16[2080,128]{1,0:T(8,128)(2,1)S(1)} %constant_dynamic-update-slice_fusion), channel_id=1, source_target_pairs={{0,48},{1,49},{2,50},{3,51},{4,52},{5,53},{6,54},{7,55},{8,120},{9... | collective-permute-start | bytes 1597448 | tf_op jit(solution)/shard_map/ppermute | solution.py:33
  22.0 21.6 %collective-permute-start.2 = (bf16[1040,128]{1,0:T(8,128)(2,1)S(1)}, bf16[1040,128]{1,0:T(8,128)(2,1)S(1)}, u32[]{:S(2)}, u32[]{:S(2)}) collective-permute-start(bf16[1040,128]{1,0:T(8,128)(2,1)S(1)} %copy-done.1), channel_id=1, source_target_pairs={{0,80},{1,81},{2,82},{3,83},{4,84},{5,85},{6,86},{7,87},{8,88},{9,... | collective-permute-start | bytes 798728 | tf_op jit(solution)/shard_map/ppermute | solution.py:33
  33.6 10.5 %copy-start.3 = (bf16[512,8,128]{2,1,0:T(8,128)(2,1)S(1)}, bf16[512,8,128]{2,1,0:T(8,128)(2,1)}, u32[]{:S(2)}) copy-start(bf16[512,8,128]{2,1,0:T(8,128)(2,1)} %param.7) | copy-start | bytes 3145732
  43.8 5.9 %collective-permute-start.6 = (bf16[3120,128]{1,0:T(8,128)(2,1)S(1)}, bf16[3120,128]{1,0:T(8,128)(2,1)S(1)}, u32[]{:S(2)}, u32[]{:S(2)}) collective-permute-start(bf16[3120,128]{1,0:T(8,128)(2,1)S(1)} %constant_dynamic-update-slice_fusion.2.refs_2_), channel_id=1, source_target_pairs={{0,8},{1,9},{2,10},{3,11},{4,12},{5,13},{6,14},{7,15},{8,0},{9,1},... | collective-permute-start | bytes 2396168 | tf_op jit(solution)/shard_map/ppermute | solution.py:33
  44.1 12.4 %slice-start = ((s8[16777216]{0:T(1024)(128)(4,1)}), s8[4194304]{0:T(1024)(128)(4,1)S(1)}, s32[]{:S(2)}) async-start(s8[16777216]{0:T(1024)(128)(4,1)} %bitcast.3), calls=%async_computation | async-start | bytes 8388608
  44.1 12.4 %slice-start.1 = ((s8[16777216]{0:T(1024)(128)(4,1)}), s8[4194304]{0:T(1024)(128)(4,1)S(1)}, s32[]{:S(2)}) async-start(s8[16777216]{0:T(1024)(128)(4,1)} %bitcast.3), calls=%async_computation.1 | async-start | bytes 8388608
  49.7 6.8 %slice-start.2 = ((s8[16777216]{0:T(1024)(128)(4,1)}), s8[4194304]{0:T(1024)(128)(4,1)S(1)}, s32[]{:S(2)}) async-start(s8[16777216]{0:T(1024)(128)(4,1)} %bitcast.3), calls=%async_computation.2 | async-start | bytes 8388608
  49.7 6.8 %slice-start.3 = ((s8[16777216]{0:T(1024)(128)(4,1)}), s8[4194304]{0:T(1024)(128)(4,1)S(1)}, s32[]{:S(2)}) async-start(s8[16777216]{0:T(1024)(128)(4,1)} %bitcast.3), calls=%async_computation.3 | async-start | bytes 8388608
  58.0 22.8 %collective-permute-start.8 = (bf16[128,4864]{1,0:T(8,128)(2,1)S(1)}, bf16[128,4864]{1,0:T(8,128)(2,1)S(1)}, u32[]{:S(2)}, u32[]{:S(2)}) collective-permute-start(bf16[128,4864]{1,0:T(8,128)(2,1)S(1)} %project_far.1), channel_id=1, source_target_pairs={{0,1},{1,2},{2,3},{3,0},{4,5},{5,6},{6,7},{7,4},{8,11},{9,8},{10,9... | collective-permute-start | bytes 3735560 | tf_op jit(solution)/shard_map/ppermute | solution.py:33
  61.5 40.3 %collective-permute-start.11 = (bf16[256,3328]{1,0:T(8,128)(2,1)S(1)}, bf16[256,3328]{1,0:T(8,128)(2,1)S(1)}, u32[]{:S(2)}, u32[]{:S(2)}) collective-permute-start(bf16[256,3328]{1,0:T(8,128)(2,1)S(1)} %project_y.1), channel_id=1, source_target_pairs={{0,4},{1,5},{2,6},{3,7},{4,0},{5,1},{6,2},{7,3},{8,12},{9,13},{10,... | collective-permute-start | bytes 5111816 | tf_op jit(solution)/shard_map/ppermute | solution.py:33
  66.8 35.2 %collective-permute-start.7 = (bf16[128,4864]{1,0:T(8,128)(2,1)S(1)}, bf16[128,4864]{1,0:T(8,128)(2,1)S(1)}, u32[]{:S(2)}, u32[]{:S(2)}) collective-permute-start(bf16[128,4864]{1,0:T(8,128)(2,1)S(1)} %project_behind.1), channel_id=1, source_target_pairs={{0,3},{1,0},{2,1},{3,2},{4,7},{5,4},{6,5},{7,6},{8,9},{9,10},{10,1... | collective-permute-start | bytes 3735560 | tf_op jit(solution)/shard_map/ppermute | solution.py:33
  81.2 21.7 %collective-permute-start.9 = (bf16[128,4864]{1,0:T(8,128)(2,1)S(1)}, bf16[128,4864]{1,0:T(8,128)(2,1)S(1)}, u32[]{:S(2)}, u32[]{:S(2)}) collective-permute-start(bf16[128,4864]{1,0:T(8,128)(2,1)S(1)} %add_convert_fusion), channel_id=1, source_target_pairs={{0,1},{1,2},{2,3},{3,0},{4,5},{5,6},{6,7},{7,4},{8,11},{9,8},{10,9... | collective-permute-start | bytes 3735560 | tf_op jit(solution)/shard_map/ppermute | solution.py:33
  103.1 13.1 %collective-permute-start.13 = (bf16[64,3328]{1,0:T(8,128)(2,1)S(1)}, bf16[64,3328]{1,0:T(8,128)(2,1)S(1)}, u32[]{:S(2)}, u32[]{:S(2)}) collective-permute-start(bf16[64,3328]{1,0:T(8,128)(2,1)S(1)} %get-tuple-element.88), channel_id=1, source_target_pairs={{0,1},{1,2},{2,3},{3,0},{4,5},{5,6},{6,7},{7,4},{8,11},{9,8},{10,9... | collective-permute-start | bytes 1277960 | tf_op jit(solution)/shard_map/ppermute | solution.py:33
  103.5 16.8 %collective-permute-start.10 = (bf16[64,4864]{1,0:T(8,128)(2,1)S(1)}, bf16[64,4864]{1,0:T(8,128)(2,1)S(1)}, u32[]{:S(2)}, u32[]{:S(2)}) collective-permute-start(bf16[64,4864]{1,0:T(8,128)(2,1)S(1)} %add_convert_fusion.1), channel_id=1, source_target_pairs={{0,4},{1,5},{2,6},{3,7},{4,0},{5,1},{6,2},{7,3},{8,12},{9,13},{10,... | collective-permute-start | bytes 1867784 | tf_op jit(solution)/shard_map/ppermute | solution.py:33
  104.2 12.3 %collective-permute-start.12 = (bf16[64,3328]{1,0:T(8,128)(2,1)S(1)}, bf16[64,3328]{1,0:T(8,128)(2,1)S(1)}, u32[]{:S(2)}, u32[]{:S(2)}) collective-permute-start(bf16[64,3328]{1,0:T(8,128)(2,1)S(1)} %get-tuple-element.87), channel_id=1, source_target_pairs={{0,3},{1,0},{2,1},{3,2},{4,7},{5,4},{6,5},{7,6},{8,9},{9,10},{10,1... | collective-permute-start | bytes 1277960 | tf_op jit(solution)/shard_map/ppermute | solution.py:33
  116.4 9.4 %collective-permute-start.14 = (bf16[64,3328]{1,0:T(8,128)(2,1)S(1)}, bf16[64,3328]{1,0:T(8,128)(2,1)S(1)}, u32[]{:S(2)}, u32[]{:S(2)}) collective-permute-start(bf16[64,3328]{1,0:T(8,128)(2,1)S(1)} %add_convert_fusion.2), channel_id=1, source_target_pairs={{0,1},{1,2},{2,3},{3,0},{4,5},{5,6},{6,7},{7,4},{8,11},{9,8},{10,9... | collective-permute-start | bytes 1277960 | tf_op jit(solution)/shard_map/ppermute | solution.py:33
